TPU v7x, 32 devices: a whole 2x2x4 slice. The times are simulated.
32 devices in a mesh: seq: 2 (over core), ctx: 16 (over z, y, x).
Axes of the slice: x: 2, y: 2, z: 4, core: 2. Of those that a mesh axis runs over, the one named last changes fastest.
Arguments:
- pixels: bfloat16 [4, 261, 16384], P('seq', None, 'ctx'), may hold values from -6 to 6
- lengths: int32 [4], P('seq'), may hold values from 1024 to 16384, as said below
- latents: bfloat16 [4, 512, 1024], P('seq', 'ctx'), may hold values from -6 to 6
- w_square: bfloat16 [10, 1024, 1024], P(None, ('seq', 'ctx'))
- w_input: bfloat16 [2, 1024, 261], P(None, ('seq', 'ctx')), may hold values from -0.375 to 0.375
- vec_d: bfloat16 [18, 1024], P(None, ('seq', 'ctx'))
- vec_c: bfloat16 [2, 261], replicated
- cotangent: bfloat16 [4, 512, 1024], P('seq', 'ctx'), may hold values from -6 to 6
Outputs:
- latents_out: bfloat16 [4, 512, 1024], P('seq', 'ctx')
- grad_latents: float32 [4, 512, 1024], P('seq', 'ctx')
- grad_pixels: float32 [4, 261, 16384], P('seq', None, 'ctx')
- grad_square: float32 [10, 1024, 1024], P(None, ('seq', 'ctx'))
- grad_input: float32 [2, 1024, 261], P(None, ('seq', 'ctx'))
- grad_vec: float32 [18, 1024], P(None, ('seq', 'ctx'))
- grad_vec_c: float32 [2, 261], replicated
Inputs may be any that keep to these rules, and one draw needn't show every extreme that they name: Slots 0 to lengths[b] - 1 of sequence b are valid, the rest padding; some sequence has all 16384 slots valid and some exactly 1024.
All inputs are finite; a program needn't handle non-finite values.
Results may differ from a plain program's by a relative error of at most 0.014.
Values may be sent and summed in bfloat16 or wider, within the bound.
No kernel may reach another device: no remote copies, remote signals or barrier semaphores. Data moves between devices by JAX's collectives and lax.ppermute only.
A program may use at most 384 MiB of HBM per device.

v0:
```python
import math

import jax
import jax.numpy as jnp
from jax import lax
from jax.sharding import PartitionSpec as P

H = 8
epsilon = 1e-05
f32 = jnp.float32
b16 = jnp.bfloat16


def matmul(form, left, right):
    return jnp.einsum(form, left, right, preferred_element_type=f32)


def layer_norm(value, gain, shift, axis):
    center = value - jnp.mean(value, axis=axis, keepdims=True)
    spread = jnp.mean(center * center, axis=axis, keepdims=True)
    inverse = lax.rsqrt(spread + epsilon)
    unit = center * inverse
    return (unit * gain + shift, unit, inverse)


def norm_back(grad, unit, inverse, gain, axis):
    scaled = grad * gain
    inner = (
        scaled
        - jnp.mean(scaled, axis=axis, keepdims=True)
        - unit * jnp.mean(scaled * unit, axis=axis, keepdims=True)
    )
    return inner * inverse


def gelu_back(value, grad):
    unused, pull = jax.vjp(jax.nn.gelu, value)
    return pull(grad)[0]


def split_two(value):
    high = value.astype(b16)
    low = (value - high.astype(f32)).astype(b16)
    return high, low


def after(value, *needed):
    return lax.optimization_barrier((value,) + needed)[0]


def pick(array, index):
    return lax.dynamic_index_in_dim(array, index, 0, keepdims=False)


def body(pixels, lengths, latents, w_square, w_input, vec_d, vec_c, cotangent):
    n = lax.axis_size("ctx")
    bits_all = n.bit_length() - 1
    rows = latents.shape[1]
    width = latents.shape[2]
    own_w = w_square.shape[1]
    channels = pixels.shape[1]
    slots = pixels.shape[2]
    total_rows = rows * n
    head_size = width // H
    scale = 1.0 / math.sqrt(width)
    scale_self = 1.0 / math.sqrt(head_size)
    core = lax.axis_index("seq")
    place = lax.axis_index("ctx")
    parity = place & 1
    pair = place >> 1
    wide = [4 << i for i in range(bits_all - 2)]

    def swap(x, bit):
        return lax.ppermute(x, "ctx", [(i, i ^ bit) for i in range(n)])

    def swap_core(x):
        return lax.ppermute(x, "seq", [(0, 1), (1, 0)])

    def ordered(mine, other, flag, axis):
        first = jnp.where(flag == 0, mine, other)
        second = jnp.where(flag == 0, other, mine)
        return jnp.concatenate([first, second], axis=axis)

    def gather(x, order, low_bit, ties=()):
        levels = bits_all - low_bit
        m, r, c = x.shape
        x = x.reshape((m,) + (1,) * levels + (r, c))
        for step, bit in enumerate(order):
            if step < len(ties):
                x = after(x, ties[step])
            level = bit.bit_length() - 1 - low_bit
            axis = 1 + (levels - 1 - level)
            other = swap(x, bit)
            x = ordered(x, other, (place // bit) & 1, axis)
        return x.reshape(m, (n >> low_bit) * r, c)

    def both(x):
        return ordered(x, swap_core(x), core, 1)

    order_a = wide + [2, 1]

    def own_sequence(array, order, ties=()):
        mine = pick(array, parity)
        theirs = swap(pick(array, 1 - parity), 1)
        block = ordered(mine, theirs, parity, 0)
        return gather(block[None], order, 1, ties)[0]

    lanes = 384
    packed = jnp.concatenate(
        [
            w_square[0],
            jnp.pad(w_input[0], ((0, 0), (0, lanes - channels))),
            w_input[1],
            vec_d.T,
            jnp.zeros((own_w, lanes - channels - vec_d.shape[0]), b16),
        ],
        axis=1,
    )
    packed = both(gather(packed[None], order_a, 0))[0]
    square_first = packed[:, :width]
    packed = packed[:, width:]
    tall = (channels + 6 + 15) // 16 * 16
    v_key = packed[:, :tall]
    v_val = jnp.where(jnp.arange(tall) < channels, packed[:, lanes : lanes + tall], jnp.zeros((), b16))
    vecf = packed[:, lanes + channels : lanes + channels + vec_d.shape[0]].T.astype(f32)
    lat = own_sequence(latents, wide + [2])
    late_squares = lax.all_gather(w_square[1:], ("seq", "ctx"), axis=1, tiled=True)
    square = [square_first] + [late_squares[k] for k in range(9)]

    latent = lat.astype(f32)
    norm_a, unit_a, inv_a = layer_norm(latent, vecf[0], vecf[1], 1)
    low_a = norm_a.astype(b16)
    query = (matmul("id,de->ie", low_a, square[0]) + vecf[2]).astype(b16)
    gate = (matmul("dc,id->ci", v_key, query) * scale).astype(b16)
    gates = ordered(gate[None], swap(gate, 1)[None], parity, 0)

    gain_in = vec_c.astype(f32)
    norm_x, unit_x, inv_x = layer_norm(pixels.astype(f32), gain_in[0][:, None], gain_in[1][:, None], 1)
    low_x = jnp.pad(norm_x.astype(b16), ((0, 0), (0, tall - channels), (0, 0)))
    position = place * slots + jnp.arange(slots, dtype=jnp.int32)
    valid = (position[None, :] < lengths[:, None])[:, None, :]
    scores = matmul("qci,qcj->qij", gates, low_x)
    top = jnp.max(jnp.where(valid, scores, -1e30), axis=2)
    top_hi, top_lo = split_two(top)
    shift = top_hi.astype(f32) + top_lo.astype(f32)
    expo = jnp.where(valid, jnp.exp(scores - shift[..., None]), 0.0)
    total_hi, total_lo = split_two(jnp.sum(expo, axis=2))
    mixed = matmul("qij,qcj->qci", expo.astype(b16), low_x).astype(b16)
    row = jnp.arange(tall)[:, None]

    def write(v, parts):
        for k, part in enumerate(parts):
            v = jnp.where(row == channels + k, part[..., None, :], v)
        return v

    pay = write(mixed, [top_hi, top_lo, total_hi, total_lo])

    def opened(p):
        s = p[channels : channels + 4].astype(f32)
        return p.astype(f32), s[0] + s[1], s[2] + s[3]

    def merge(a, b):
        va, ta, la = opened(a)
        vb, tb, lb = opened(b)
        t = jnp.maximum(ta, tb)
        ea = jnp.exp(ta - t)
        eb = jnp.exp(tb - t)
        return va * ea + vb * eb, t, la * ea + lb * eb

    def closed(v, t, l):
        return write(v.astype(b16), split_two(t) + split_two(l))

    state = merge(pick(pay, parity), swap(pick(pay, 1 - parity), 1))
    for bit in [2] + wide:
        mine = closed(*state)
        state = merge(mine, swap(mine, bit))
    mix_sum, top_all, total_all = state
    mean_x = jnp.where(row < channels, mix_sum / total_all, 0.0)
    mean_low = mean_x.astype(b16)

    attended = (matmul("ci,dc->id", mean_low, v_val) + vecf[3]).astype(b16)
    after_cross = latent + matmul("id,de->ie", attended, square[1]) + vecf[4]
    norm_b, unit_b, inv_b = layer_norm(after_cross, vecf[5], vecf[6], 1)
    low_b = norm_b.astype(b16)
    ffn_pre = matmul("id,de->ie", low_b, square[2]) + vecf[7]
    ffn_act = jax.nn.gelu(ffn_pre).astype(b16)
    after_ffn = after_cross + matmul("id,de->ie", ffn_act, square[3]) + vecf[8]
    norm_c, unit_c, inv_c = layer_norm(after_ffn, vecf[9], vecf[10], 1)
    low_c = norm_c.astype(b16)

    def heads(x):
        return x.reshape(total_rows, H, head_size)

    self_query = (matmul("id,de->ie", low_c, square[4]) + vecf[11]).astype(b16)
    self_keys = matmul("id,de->ie", low_c, square[5]).astype(b16)
    self_values = (matmul("id,de->ie", low_c, square[6]) + vecf[12]).astype(b16)
    query_heads, key_heads, value_heads = heads(self_query), heads(self_keys), heads(self_values)
    self_scores = matmul("ihe,jhe->hij", query_heads, key_heads) * scale_self
    self_exp = jnp.exp(self_scores - jnp.max(self_scores, axis=2, keepdims=True))
    self_weight = self_exp / jnp.sum(self_exp, axis=2, keepdims=True)
    self_low = self_weight.astype(b16)
    self_mix = matmul("hij,jhe->ihe", self_low, value_heads).reshape(total_rows, width).astype(b16)
    after_self = after_ffn + matmul("id,de->ie", self_mix, square[7]) + vecf[13]
    norm_e, unit_e, inv_e = layer_norm(after_self, vecf[14], vecf[15], 1)
    low_e = norm_e.astype(b16)
    out_pre = matmul("id,de->ie", low_e, square[8]) + vecf[16]
    out_act = jax.nn.gelu(out_pre).astype(b16)
    final = (after_self + matmul("id,de->ie", out_act, square[9]) + vecf[17]).astype(b16)

    def own_rows(array):
        mine = lax.dynamic_slice_in_dim(array, place * rows, rows, 0)
        theirs = lax.dynamic_slice_in_dim(array, (place ^ 1) * rows, rows, 0)
        return ordered(mine[None], swap(theirs, 1)[None], parity, 0)

    latents_out = own_rows(final)

    cot = own_sequence(after(cotangent, low_b), wide + [2], (low_c, self_keys, self_mix))

    def share(a):
        parts = [lax.dynamic_slice_in_dim(a, s * n * own_w + pair * 2 * own_w, 2 * own_w, a.ndim - 1) for s in range(2)]
        return jnp.stack(parts, axis=0)

    def settle(x, axis):
        x = pick(x, core) + swap_core(pick(x, 1 - core))
        mine = lax.dynamic_slice_in_dim(x, parity * own_w, own_w, axis)
        theirs = lax.dynamic_slice_in_dim(x, (1 - parity) * own_w, own_w, axis)
        return mine + swap(theirs, 1)

    def weight_grad(a, r):
        return matmul("sia,ie->sae", jnp.moveaxis(share(a), 0, 0), r)

    def sums(x):
        return jnp.sum(x.astype(f32), axis=0)

    d_final = cot.astype(f32)
    round_nine = cot
    part9 = weight_grad(out_act, round_nine)
    d_out_pre = gelu_back(out_pre, matmul("ie,de->id", round_nine, square[9])).astype(b16)
    part8 = weight_grad(low_e, d_out_pre)
    d_norm_e = matmul("ie,de->id", d_out_pre, square[8])
    d_after_self = d_final + norm_back(d_norm_e, unit_e, inv_e, vecf[14], 1)
    round_seven = d_after_self.astype(b16)
    part7 = weight_grad(self_mix, round_seven)
    d_mix = matmul("ie,de->id", round_seven, square[7]).astype(b16)
    d_mix_heads = heads(d_mix)
    d_self_weight = matmul("ihe,jhe->hij", d_mix_heads, value_heads)
    d_self_scores = (
        self_weight * (d_self_weight - jnp.sum(d_self_weight * self_weight, axis=2, keepdims=True))
    ).astype(b16)
    d_self_query = (matmul("hij,jhe->ihe", d_self_scores, key_heads) * scale_self).reshape(total_rows, width).astype(b16)
    d_self_keys = (matmul("hij,ihe->jhe", d_self_scores, query_heads) * scale_self).reshape(total_rows, width).astype(b16)
    d_self_values = matmul("hij,ihe->jhe", self_low, d_mix_heads).reshape(total_rows, width).astype(b16)
    part4 = weight_grad(low_c, d_self_query)
    part5 = weight_grad(low_c, d_self_keys)
    part6 = weight_grad(low_c, d_self_values)
    d_norm_c = (
        matmul("ie,de->id", d_self_query, square[4])
        + matmul("ie,de->id", d_self_keys, square[5])
        + matmul("ie,de->id", d_self_values, square[6])
    )
    d_after_ffn = d_after_self + norm_back(d_norm_c, unit_c, inv_c, vecf[9], 1)
    round_three = d_after_ffn.astype(b16)
    part3 = weight_grad(ffn_act, round_three)
    d_ffn_pre = gelu_back(ffn_pre, matmul("ie,de->id", round_three, square[3])).astype(b16)
    part2 = weight_grad(low_b, d_ffn_pre)
    d_norm_b = matmul("ie,de->id", d_ffn_pre, square[2])
    d_after_cross = d_after_ffn + norm_back(d_norm_b, unit_b, inv_b, vecf[5], 1)
    round_one = d_after_cross.astype(b16)
    part1 = weight_grad(attended, round_one)
    d_attended = matmul("ie,de->id", round_one, square[1]).astype(b16)

    pull = matmul("dc,id->ci", v_val, d_attended).astype(b16)
    delta = jnp.sum(pull.astype(f32) * mean_x, axis=0)
    pieces = split_two(top_all) + split_two(total_all) + split_two(delta)
    sent = write(pull, pieces)
    sents = ordered(sent[None], swap(sent, 1)[None], parity, 0)
    pulls = sents
    side = sents[:, channels : channels + 6].astype(f32)
    top_q = side[:, 0] + side[:, 1]
    total_q = side[:, 2] + side[:, 3]
    delta_q = side[:, 4] + side[:, 5]
    scores_again = matmul("qci,qcj->qij", gates, low_x)
    weight = jnp.where(valid, jnp.exp(scores_again - top_q[..., None]), 0.0) / total_q[..., None]
    d_weight = matmul("qci,qcj->qij", pulls, low_x)
    d_scores = (weight * (d_weight - delta_q[..., None])).astype(b16)
    weight_low = weight.astype(b16)
    force = matmul("qij,qcj->qci", d_scores, low_x).astype(b16)
    d_in_norm = (matmul("qci,qij->qcj", gates, d_scores) + matmul("qci,qij->qcj", pulls, weight_low))[:, :channels]
    grad_pixels = norm_back(d_in_norm, unit_x, inv_x, gain_in[0][:, None], 1)
    grad_vc = jnp.stack([jnp.sum(d_in_norm * unit_x, axis=(0, 2)), jnp.sum(d_in_norm, axis=(0, 2))])
    grad_vc = grad_vc + swap_core(grad_vc)
    for bit in [1, 2] + wide:
        grad_vc = grad_vc + swap(grad_vc, bit)

    force_sum = pick(force, parity).astype(f32) + swap(pick(force, 1 - parity), 1).astype(f32)
    for bit in [2] + wide:
        mine = force_sum.astype(b16)
        force_sum = mine.astype(f32) + swap(mine, bit).astype(f32)
    force_low = (force_sum * scale).astype(b16)
    d_query = matmul("ci,dc->id", force_low, v_key).astype(b16)
    part0 = weight_grad(low_a, d_query)
    d_norm_a = matmul("ie,de->id", d_query, square[0])
    grad_lat = d_after_cross + norm_back(d_norm_a, unit_a, inv_a, vecf[0], 1)
    grad_latents = own_rows(grad_lat)

    share_q = share(query)
    share_att = share(d_attended)
    part_in = jnp.stack(
        [matmul("sia,ci->sac", share_q, force_low), matmul("sia,ci->sac", share_att, mean_low)], axis=1
    )[..., :channels]
    grad_input = settle(part_in, 1)
    vec_part = jnp.stack(
        [
            sums(d_norm_a * unit_a),
            sums(d_norm_a),
            sums(d_query),
            sums(d_attended),
            sums(round_one),
            sums(d_norm_b * unit_b),
            sums(d_norm_b),
            sums(d_ffn_pre),
            sums(round_three),
            sums(d_norm_c * unit_c),
            sums(d_norm_c),
            sums(d_self_query),
            sums(d_self_values),
            sums(round_seven),
            sums(d_norm_e * unit_e),
            sums(d_norm_e),
            sums(d_out_pre),
            sums(round_nine),
        ]
    )
    grad_vec = settle(share(vec_part), 1)
    late = settle(part0, 0)[None]
    mid = settle(jnp.stack([part1, part2, part3], axis=1), 1)
    heads_part = settle(jnp.stack([part4, part5, part6], axis=1), 1)
    early = settle(jnp.stack([part7, part8, part9], axis=1), 1)
    grad_square = jnp.concatenate([late, mid, heads_part, early], axis=0)
    return (latents_out, grad_latents, grad_pixels, grad_square, grad_input, grad_vec, grad_vc)


def solution(mesh):
    placed = (
        P("seq", None, "ctx"),
        P("seq"),
        P("seq", "ctx", None),
        P(None, ("seq", "ctx"), None),
        P(None, ("seq", "ctx"), None),
        P(None, ("seq", "ctx")),
        P(),
        P("seq", "ctx", None),
    )
    return jax.shard_map(
        body,
        mesh=mesh,
        in_specs=placed,
        out_specs=(
            P("seq", "ctx", None),
            P("seq", "ctx", None),
            P("seq", None, "ctx"),
            P(None, ("seq", "ctx"), None),
            P(None, ("seq", "ctx"), None),
            P(None, ("seq", "ctx")),
            P(),
        ),
        check_vma=False,
    )
```

profile of v0, /device:TPU:0, one launch (start us, length us, event | category | flops | bytes accessed | tf_op | source)
XLA Modules:
  0.0 440.5 jit_solution(984071426889248289)
XLA Ops:
  11.8 3.1 collective-permute-start.4
  14.9 3.1 collective-permute-done.4
  22.7 18.0 %collective-permute-done.5 = bf16[1,1,2,1,1,32,1792]{6,5,4,3,2,1,0:T(8,128)(2,1)S(1)} collective-permute-done((bf16[1,1,2,1,1,32,1792]{6,5,4,3,2,1,0:T(8,128)(2,1)S(1)}, bf16[1,1,2,1,1,32,1792]{6,5,4,3,2,1,0:T(8,128)(2,1)S(1)}, u32[]{:S(2)}, u32[]{:S(2)}) %collective-permute-start.5) | collective-permute-done | bytes 229408 | tf_op jit(solution)/shard_map/ppermute | solution.py:74
  42.6 6.7 %collective-permute-done.6 = bf16[1,2,2,1,1,32,1792]{6,5,4,3,2,1,0:T(8,128)(2,1)S(1)} collective-permute-done((bf16[1,2,2,1,1,32,1792]{6,5,4,3,2,1,0:T(8,128)(2,1)S(1)}, bf16[1,2,2,1,1,32,1792]{6,5,4,3,2,1,0:T(8,128)(2,1)S(1)}, u32[]{:S(2)}, u32[]{:S(2)}) %collective-permute-start.6) | collective-permute-done | bytes 458784 | tf_op jit(solution)/shard_map/ppermute | solution.py:74
  50.9 7.6 %collective-permute-start.1 = (bf16[1,1,1,1,64,1024]{5,4,3,2,1,0:T(8,128)(2,1)S(1)}, bf16[1,1,1,1,64,1024]{5,4,3,2,1,0:T(8,128)(2,1)S(1)}, u32[]{:S(2)}, u32[]{:S(2)}) collective-permute-start(bf16[1,1,1,1,64,1024]{5,4,3,2,1,0:T(8,128)(2,1)S(1)} %maximum_bitcast_fusion.1), channel_id=1, source_target_pairs={{0,4},{1,5},{2,6},{3,7},{4,0},{5,1},{6,2},{7,3},{8,12},{9,13},{10,... | collective-permute-start | bytes 393224 | tf_op jit(solution)/shard_map/ppermute | solution.py:74
  58.6 8.8 %collective-permute-done.1 = bf16[1,1,1,1,64,1024]{5,4,3,2,1,0:T(8,128)(2,1)S(1)} collective-permute-done((bf16[1,1,1,1,64,1024]{5,4,3,2,1,0:T(8,128)(2,1)S(1)}, bf16[1,1,1,1,64,1024]{5,4,3,2,1,0:T(8,128)(2,1)S(1)}, u32[]{:S(2)}, u32[]{:S(2)}) %collective-permute-start.1) | collective-permute-done | bytes 131104 | tf_op jit(solution)/shard_map/ppermute | solution.py:74
  69.6 13.4 %collective-permute-done.7 = bf16[1,2,2,2,1,32,1792]{6,5,4,3,2,1,0:T(8,128)(2,1)} collective-permute-done((bf16[1,2,2,2,1,32,1792]{6,5,4,3,2,1,0:T(8,128)(2,1)S(1)}, bf16[1,2,2,2,1,32,1792]{6,5,4,3,2,1,0:T(8,128)(2,1)}, u32[]{:S(2)}, u32[]{:S(2)}) %collective-permute-start.7) | collective-permute-done | bytes 917536 | tf_op jit(solution)/shard_map/ppermute | solution.py:74
  84.4 2.8 copy.35
  89.8 3.8 collective-permute-start.3
  93.8 14.8 %collective-permute-done.3 = bf16[1,2,2,1,64,1024]{5,4,3,2,1,0:T(8,128)(2,1)S(1)} collective-permute-done((bf16[1,2,2,1,64,1024]{5,4,3,2,1,0:T(8,128)(2,1)S(1)}, bf16[1,2,2,1,64,1024]{5,4,3,2,1,0:T(8,128)(2,1)S(1)}, u32[]{:S(2)}, u32[]{:S(2)}) %collective-permute-start.3) | collective-permute-done | bytes 524320 | tf_op jit(solution)/shard_map/ppermute | solution.py:74
  117.5 11.7 %collective-permute-done.9 = bf16[272,512]{1,0:T(8,128)(2,1)S(1)} collective-permute-done((bf16[272,512]{1,0:T(8,128)(2,1)S(1)}, bf16[272,512]{1,0:T(8,128)(2,1)S(1)}, u32[]{:S(2)}, u32[]{:S(2)}) %collective-permute-start.9) | collective-permute-done | bytes 278560 | tf_op jit(solution)/shard_map/ppermute | solution.py:74
  136.3 8.6 %collective-permute-done.10 = bf16[272,512]{1,0:T(8,128)(2,1)S(1)} collective-permute-done((bf16[272,512]{1,0:T(8,128)(2,1)S(1)}, bf16[272,512]{1,0:T(8,128)(2,1)S(1)}, u32[]{:S(2)}, u32[]{:S(2)}) %collective-permute-start.10) | collective-permute-done | bytes 278560 | tf_op jit(solution)/shard_map/ppermute | solution.py:74
  146.9 5.0 %collective-permute-done.11 = bf16[272,512]{1,0:T(8,128)(2,1)S(1)} collective-permute-done((bf16[272,512]{1,0:T(8,128)(2,1)S(1)}, bf16[272,512]{1,0:T(8,128)(2,1)S(1)}, u32[]{:S(2)}, u32[]{:S(2)}) %collective-permute-start.11) | collective-permute-done | bytes 278560 | tf_op jit(solution)/shard_map/ppermute | solution.py:74
  152.2 8.4 %collective-permute-start.12 = (bf16[272,512]{1,0:T(8,128)(2,1)S(1)}, bf16[272,512]{1,0:T(8,128)(2,1)S(1)}, u32[]{:S(2)}, u32[]{:S(2)}) collective-permute-start(bf16[272,512]{1,0:T(8,128)(2,1)S(1)} %fusion.138), channel_id=1, source_target_pairs={{0,4},{1,5},{2,6},{3,7},{4,0},{5,1},{6,2},{7,3},{8,12},{9,13},{10,... | collective-permute-start | bytes 835592 | tf_op jit(solution)/shard_map/ppermute | solution.py:74
  160.8 7.3 %collective-permute-done.12 = bf16[272,512]{1,0:T(8,128)(2,1)S(1)} collective-permute-done((bf16[272,512]{1,0:T(8,128)(2,1)S(1)}, bf16[272,512]{1,0:T(8,128)(2,1)S(1)}, u32[]{:S(2)}, u32[]{:S(2)}) %collective-permute-start.12) | collective-permute-done | bytes 278560 | tf_op jit(solution)/shard_map/ppermute | solution.py:74
  174.5 8.5 %collective-permute-done.13 = bf16[272,512]{1,0:T(8,128)(2,1)S(1)} collective-permute-done((bf16[272,512]{1,0:T(8,128)(2,1)S(1)}, bf16[272,512]{1,0:T(8,128)(2,1)S(1)}, u32[]{:S(2)}, u32[]{:S(2)}) %collective-permute-start.13) | collective-permute-done | bytes 278560 | tf_op jit(solution)/shard_map/ppermute | solution.py:74
  187.9 2.9 fusion.253
  193.1 4.6 %multiply_convert_fusion.5 = (bf16[512,1024]{1,0:T(8,128)(2,1)S(1)}, f32[512,1024]{1,0:T(8,128)}) fusion(f32[1024]{0:T(1024)S(1)} %bitcast.484, bf16[512,1024]{1,0:T(8,128)(2,1)S(1)} %add_convert_fusion.5, bf16[9,1024,1024]{2,1,0:T(8,128)(2,1)} %all-gather.2.cloned.1.call-done), kind=kOutput, calls=%fused_computation.116 | convolution fusion | flops 1078984704 | bytes 6295552 | tf_op jit(solution)/shard_map/id,de->ie/dot_general | solution.py:15
  198.4 3.0 fusion.254
  202.7 2.8 add_convert_fusion.2
  206.1 4.2 fusion.89
  211.8 6.1 %fusion.255 = (f32[8,512]{1,0:T(8,128)}, f32[8,512,512]{1,2,0:T(8,128)}) fusion(bf16[512,8,128]{0,2,1:T(8,128)(2,1)S(1)} %bitcast.421, bf16[512,8,128]{0,2,1:T(8,128)(2,1)S(1)} %bitcast.419), kind=kOutput, calls=%fused_computation.536 | convolution fusion | flops 543162880 | bytes 10502144 | tf_op jit(solution)/shard_map/sub | solution.py:199
  218.0 3.0 fusion.93
  223.6 3.0 fusion.256
  227.7 5.0 %multiply_convert_fusion.4 = (bf16[512,1024]{1,0:T(8,128)(2,1)}, f32[512,1024]{1,0:T(8,128)}) fusion(f32[1024]{0:T(1024)S(1)} %bitcast.486, bf16[512,1024]{1,0:T(8,128)(2,1)S(1)} %add_convert_fusion.1, bf16[9,1024,1024]{2,1,0:T(8,128)(2,1)} %all-gather.2.cloned.1.call-done), kind=kOutput, calls=%fused_computation.103 | convolution fusion | flops 1078984704 | bytes 6295552 | tf_op jit(solution)/shard_map/id,de->ie/dot_general | solution.py:15
  243.1 3.4 collective-permute-start.17
  246.5 3.2 add_convert_fusion
  249.7 8.1 %collective-permute-done.17 = bf16[1,1,2,1,64,1024]{5,4,3,2,1,0:T(8,128)(2,1)S(1)} collective-permute-done((bf16[1,1,2,1,64,1024]{5,4,3,2,1,0:T(8,128)(2,1)S(1)}, bf16[1,1,2,1,64,1024]{5,4,3,2,1,0:T(8,128)(2,1)S(1)}, u32[]{:S(2)}, u32[]{:S(2)}) %collective-permute-start.17) | collective-permute-done | bytes 262176 | tf_op jit(solution)/shard_map/ppermute | solution.py:74
  264.3 7.5 %collective-permute-done.18 = bf16[1,2,2,1,64,1024]{5,4,3,2,1,0:T(8,128)(2,1)S(1)} collective-permute-done((bf16[1,2,2,1,64,1024]{5,4,3,2,1,0:T(8,128)(2,1)S(1)}, bf16[1,2,2,1,64,1024]{5,4,3,2,1,0:T(8,128)(2,1)S(1)}, u32[]{:S(2)}, u32[]{:S(2)}) %collective-permute-start.18) | collective-permute-done | bytes 524320 | tf_op jit(solution)/shard_map/ppermute | solution.py:74
  272.9 4.7 %convert_reduce_fusion.3 = (f32[1024]{0:T(1024)}, bf16[512,1024]{1,0:T(8,128)(2,1)S(1)}) fusion(f32[512,1024]{1,0:T(8,128)S(1)} %copy-done.145, f32[1024]{0:T(1024)S(1)} %bitcast.487, bf16[512,1024]{1,0:T(8,128)(2,1)S(1)} %bitcast.414, bf16[9,1024,1024]{2,1,0:T(8,128)(2,1)} %all-gather.2.cloned.1.call-done), kind=kOutput, calls=%fused_computation.79 | convolution fusion | flops 1085799424 | bytes 6299648 | tf_op jit(solution)/shard_map/ie,de->id/dot_general | solution.py:15
  277.6 4.4 multiply_reduce_fusion.2
  285.0 2.9 fusion.88
  288.5 5.7 %convert_reduce_fusion.5 = (f32[8,128]{1,0:T(8,128)}, bf16[8,128,512]{2,1,0:T(8,128)(2,1)S(1)}) fusion(bf16[512,8,128]{0,2,1:T(8,128)(2,1)S(1)} %bitcast.427, f32[8,512,512]{1,2,0:T(8,128)} %get-tuple-element.185, f32[8,512]{1,0:T(8,128)} %get-tuple-element.184), kind=kOutput, calls=%fused_computation.82 | convolution fusion | flops 542637056 | bytes 10506240 | tf_op jit(solution)/shard_map/hij,ihe->jhe/dot_general | solution.py:15
  294.2 4.3 multiply_reduce_fusion
  311.1 2.9 fusion.66
  314.0 3.0 fusion.68
  317.1 4.4 multiply_reduce_fusion.3
  323.0 4.8 %convert_reduce_fusion.8 = (f32[1024]{0:T(1024)}, bf16[512,1024]{1,0:T(8,128)(2,1)S(1)}) fusion(f32[512,1024]{1,0:T(8,128)S(1)} %copy-done.144, f32[1024]{0:T(1024)S(1)} %bitcast.485, bf16[9,1024,1024]{2,1,0:T(8,128)(2,1)} %all-gather.2.cloned.1.call-done, f32[512,1024]{1,0:T(8,128)S(1)} %get-tuple-element.70), kind=kOutput, calls=%fused_computation.86 | convolution fusion | flops 1086323712 | bytes 7348224 | tf_op jit(solution)/shard_map/ie,de->id/dot_general | solution.py:15
  327.9 4.3 multiply_reduce_fusion.4
  333.6 3.5 convert_reduce_fusion.10
  371.0 3.0 copy.71
  384.7 7.0 %collective-permute-done.22 = bf16[272,512]{1,0:T(8,128)(2,1)S(1)} collective-permute-done((bf16[272,512]{1,0:T(8,128)(2,1)S(1)}, bf16[272,512]{1,0:T(8,128)(2,1)S(1)}, u32[]{:S(2)}, u32[]{:S(2)}) %collective-permute-start.22) | collective-permute-done | bytes 278560 | tf_op jit(solution)/shard_map/ppermute | solution.py:74
  394.2 3.9 collective-permute-done.30
  398.9 3.4 collective-permute-done.28
  405.6 3.5 fusion.49
  410.4 4.1 stack.279
  421.0 3.1 collective-permute-done.36
  427.7 3.1 collective-permute-done.34
  (590 shorter events, 159.4 us)
Async XLA Ops:
  7.2 180.7 %all-gather.2.cloned.1.call-start = ((), (), s32[]{:S(2)}) async-start(), calls=%async_computation | async-start | bytes 19464192 | tf_op jit(solution)/shard_map/all_gather | solution.py:127
  11.8 6.3 %collective-permute-start.4 = (bf16[1,1,1,1,1,32,1792]{6,5,4,3,2,1,0:T(8,128)(2,1)S(1)}, bf16[1,1,1,1,1,32,1792]{6,5,4,3,2,1,0:T(8,128)(2,1)S(1)}, u32[]{:S(2)}, u32[]{:S(2)}) collective-permute-start(bf16[1,1,1,1,1,32,1792]{6,5,4,3,2,1,0:T(8,128)(2,1)S(1)} %bitcast.437), channel_id=1, source_target_pairs={{0,4},{1,5},{2,6},{3,7},{4,0},{5,1},{6,2},{7,3},{8,12},{9,13},{10,... | collective-permute-start | bytes 344072 | tf_op jit(solution)/shard_map/ppermute | solution.py:74
  18.1 22.5 %collective-permute-start.5 = (bf16[1,1,2,1,1,32,1792]{6,5,4,3,2,1,0:T(8,128)(2,1)S(1)}, bf16[1,1,2,1,1,32,1792]{6,5,4,3,2,1,0:T(8,128)(2,1)S(1)}, u32[]{:S(2)}, u32[]{:S(2)}) collective-permute-start(bf16[1,1,2,1,1,32,1792]{6,5,4,3,2,1,0:T(8,128)(2,1)S(1)} %pad_maximum_fusion.20), channel_id=1, source_target_pairs={{0,8},{1,9},{2,10},{3,11},{4,12},{5,13},{6,14},{7,15},{8,0},{9,1},... | collective-permute-start | bytes 688136 | tf_op jit(solution)/shard_map/ppermute | solution.py:74
  20.9 30.0 %collective-permute-start = (bf16[32,1024]{1,0:T(8,128)(2,1)S(1)}, bf16[32,1024]{1,0:T(8,128)(2,1)S(1)}, u32[]{:S(2)}, u32[]{:S(2)}) collective-permute-start(bf16[32,1024]{1,0:T(8,128)(2,1)S(1)} %dynamic-slice_bitcast_fusion.9), channel_id=1, source_target_pairs={{0,1},{1,0},{2,3},{3,2},{4,5},{5,4},{6,7},{7,6},{8,9},{9,8},{10,11... | collective-permute-start | bytes 196616 | tf_op jit(solution)/shard_map/ppermute | solution.py:74
  40.7 8.5 %collective-permute-start.6 = (bf16[1,2,2,1,1,32,1792]{6,5,4,3,2,1,0:T(8,128)(2,1)S(1)}, bf16[1,2,2,1,1,32,1792]{6,5,4,3,2,1,0:T(8,128)(2,1)S(1)}, u32[]{:S(2)}, u32[]{:S(2)}) collective-permute-start(bf16[1,2,2,1,1,32,1792]{6,5,4,3,2,1,0:T(8,128)(2,1)S(1)} %pad_maximum_fusion.12), channel_id=1, source_target_pairs={{0,2},{1,3},{2,0},{3,1},{4,6},{5,7},{6,4},{7,5},{8,10},{9,11},{10,... | collective-permute-start | bytes 1376264 | tf_op jit(solution)/shard_map/ppermute | solution.py:74
  42.2 74.9 %copy-start.62 = (f32[2,1024]{1,0:T(2,128)}, f32[2,1024]{1,0:T(2,128)S(1)}, u32[]{:S(2)}) copy-start(f32[2,1024]{1,0:T(2,128)S(1)} %broadcast_multiply_fusion.2) | copy-start | bytes 24580
  49.4 33.5 %collective-permute-start.7 = (bf16[1,2,2,2,1,32,1792]{6,5,4,3,2,1,0:T(8,128)(2,1)S(1)}, bf16[1,2,2,2,1,32,1792]{6,5,4,3,2,1,0:T(8,128)(2,1)}, u32[]{:S(2)}, u32[]{:S(2)}) collective-permute-start(bf16[1,2,2,2,1,32,1792]{6,5,4,3,2,1,0:T(8,128)(2,1)S(1)} %pad_maximum_fusion.7), channel_id=1, source_target_pairs={{0,1},{1,0},{2,3},{3,2},{4,5},{5,4},{6,7},{7,6},{8,9},{9,8},{10,11... | collective-permute-start | bytes 2752520 | tf_op jit(solution)/shard_map/ppermute | solution.py:74
  50.9 16.4 %collective-permute-start.1 = (bf16[1,1,1,1,64,1024]{5,4,3,2,1,0:T(8,128)(2,1)S(1)}, bf16[1,1,1,1,64,1024]{5,4,3,2,1,0:T(8,128)(2,1)S(1)}, u32[]{:S(2)}, u32[]{:S(2)}) collective-permute-start(bf16[1,1,1,1,64,1024]{5,4,3,2,1,0:T(8,128)(2,1)S(1)} %maximum_bitcast_fusion.1), channel_id=1, source_target_pairs={{0,4},{1,5},{2,6},{3,7},{4,0},{5,1},{6,2},{7,3},{8,12},{9,13},{10,... | collective-permute-start | bytes 393224 | tf_op jit(solution)/shard_map/ppermute | solution.py:74
  58.5 109.6 %copy-start.95 = (pred[272]{0:T(512)(128)(4,1)}, pred[272]{0:T(512)(128)(4,1)S(1)}, u32[]{:S(2)}) copy-start(pred[272]{0:T(512)(128)(4,1)S(1)} %get-tuple-element.212) | copy-start | bytes 820
  58.5 109.6 %copy-start.98 = (pred[272]{0:T(512)(128)(4,1)}, pred[272]{0:T(512)(128)(4,1)S(1)}, u32[]{:S(2)}) copy-start(pred[272]{0:T(512)(128)(4,1)S(1)} %get-tuple-element.213) | copy-start | bytes 820
  67.5 21.3 %collective-permute-start.2 = (bf16[1,1,2,1,64,1024]{5,4,3,2,1,0:T(8,128)(2,1)S(1)}, bf16[1,1,2,1,64,1024]{5,4,3,2,1,0:T(8,128)(2,1)}, u32[]{:S(2)}, u32[]{:S(2)}) collective-permute-start(bf16[1,1,2,1,64,1024]{5,4,3,2,1,0:T(8,128)(2,1)S(1)} %pad_maximum_fusion.17), channel_id=1, source_target_pairs={{0,8},{1,9},{2,10},{3,11},{4,12},{5,13},{6,14},{7,15},{8,0},{9,1},... | collective-permute-start | bytes 786440 | tf_op jit(solution)/shard_map/ppermute | solution.py:74
  87.3 22.3 %collective-permute-start.8 = (bf16[1,512,1792]{1,2,0:T(8,128)(2,1)}, bf16[1,512,1792]{1,2,0:T(8,128)(2,1)}, u32[]{:S(2)}, u32[]{:S(2)}) collective-permute-start(bf16[1,512,1792]{1,2,0:T(8,128)(2,1)} %copy.35), channel_id=1, source_target_pairs={{0,16},{16,0},{1,17},{17,1},{2,18},{18,2},{3,19},{19,3},{4,20},{20... | collective-permute-start | bytes 5505032 | tf_op jit(solution)/shard_map/ppermute | solution.py:77
  89.8 18.8 %collective-permute-start.3 = (bf16[1,2,2,1,64,1024]{5,4,3,2,1,0:T(8,128)(2,1)S(1)}, bf16[1,2,2,1,64,1024]{5,4,3,2,1,0:T(8,128)(2,1)S(1)}, u32[]{:S(2)}, u32[]{:S(2)}) collective-permute-start(bf16[1,2,2,1,64,1024]{5,4,3,2,1,0:T(8,128)(2,1)S(1)} %pad_maximum_fusion.10), channel_id=1, source_target_pairs={{0,2},{1,3},{2,0},{3,1},{4,6},{5,7},{6,4},{7,5},{8,10},{9,11},{10,... | collective-permute-start | bytes 1572872 | tf_op jit(solution)/shard_map/ppermute | solution.py:74
  93.7 74.5 %copy-start.104 = (pred[272]{0:T(512)(128)(4,1)}, pred[272]{0:T(512)(128)(4,1)S(1)}, u32[]{:S(2)}) copy-start(pred[272]{0:T(512)(128)(4,1)S(1)} %get-tuple-element.211) | copy-start | bytes 820
  113.2 79.8 %copy-start.119 = (f32[1,1024]{1,0:T(1,128)}, f32[1,1024]{1,0:T(1,128)S(1)}, u32[]{:S(2)}) copy-start(f32[1,1024]{1,0:T(1,128)S(1)} %get-tuple-element.163) | copy-start | bytes 12292
  115.5 13.7 %collective-permute-start.9 = (bf16[272,512]{1,0:T(8,128)(2,1)S(1)}, bf16[272,512]{1,0:T(8,128)(2,1)S(1)}, u32[]{:S(2)}, u32[]{:S(2)}) collective-permute-start(bf16[272,512]{1,0:T(8,128)(2,1)S(1)} %fusion.97), channel_id=1, source_target_pairs={{0,1},{1,0},{2,3},{3,2},{4,5},{5,4},{6,7},{7,6},{8,9},{9,8},{10,11... | collective-permute-start | bytes 835592 | tf_op jit(solution)/shard_map/ppermute | solution.py:74
  133.8 11.1 %collective-permute-start.10 = (bf16[272,512]{1,0:T(8,128)(2,1)S(1)}, bf16[272,512]{1,0:T(8,128)(2,1)S(1)}, u32[]{:S(2)}, u32[]{:S(2)}) collective-permute-start(bf16[272,512]{1,0:T(8,128)(2,1)S(1)} %dynamic-slice_bitcast_fusion.4), channel_id=1, source_target_pairs={{0,1},{1,0},{2,3},{3,2},{4,5},{5,4},{6,7},{7,6},{8,9},{9,8},{10,11... | collective-permute-start | bytes 835592 | tf_op jit(solution)/shard_map/ppermute | solution.py:74
  145.3 6.6 %collective-permute-start.11 = (bf16[272,512]{1,0:T(8,128)(2,1)S(1)}, bf16[272,512]{1,0:T(8,128)(2,1)S(1)}, u32[]{:S(2)}, u32[]{:S(2)}) collective-permute-start(bf16[272,512]{1,0:T(8,128)(2,1)S(1)} %fusion.146), channel_id=1, source_target_pairs={{0,2},{1,3},{2,0},{3,1},{4,6},{5,7},{6,4},{7,5},{8,10},{9,11},{10,... | collective-permute-start | bytes 835592 | tf_op jit(solution)/shard_map/ppermute | solution.py:74
  152.2 15.8 %collective-permute-start.12 = (bf16[272,512]{1,0:T(8,128)(2,1)S(1)}, bf16[272,512]{1,0:T(8,128)(2,1)S(1)}, u32[]{:S(2)}, u32[]{:S(2)}) collective-permute-start(bf16[272,512]{1,0:T(8,128)(2,1)S(1)} %fusion.138), channel_id=1, source_target_pairs={{0,4},{1,5},{2,6},{3,7},{4,0},{5,1},{6,2},{7,3},{8,12},{9,13},{10,... | collective-permute-start | bytes 835592 | tf_op jit(solution)/shard_map/ppermute | solution.py:74
  168.5 14.5 %collective-permute-start.13 = (bf16[272,512]{1,0:T(8,128)(2,1)S(1)}, bf16[272,512]{1,0:T(8,128)(2,1)S(1)}, u32[]{:S(2)}, u32[]{:S(2)}) collective-permute-start(bf16[272,512]{1,0:T(8,128)(2,1)S(1)} %fusion.142), channel_id=1, source_target_pairs={{0,8},{1,9},{2,10},{3,11},{4,12},{5,13},{6,14},{7,15},{8,0},{9,1},... | collective-permute-start | bytes 835592 | tf_op jit(solution)/shard_map/ppermute | solution.py:74
  192.9 40.6 %collective-permute-start.15 = (bf16[32,1024]{1,0:T(8,128)(2,1)}, bf16[32,1024]{1,0:T(8,128)(2,1)}, u32[]{:S(2)}, u32[]{:S(2)}) collective-permute-start(bf16[32,1024]{1,0:T(8,128)(2,1)} %dynamic-slice_bitcast_fusion.8), channel_id=1, source_target_pairs={{0,1},{1,0},{2,3},{3,2},{4,5},{5,4},{6,7},{7,6},{8,9},{9,8},{10,11... | collective-permute-start | bytes 196616 | tf_op jit(solution)/shard_map/ppermute | solution.py:74
  234.4 8.6 %collective-permute-start.16 = (bf16[1,1,1,1,64,1024]{5,4,3,2,1,0:T(8,128)(2,1)S(1)}, bf16[1,1,1,1,64,1024]{5,4,3,2,1,0:T(8,128)(2,1)S(1)}, u32[]{:S(2)}, u32[]{:S(2)}) collective-permute-start(bf16[1,1,1,1,64,1024]{5,4,3,2,1,0:T(8,128)(2,1)S(1)} %maximum_bitcast_fusion.2), channel_id=1, source_target_pairs={{0,4},{1,5},{2,6},{3,7},{4,0},{5,1},{6,2},{7,3},{8,12},{9,13},{10,... | collective-permute-start | bytes 393224 | tf_op jit(solution)/shard_map/ppermute | solution.py:74
  243.1 14.7 %collective-permute-start.17 = (bf16[1,1,2,1,64,1024]{5,4,3,2,1,0:T(8,128)(2,1)S(1)}, bf16[1,1,2,1,64,1024]{5,4,3,2,1,0:T(8,128)(2,1)S(1)}, u32[]{:S(2)}, u32[]{:S(2)}) collective-permute-start(bf16[1,1,2,1,64,1024]{5,4,3,2,1,0:T(8,128)(2,1)S(1)} %pad_maximum_fusion.18), channel_id=1, source_target_pairs={{0,8},{1,9},{2,10},{3,11},{4,12},{5,13},{6,14},{7,15},{8,0},{9,1},... | collective-permute-start | bytes 786440 | tf_op jit(solution)/shard_map/ppermute | solution.py:74
  257.9 13.9 %collective-permute-start.18 = (bf16[1,2,2,1,64,1024]{5,4,3,2,1,0:T(8,128)(2,1)S(1)}, bf16[1,2,2,1,64,1024]{5,4,3,2,1,0:T(8,128)(2,1)S(1)}, u32[]{:S(2)}, u32[]{:S(2)}) collective-permute-start(bf16[1,2,2,1,64,1024]{5,4,3,2,1,0:T(8,128)(2,1)S(1)} %pad_maximum_fusion.11), channel_id=1, source_target_pairs={{0,2},{1,3},{2,0},{3,1},{4,6},{5,7},{6,4},{7,5},{8,10},{9,11},{10,... | collective-permute-start | bytes 1572872 | tf_op jit(solution)/shard_map/ppermute | solution.py:74
  259.3 4.3 collective-permute-start.14
  306.8 70.4 %collective-permute-start.31 = (f32[3,64,1024]{2,1,0:T(8,128)}, f32[3,64,1024]{2,1,0:T(8,128)}, u32[]{:S(2)}, u32[]{:S(2)}) collective-permute-start(f32[3,64,1024]{2,1,0:T(8,128)} %dynamic-slice_bitcast_fusion), channel_id=1, source_target_pairs={{0,16},{16,0},{1,17},{17,1},{2,18},{18,2},{3,19},{19,3},{4,20},{20... | collective-permute-start | bytes 2359304 | tf_op jit(solution)/shard_map/ppermute | solution.py:77
  310.6 68.6 %collective-permute-start.29 = (f32[3,64,1024]{2,1,0:T(8,128)}, f32[3,64,1024]{2,1,0:T(8,128)}, u32[]{:S(2)}, u32[]{:S(2)}) collective-permute-start(f32[3,64,1024]{2,1,0:T(8,128)} %dynamic-slice_bitcast_fusion.1), channel_id=1, source_target_pairs={{0,16},{16,0},{1,17},{17,1},{2,18},{18,2},{3,19},{19,3},{4,20},{20... | collective-permute-start | bytes 2359304 | tf_op jit(solution)/shard_map/ppermute | solution.py:77
  340.1 10.3 %collective-permute-start.19 = (bf16[272,512]{1,0:T(8,128)(2,1)}, bf16[272,512]{1,0:T(8,128)(2,1)}, u32[]{:S(2)}, u32[]{:S(2)}) collective-permute-start(bf16[272,512]{1,0:T(8,128)(2,1)} %select_select_fusion), channel_id=1, source_target_pairs={{0,1},{1,0},{2,3},{3,2},{4,5},{5,4},{6,7},{7,6},{8,9},{9,8},{10,11... | collective-permute-start | bytes 835592 | tf_op jit(solution)/shard_map/ppermute | solution.py:74
  347.9 35.6 %collective-permute-start.27 = (f32[3,64,1024]{2,1,0:T(8,128)}, f32[3,64,1024]{2,1,0:T(8,128)S(1)}, u32[]{:S(2)}, u32[]{:S(2)}) collective-permute-start(f32[3,64,1024]{2,1,0:T(8,128)} %dynamic-slice_bitcast_fusion.2), channel_id=1, source_target_pairs={{0,16},{16,0},{1,17},{17,1},{2,18},{18,2},{3,19},{19,3},{4,20},{20... | collective-permute-start | bytes 2359304 | tf_op jit(solution)/shard_map/ppermute | solution.py:77
  357.9 1.4 collective-permute-start.37
  359.3 3.7 collective-permute-start.38
  363.0 3.7 collective-permute-start.39
  366.7 3.6 collective-permute-start.40
  366.7 8.7 %collective-permute-start.20 = (bf16[272,512]{1,0:T(8,128)(2,1)S(1)}, bf16[272,512]{1,0:T(8,128)(2,1)S(1)}, u32[]{:S(2)}, u32[]{:S(2)}) collective-permute-start(bf16[272,512]{1,0:T(8,128)(2,1)S(1)} %dynamic-slice_bitcast_fusion.3), channel_id=1, source_target_pairs={{0,1},{1,0},{2,3},{3,2},{4,5},{5,4},{6,7},{7,6},{8,9},{9,8},{10,11... | collective-permute-start | bytes 835592 | tf_op jit(solution)/shard_map/ppermute | solution.py:74
  370.3 4.5 %collective-permute-start.41 = (f32[2,261]{1,0:T(2,128)S(1)}, f32[2,261]{1,0:T(2,128)S(1)}, u32[]{:S(2)}, u32[]{:S(2)}) collective-permute-start(f32[2,261]{1,0:T(2,128)S(1)} %add.756), channel_id=1, source_target_pairs={{0,8},{1,9},{2,10},{3,11},{4,12},{5,13},{6,14},{7,15},{8,0},{9,1},... | collective-permute-start | bytes 6272 | tf_op jit(solution)/shard_map/ppermute | solution.py:74
  375.4 6.6 %collective-permute-start.21 = (bf16[272,512]{1,0:T(8,128)(2,1)S(1)}, bf16[272,512]{1,0:T(8,128)(2,1)S(1)}, u32[]{:S(2)}, u32[]{:S(2)}) collective-permute-start(bf16[272,512]{1,0:T(8,128)(2,1)S(1)} %fusion.129), channel_id=1, source_target_pairs={{0,2},{1,3},{2,0},{3,1},{4,6},{5,7},{6,4},{7,5},{8,10},{9,11},{10,... | collective-permute-start | bytes 835592 | tf_op jit(solution)/shard_map/ppermute | solution.py:74
  378.5 14.9 %collective-permute-start.32 = (f32[3,32,1024]{2,1,0:T(8,128)S(1)}, f32[3,32,1024]{2,1,0:T(8,128)S(1)}, u32[]{:S(2)}, u32[]{:S(2)}) collective-permute-start(f32[3,32,1024]{2,1,0:T(8,128)S(1)} %constant_dynamic-slice_fusion.10), channel_id=1, source_target_pairs={{0,1},{1,0},{2,3},{3,2},{4,5},{5,4},{6,7},{7,6},{8,9},{9,8},{10,11... | collective-permute-start | bytes 1179656 | tf_op jit(solution)/shard_map/ppermute | solution.py:74
  380.5 17.7 %collective-permute-start.30 = (f32[3,32,1024]{2,1,0:T(8,128)S(1)}, f32[3,32,1024]{2,1,0:T(8,128)S(1)}, u32[]{:S(2)}, u32[]{:S(2)}) collective-permute-start(f32[3,32,1024]{2,1,0:T(8,128)S(1)} %constant_dynamic-slice_fusion.15), channel_id=1, source_target_pairs={{0,1},{1,0},{2,3},{3,2},{4,5},{5,4},{6,7},{7,6},{8,9},{9,8},{10,11... | collective-permute-start | bytes 1179656 | tf_op jit(solution)/shard_map/ppermute | solution.py:74
  382.1 9.6 %collective-permute-start.22 = (bf16[272,512]{1,0:T(8,128)(2,1)S(1)}, bf16[272,512]{1,0:T(8,128)(2,1)S(1)}, u32[]{:S(2)}, u32[]{:S(2)}) collective-permute-start(bf16[272,512]{1,0:T(8,128)(2,1)S(1)} %add_convert_fusion.9), channel_id=1, source_target_pairs={{0,4},{1,5},{2,6},{3,7},{4,0},{5,1},{6,2},{7,3},{8,12},{9,13},{10,... | collective-permute-start | bytes 835592 | tf_op jit(solution)/shard_map/ppermute | solution.py:74
  383.6 18.7 %collective-permute-start.28 = (f32[3,32,1024]{2,1,0:T(8,128)S(1)}, f32[3,32,1024]{2,1,0:T(8,128)S(1)}, u32[]{:S(2)}, u32[]{:S(2)}) collective-permute-start(f32[3,32,1024]{2,1,0:T(8,128)S(1)} %constant_dynamic-slice_fusion.18), channel_id=1, source_target_pairs={{0,1},{1,0},{2,3},{3,2},{4,5},{5,4},{6,7},{7,6},{8,9},{9,8},{10,11... | collective-permute-start | bytes 1179656 | tf_op jit(solution)/shard_map/ppermute | solution.py:74
  391.8 11.4 %collective-permute-start.23 = (bf16[272,512]{1,0:T(8,128)(2,1)S(1)}, bf16[272,512]{1,0:T(8,128)(2,1)S(1)}, u32[]{:S(2)}, u32[]{:S(2)}) collective-permute-start(bf16[272,512]{1,0:T(8,128)(2,1)S(1)} %add_convert_fusion.8), channel_id=1, source_target_pairs={{0,8},{1,9},{2,10},{3,11},{4,12},{5,13},{6,14},{7,15},{8,0},{9,1},... | collective-permute-start | bytes 835592 | tf_op jit(solution)/shard_map/ppermute | solution.py:74
  404.2 21.2 %collective-permute-start.33 = (f32[2,64,261]{2,1,0:T(8,128)}, f32[2,64,261]{2,1,0:T(8,128)S(1)}, u32[]{:S(2)}, u32[]{:S(2)}) collective-permute-start(f32[2,64,261]{2,1,0:T(8,128)} %fusion.150), channel_id=1, source_target_pairs={{0,16},{16,0},{1,17},{17,1},{2,18},{18,2},{3,19},{19,3},{4,20},{20... | collective-permute-start | bytes 400904 | tf_op jit(solution)/shard_map/ppermute | solution.py:77
  415.3 4.3 collective-permute-start.35
  418.3 6.4 %collective-permute-start.24 = (f32[32,1024]{1,0:T(8,128)S(1)}, f32[32,1024]{1,0:T(8,128)S(1)}, u32[]{:S(2)}, u32[]{:S(2)}) collective-permute-start(f32[32,1024]{1,0:T(8,128)S(1)} %constant_dynamic-slice_fusion.28), channel_id=1, source_target_pairs={{0,1},{1,0},{2,3},{3,2},{4,5},{5,4},{6,7},{7,6},{8,9},{9,8},{10,11... | collective-permute-start | bytes 393224 | tf_op jit(solution)/shard_map/ppermute | solution.py:74
  419.6 4.4 collective-permute-start.36
  420.9 5.6 %collective-permute-start.25 = (f32[64,1024]{1,0:T(8,128)S(1)}, f32[64,1024]{1,0:T(8,128)S(1)}, u32[]{:S(2)}, u32[]{:S(2)}) collective-permute-start(f32[64,1024]{1,0:T(8,128)S(1)} %dynamic-slice_bitcast_fusion.5), channel_id=1, source_target_pairs={{0,16},{16,0},{1,17},{17,1},{2,18},{18,2},{3,19},{19,3},{4,20},{20... | collective-permute-start | bytes 786440 | tf_op jit(solution)/shard_map/ppermute | solution.py:77
  425.5 5.3 %collective-permute-start.34 = (f32[2,32,261]{2,1,0:T(8,128)S(1)}, f32[2,32,261]{2,1,0:T(8,128)S(1)}, u32[]{:S(2)}, u32[]{:S(2)}) collective-permute-start(f32[2,32,261]{2,1,0:T(8,128)S(1)} %constant_dynamic-slice_fusion.5), channel_id=1, source_target_pairs={{0,1},{1,0},{2,3},{3,2},{4,5},{5,4},{6,7},{7,6},{8,9},{9,8},{10,11... | collective-permute-start | bytes 200456 | tf_op jit(solution)/shard_map/ppermute | solution.py:74
  426.5 5.8 %collective-permute-start.26 = (f32[32,1024]{1,0:T(8,128)S(1)}, f32[32,1024]{1,0:T(8,128)S(1)}, u32[]{:S(2)}, u32[]{:S(2)}) collective-permute-start(f32[32,1024]{1,0:T(8,128)S(1)} %constant_dynamic-slice_fusion.25), channel_id=1, source_target_pairs={{0,1},{1,0},{2,3},{3,2},{4,5},{5,4},{6,7},{7,6},{8,9},{9,8},{10,11... | collective-permute-start | bytes 393224 | tf_op jit(solution)/shard_map/ppermute | solution.py:74
  (145 other events, 928.2 us)
Sparse Core Ops, SparseCore 0:
  10.9 155.5 all-gather.1
where the time goes:
time: 445 us; the launch traced here: 441 us
  waiting for transfers between devices  154 us (35%)
  matrix products  110 us (25%)
  starting transfers between devices  65.7 us (15%)
  local copies, waits for them, and re-layouts  52.3 us (12%)
  other arithmetic  42.3 us (10%)
  between operations  16.6 us (4%)
    ppermute x34, waiting for transfers between devices, swap(): return lax.ppermute(x, 'ctx', [(i, i ^ bit) for i in range(n)])  154 us
    dot_general x47, matrix products, matmul(): return jnp.einsum(form, left, right, preferred_element_type=f32)  104 us
    ppermute x34, starting transfers between devices, swap(): return lax.ppermute(x, 'ctx', [(i, i ^ bit) for i in range(n)])  63.8 us
    dynamic_slice x27, local copies, waits for them, and re-layouts, share(): lax.dynamic_slice_in_dim(a, s * n * own_w + pair * 2 * own_w, 2 * own_w,...  18.3 us
    unnamed x304, local copies, waits for them, and re-layouts  13.3 us
  transfers between devices with their start and end apart: 43, of which 26 were waited for; matrix products, arithmetic and copies ran while one was open for 35% of the time, Pallas kernels for 0%

commit v1 on v0

--- a/solution.py
+++ b/solution.py
@@ -81,29 +81,37 @@
         second = jnp.where(flag == 0, other, mine)
         return jnp.concatenate([first, second], axis=axis)
 
-    def gather(x, order, low_bit, ties=()):
-        levels = bits_all - low_bit
-        m, r, c = x.shape
-        x = x.reshape((m,) + (1,) * levels + (r, c))
-        for step, bit in enumerate(order):
-            if step < len(ties):
-                x = after(x, ties[step])
-            level = bit.bit_length() - 1 - low_bit
-            axis = 1 + (levels - 1 - level)
-            other = swap(x, bit)
-            x = ordered(x, other, (place // bit) & 1, axis)
-        return x.reshape(m, (n >> low_bit) * r, c)
+    def quad(x, low, high, axis):
+        one, two, three = swap(x, low), swap(x, high), swap(x, low | high)
+        bit_low, bit_high = (place // low) & 1, (place // high) & 1
+        near = ordered(x, one, bit_low, axis)
+        far = ordered(two, three, bit_low, axis)
+        return ordered(near, far, bit_high, axis)
 
     def both(x):
         return ordered(x, swap_core(x), core, 1)
 
-    order_a = wide + [2, 1]
-
-    def own_sequence(array, order, ties=()):
-        mine = pick(array, parity)
-        theirs = swap(pick(array, 1 - parity), 1)
-        block = ordered(mine, theirs, parity, 0)
-        return gather(block[None], order, 1, ties)[0]
+    def gather_wide(x):
+        rest = list(wide)
+        x = x[None]
+        while len(rest) > 1:
+            x = quad(x[None], rest[0], rest[1], 0)
+            x = x.reshape((-1,) + x.shape[2:])
+            rest = rest[2:]
+        for bit in rest:
+            x = ordered(x[None], swap(x[None], bit), (place // bit) & 1, 0)
+            x = x.reshape((-1,) + x.shape[2:])
+        return x
+
+    def own_steps(array):
+        other = yield swap(pick(array, 1 - parity), 1)
+        x = ordered(pick(array, parity), other, parity, 0)[None]
+        for bit in wide:
+            other = yield swap(x, bit)
+            x = ordered(x, other, (place // bit) & 1, 0)
+        other = yield swap(x, 2)
+        x = ordered(x[:, None], other[:, None], (place // 2) & 1, 1)
+        return x.reshape(total_rows, width)
 
     lanes = 384
     packed = jnp.concatenate(
@@ -116,14 +124,18 @@
         ],
         axis=1,
     )
-    packed = both(gather(packed[None], order_a, 0))[0]
+    packed = gather_wide(packed[None])[:, 0]
+    packed = quad(packed[:, None], 1, 2, 1)
+    packed = both(packed.reshape(1, n * own_w, -1))[0]
     square_first = packed[:, :width]
-    packed = packed[:, width:]
+    packed = lax.optimization_barrier(packed[:, width:])
     tall = (channels + 6 + 15) // 16 * 16
     v_key = packed[:, :tall]
     v_val = jnp.where(jnp.arange(tall) < channels, packed[:, lanes : lanes + tall], jnp.zeros((), b16))
     vecf = packed[:, lanes + channels : lanes + channels + vec_d.shape[0]].T.astype(f32)
-    lat = own_sequence(latents, wide + [2])
+    lat = ordered(pick(latents, parity), swap(pick(latents, 1 - parity), 1), parity, 0)
+    lat = gather_wide(lat[None])
+    lat = ordered(lat, swap(lat, 2), (place // 2) & 1, 1).reshape(total_rows, width)
     late_squares = lax.all_gather(w_square[1:], ("seq", "ctx"), axis=1, tiled=True)
     square = [square_first] + [late_squares[k] for k in range(9)]
 
@@ -179,14 +191,28 @@
     mean_low = mean_x.astype(b16)
 
     attended = (matmul("ci,dc->id", mean_low, v_val) + vecf[3]).astype(b16)
+    steps = own_steps(after(cotangent, attended))
+    hanging = [next(steps)]
+    gathered = []
+
+    def pace(value):
+        if not hanging:
+            return value
+        value, other = lax.optimization_barrier((value, hanging.pop()))
+        try:
+            hanging.append(steps.send(other))
+        except StopIteration as stop:
+            gathered.append(stop.value)
+        return value
+
     after_cross = latent + matmul("id,de->ie", attended, square[1]) + vecf[4]
     norm_b, unit_b, inv_b = layer_norm(after_cross, vecf[5], vecf[6], 1)
     low_b = norm_b.astype(b16)
     ffn_pre = matmul("id,de->ie", low_b, square[2]) + vecf[7]
-    ffn_act = jax.nn.gelu(ffn_pre).astype(b16)
+    ffn_act = pace(jax.nn.gelu(ffn_pre).astype(b16))
     after_ffn = after_cross + matmul("id,de->ie", ffn_act, square[3]) + vecf[8]
     norm_c, unit_c, inv_c = layer_norm(after_ffn, vecf[9], vecf[10], 1)
-    low_c = norm_c.astype(b16)
+    low_c = pace(norm_c.astype(b16))
 
     def heads(x):
         return x.reshape(total_rows, H, head_size)
@@ -200,11 +226,12 @@
     self_weight = self_exp / jnp.sum(self_exp, axis=2, keepdims=True)
     self_low = self_weight.astype(b16)
     self_mix = matmul("hij,jhe->ihe", self_low, value_heads).reshape(total_rows, width).astype(b16)
+    self_mix = pace(self_mix)
     after_self = after_ffn + matmul("id,de->ie", self_mix, square[7]) + vecf[13]
     norm_e, unit_e, inv_e = layer_norm(after_self, vecf[14], vecf[15], 1)
     low_e = norm_e.astype(b16)
     out_pre = matmul("id,de->ie", low_e, square[8]) + vecf[16]
-    out_act = jax.nn.gelu(out_pre).astype(b16)
+    out_act = pace(jax.nn.gelu(out_pre).astype(b16))
     final = (after_self + matmul("id,de->ie", out_act, square[9]) + vecf[17]).astype(b16)
 
     def own_rows(array):
@@ -214,33 +241,42 @@
 
     latents_out = own_rows(final)
 
-    cot = own_sequence(after(cotangent, low_b), wide + [2], (low_c, self_keys, self_mix))
+    part_rows = 2 * own_w
+    aligned = max(part_rows, 128)
+    base = pair * part_rows // aligned * aligned
+    inner = pair * part_rows - base
 
     def share(a):
-        parts = [lax.dynamic_slice_in_dim(a, s * n * own_w + pair * 2 * own_w, 2 * own_w, a.ndim - 1) for s in range(2)]
-        return jnp.stack(parts, axis=0)
-
-    def settle(x, axis):
-        x = pick(x, core) + swap_core(pick(x, 1 - core))
-        mine = lax.dynamic_slice_in_dim(x, parity * own_w, own_w, axis)
-        theirs = lax.dynamic_slice_in_dim(x, (1 - parity) * own_w, own_w, axis)
-        return mine + swap(theirs, 1)
+        return jnp.concatenate([lax.dynamic_slice_in_dim(a, s * n * own_w + base, aligned, 1) for s in range(2)], axis=1)
 
     def weight_grad(a, r):
-        return matmul("sia,ie->sae", jnp.moveaxis(share(a), 0, 0), r)
+        return matmul("ia,ie->ae", share(a), r)
+
+    def window(part, which):
+        return lax.dynamic_slice_in_dim(part, which * aligned + inner, part_rows, 0)
+
+    def halves(x, which):
+        return lax.dynamic_slice_in_dim(x, which * own_w, own_w, x.ndim - 2)
+
+    def settle(parts):
+        other = swap_core(jnp.stack([window(p, 1 - core) for p in parts]))
+        return jnp.stack([window(p, core) for p in parts]) + other
+
+    def settle_last(x):
+        return halves(x, parity) + swap(halves(x, 1 - parity), 1)
 
     def sums(x):
-        return jnp.sum(x.astype(f32), axis=0)
-
+        return jnp.sum(x.astype(f32), axis=0, keepdims=True)
+
+    while hanging:
+        pace(out_act)
+    cot = gathered[0]
     d_final = cot.astype(f32)
     round_nine = cot
-    part9 = weight_grad(out_act, round_nine)
     d_out_pre = gelu_back(out_pre, matmul("ie,de->id", round_nine, square[9])).astype(b16)
-    part8 = weight_grad(low_e, d_out_pre)
     d_norm_e = matmul("ie,de->id", d_out_pre, square[8])
     d_after_self = d_final + norm_back(d_norm_e, unit_e, inv_e, vecf[14], 1)
     round_seven = d_after_self.astype(b16)
-    part7 = weight_grad(self_mix, round_seven)
     d_mix = matmul("ie,de->id", round_seven, square[7]).astype(b16)
     d_mix_heads = heads(d_mix)
     d_self_weight = matmul("ihe,jhe->hij", d_mix_heads, value_heads)
@@ -250,9 +286,6 @@
     d_self_query = (matmul("hij,jhe->ihe", d_self_scores, key_heads) * scale_self).reshape(total_rows, width).astype(b16)
     d_self_keys = (matmul("hij,ihe->jhe", d_self_scores, query_heads) * scale_self).reshape(total_rows, width).astype(b16)
     d_self_values = matmul("hij,ihe->jhe", self_low, d_mix_heads).reshape(total_rows, width).astype(b16)
-    part4 = weight_grad(low_c, d_self_query)
-    part5 = weight_grad(low_c, d_self_keys)
-    part6 = weight_grad(low_c, d_self_values)
     d_norm_c = (
         matmul("ie,de->id", d_self_query, square[4])
         + matmul("ie,de->id", d_self_keys, square[5])
@@ -260,20 +293,21 @@
     )
     d_after_ffn = d_after_self + norm_back(d_norm_c, unit_c, inv_c, vecf[9], 1)
     round_three = d_after_ffn.astype(b16)
-    part3 = weight_grad(ffn_act, round_three)
     d_ffn_pre = gelu_back(ffn_pre, matmul("ie,de->id", round_three, square[3])).astype(b16)
-    part2 = weight_grad(low_b, d_ffn_pre)
     d_norm_b = matmul("ie,de->id", d_ffn_pre, square[2])
     d_after_cross = d_after_ffn + norm_back(d_norm_b, unit_b, inv_b, vecf[5], 1)
     round_one = d_after_cross.astype(b16)
-    part1 = weight_grad(attended, round_one)
     d_attended = matmul("ie,de->id", round_one, square[1]).astype(b16)
 
     pull = matmul("dc,id->ci", v_val, d_attended).astype(b16)
     delta = jnp.sum(pull.astype(f32) * mean_x, axis=0)
     pieces = split_two(top_all) + split_two(total_all) + split_two(delta)
     sent = write(pull, pieces)
-    sents = ordered(sent[None], swap(sent, 1)[None], parity, 0)
+    other = swap(sent, 1)
+    part9 = weight_grad(after(out_act, sent), round_nine)
+    part8 = weight_grad(after(low_e, sent), d_out_pre)
+    other = after(other, part9, part8)
+    sents = ordered(sent[None], other[None], parity, 0)
     pulls = sents
     side = sents[:, channels : channels + 6].astype(f32)
     top_q = side[:, 0] + side[:, 1]
@@ -285,35 +319,59 @@
     d_scores = (weight * (d_weight - delta_q[..., None])).astype(b16)
     weight_low = weight.astype(b16)
     force = matmul("qij,qcj->qci", d_scores, low_x).astype(b16)
-    d_in_norm = (matmul("qci,qij->qcj", gates, d_scores) + matmul("qci,qij->qcj", pulls, weight_low))[:, :channels]
+    mine = pick(force, parity)
+    other = swap(pick(force, 1 - parity), 1)
+    held = after(d_scores, force)
+    d_in_norm = (matmul("qci,qij->qcj", gates, held) + matmul("qci,qij->qcj", pulls, weight_low))[:, :channels]
     grad_pixels = norm_back(d_in_norm, unit_x, inv_x, gain_in[0][:, None], 1)
-    grad_vc = jnp.stack([jnp.sum(d_in_norm * unit_x, axis=(0, 2)), jnp.sum(d_in_norm, axis=(0, 2))])
-    grad_vc = grad_vc + swap_core(grad_vc)
-    for bit in [1, 2] + wide:
-        grad_vc = grad_vc + swap(grad_vc, bit)
-
-    force_sum = pick(force, parity).astype(f32) + swap(pick(force, 1 - parity), 1).astype(f32)
-    for bit in [2] + wide:
-        mine = force_sum.astype(b16)
-        force_sum = mine.astype(f32) + swap(mine, bit).astype(f32)
-    force_low = (force_sum * scale).astype(b16)
+    grad_vc = [jnp.sum(d_in_norm * unit_x, axis=(0, 2)), jnp.sum(d_in_norm, axis=(0, 2))]
+    grad_vc = jnp.pad(jnp.stack(grad_vc), ((0, 0), (0, total_rows - channels)))
+    other = after(other, grad_vc)
+    force_sum = mine.astype(f32) + other.astype(f32)
+    work = [
+        lambda t: [weight_grad(after(self_mix, t), round_seven), weight_grad(after(low_c, t), d_self_values)],
+        lambda t: [weight_grad(after(low_c, t), d_self_keys), weight_grad(after(low_c, t), d_self_query)],
+        lambda t: [
+            weight_grad(after(ffn_act, t), round_three),
+            weight_grad(after(low_b, t), d_ffn_pre),
+            weight_grad(after(attended, t), round_one),
+        ],
+    ]
+    ready = []
+    for step, bit in enumerate([2] + wide):
+        mine = write(force_sum.astype(b16), split_two(grad_vc[0]) + split_two(grad_vc[1]))
+        other = swap(mine, bit)
+        if step < len(work):
+            ready.append(work[step](mine))
+            other = after(other, *ready[-1])
+        force_sum = mine.astype(f32) + other.astype(f32)
+        grad_vc = jnp.stack([force_sum[channels] + force_sum[channels + 1], force_sum[channels + 2] + force_sum[channels + 3]])
+    while len(ready) < len(work):
+        ready.append(work[len(ready)](force_sum))
+    part7, part6 = ready[0]
+    part5, part4 = ready[1]
+    part3, part2, part1 = ready[2]
+    force_low = jnp.where(row < channels, force_sum * scale, 0.0).astype(b16)
     d_query = matmul("ci,dc->id", force_low, v_key).astype(b16)
     part0 = weight_grad(low_a, d_query)
     d_norm_a = matmul("ie,de->id", d_query, square[0])
     grad_lat = d_after_cross + norm_back(d_norm_a, unit_a, inv_a, vecf[0], 1)
     grad_latents = own_rows(grad_lat)
 
-    share_q = share(query)
-    share_att = share(d_attended)
-    part_in = jnp.stack(
-        [matmul("sia,ci->sac", share_q, force_low), matmul("sia,ci->sac", share_att, mean_low)], axis=1
-    )[..., :channels]
-    grad_input = settle(part_in, 1)
-    vec_part = jnp.stack(
+    part_q = matmul("ia,ci->ac", share(query), force_low)
+    part_att = matmul("ia,ci->ac", share(d_attended), mean_low)
+    pad_lanes = lanes - tall
+    wide_all = width + 2 * lanes
+
+    def gradients(which):
+        full = [window(part0, which)]
+        for part in (part_q, part_att):
+            full.append(jnp.pad(window(part, which), ((0, 0), (0, pad_lanes))))
+        return jnp.concatenate(full, axis=1)
+
+    late_vec = jnp.concatenate([sums(d_norm_a * unit_a), sums(d_norm_a), sums(d_query), jnp.pad(grad_vc, ((0, 0), (0, width - total_rows)))], axis=0)
+    early_vec = jnp.concatenate(
         [
-            sums(d_norm_a * unit_a),
-            sums(d_norm_a),
-            sums(d_query),
             sums(d_attended),
             sums(round_one),
             sums(d_norm_b * unit_b),
@@ -329,13 +387,27 @@
             sums(d_norm_e),
             sums(d_out_pre),
             sums(round_nine),
-        ]
-    )
-    grad_vec = settle(share(vec_part), 1)
-    late = settle(part0, 0)[None]
-    mid = settle(jnp.stack([part1, part2, part3], axis=1), 1)
-    heads_part = settle(jnp.stack([part4, part5, part6], axis=1), 1)
-    early = settle(jnp.stack([part7, part8, part9], axis=1), 1)
+        ],
+        axis=0,
+    )
+    vectors = jnp.concatenate([late_vec, early_vec, jnp.zeros((4, width), f32)], axis=0)
+    tail = jnp.pad(vectors, ((0, 0), (0, wide_all - width)))
+    own = jnp.concatenate([gradients(core), tail], axis=0)
+    own = own + swap_core(jnp.concatenate([gradients(1 - core), tail], axis=0))
+
+    def reduced(which):
+        return jnp.concatenate([halves(own[:part_rows], which), own[part_rows:]], axis=0)
+
+    own = reduced(parity) + swap(reduced(1 - parity), 1)
+    late = own[None, :own_w, :width]
+    grad_input = jnp.stack([own[:own_w, width : width + channels], own[:own_w, width + lanes : width + lanes + channels]])
+    tail = own[own_w:, :width]
+    grad_vc = tail[3:5, :channels]
+    grad_vec = lax.dynamic_slice_in_dim(tail, core * n * own_w + place * own_w, own_w, 1)
+    grad_vec = jnp.concatenate([grad_vec[:3], grad_vec[5 : 2 + vec_d.shape[0]]], axis=0)
+    early = settle_last(settle([part7, part8, part9]))
+    heads_part = settle_last(settle([part4, part5, part6]))
+    mid = settle_last(settle([part1, part2, part3]))
     grad_square = jnp.concatenate([late, mid, heads_part, early], axis=0)
     return (latents_out, grad_latents, grad_pixels, grad_square, grad_input, grad_vec, grad_vc)
 

time: 445 us -> 411 us (0.924)
  starting transfers between devices: 65.7 us -> 40.2 us
  waiting for transfers between devices: 154 us -> 141 us
  local copies, waits for them, and re-layouts: 52.3 us -> 63 us
  matrix products: 110 us -> 103 us
    ppermute x34 -> x31, starting transfers between devices: 63.8 us -> 40 us  [swap(): return lax.ppermute(x, 'ctx', [(i, i ^ bit) for i in range(n)])]
    reshape x3, local copies, waits for them, and re-layouts: 2.58 us -> 16.6 us  [heads(): return x.reshape(total_rows, H, head_size)]
    ppermute x34 -> x31, waiting for transfers between devices: 154 us -> 141 us  [swap(): return lax.ppermute(x, 'ctx', [(i, i ^ bit) for i in range(n)])]
    dynamic_slice x33 -> x18, local copies, waits for them, and re-layouts: 18.6 us -> 12.3 us  [the longest x11 8.7 us: share(): lax.dynamic_slice_in_dim(a, s * n * own_w + base, aligned, 1)]
    dot_general x47, matrix products: 104 us -> 98.1 us  [matmul(): return jnp.einsum(form, left, right, preferred_element_type=f32)]
    slice x1, local copies, waits for them, and re-layouts: 0.74 us -> 5.29 us  [body(): vecf[17]]
    unnamed x304 -> x209, local copies, waits for them, and re-layouts: 13.3 us -> 15.9 us
  transfers between devices with their start and end apart: 43 -> 37, of which waited for: 26 -> 21; matrix products, arithmetic and copies ran while one was open for 35% -> 32% of each run, Pallas kernels for 0% -> 0%
where the time goes in v1:
time: 411 us; the launch traced here: 406 us
  waiting for transfers between devices  141 us (34%)
  matrix products  103 us (25%)
  local copies, waits for them, and re-layouts  63 us (15%)
  other arithmetic  42.8 us (10%)
  starting transfers between devices  40.2 us (10%)
  between operations  16.3 us (4%)
    ppermute x31, waiting for transfers between devices, swap(): return lax.ppermute(x, 'ctx', [(i, i ^ bit) for i in range(n)])  141 us
    dot_general x47, matrix products, matmul(): return jnp.einsum(form, left, right, preferred_element_type=f32)  98.1 us
    ppermute x31, starting transfers between devices, swap(): return lax.ppermute(x, 'ctx', [(i, i ^ bit) for i in range(n)])  40 us
    reshape x3, local copies, waits for them, and re-layouts, heads(): return x.reshape(total_rows, H, head_size)  16.6 us
    unnamed x209, local copies, waits for them, and re-layouts  15.9 us
    dynamic_slice x11, local copies, waits for them, and re-layouts, share(): lax.dynamic_slice_in_dim(a, s * n * own_w + base, aligned, 1)  8.7 us
  transfers between devices with their start and end apart: 37, of which 21 were waited for; matrix products, arithmetic and copies ran while one was open for 32% of the time, Pallas kernels for 0%

profile of v1, /device:TPU:0, one launch (start us, length us, event | category | flops | bytes accessed | tf_op | source)
XLA Modules:
  0.0 406.5 jit_solution(16757640713471695562)
XLA Ops:
  11.8 5.1 %collective-permute-start.7 = (bf16[1,1,1,32,1792]{4,3,0,2,1:T(8,128)(2,1)S(1)}, bf16[1,1,1,32,1792]{4,3,0,2,1:T(8,128)(2,1)S(1)}, u32[]{:S(2)}, u32[]{:S(2)}) collective-permute-start(bf16[1,1,1,32,1792]{4,3,0,2,1:T(8,128)(2,1)S(1)} %bitcast.353), channel_id=1, source_target_pairs={{0,12},{1,13},{2,14},{3,15},{4,8},{5,9},{6,10},{7,11},{8,4},{9,5},... | collective-permute-start | bytes 344072 | tf_op jit(solution)/shard_map/ppermute | solution.py:74
  21.9 3.8 collective-permute-start.3
  27.1 2.5 collective-permute-start.1
  29.6 9.1 %collective-permute-done.6 = bf16[1,1,1,32,1792]{4,3,0,2,1:T(8,128)(2,1)S(1)} collective-permute-done((bf16[1,1,1,32,1792]{4,3,0,2,1:T(8,128)(2,1)S(1)}, bf16[1,1,1,32,1792]{4,3,0,2,1:T(8,128)(2,1)S(1)}, u32[]{:S(2)}, u32[]{:S(2)}) %collective-permute-start.6) | collective-permute-done | bytes 114720 | tf_op jit(solution)/shard_map/ppermute | solution.py:74
  38.9 2.5 collective-permute-start.10
  44.4 5.9 %collective-permute-done.2 = bf16[1,1,1,64,1024]{4,3,2,1,0:T(8,128)(2,1)S(1)} collective-permute-done((bf16[1,1,1,64,1024]{4,3,2,1,0:T(8,128)(2,1)S(1)}, bf16[1,1,1,64,1024]{4,3,2,1,0:T(8,128)(2,1)S(1)}, u32[]{:S(2)}, u32[]{:S(2)}) %collective-permute-start.2) | collective-permute-done | bytes 131104 | tf_op jit(solution)/shard_map/ppermute | solution.py:74
  50.3 9.9 %collective-permute-done.8 = bf16[4,1,32,1792]{3,2,1,0:T(8,128)(2,1)S(1)} collective-permute-done((bf16[4,1,32,1792]{3,2,1,0:T(8,128)(2,1)S(1)}, bf16[4,1,32,1792]{3,2,1,0:T(8,128)(2,1)S(1)}, u32[]{:S(2)}, u32[]{:S(2)}) %collective-permute-start.8) | collective-permute-done | bytes 458784 | tf_op jit(solution)/shard_map/ppermute | solution.py:74
  62.2 15.1 %collective-permute-done.4 = bf16[4,1,64,1024]{3,2,0,1:T(8,128)(2,1)S(1)} collective-permute-done((bf16[4,1,64,1024]{3,2,0,1:T(8,128)(2,1)S(1)}, bf16[4,1,64,1024]{3,2,0,1:T(8,128)(2,1)S(1)}, u32[]{:S(2)}, u32[]{:S(2)}) %collective-permute-start.4) | collective-permute-done | bytes 524320 | tf_op jit(solution)/shard_map/ppermute | solution.py:74
  78.6 3.1 broadcast_select_fusion.1
  82.2 5.3 %slice_reduce_fusion = (f32[1024]{0:T(1024)}, f32[1024]{0:T(1024)S(1)}, f32[1024]{0:T(1024)S(1)}, f32[1024]{0:T(1024)S(1)}, f32[1024]{0:T(1024)S(1)}, /*index=5*...) fusion(f32[18,1024]{0,1:T(8,128)S(1)} %convert_bitcast_fusion), kind=kLoop, calls=%fused_computation.221 | loop fusion | bytes 147456 | tf_op jit(solution)/shard_map/slice | solution.py:235
  92.1 12.4 %collective-permute-done.12 = bf16[272,512]{1,0:T(8,128)(2,1)S(1)} collective-permute-done((bf16[272,512]{1,0:T(8,128)(2,1)S(1)}, bf16[272,512]{1,0:T(8,128)(2,1)S(1)}, u32[]{:S(2)}, u32[]{:S(2)}) %collective-permute-start.12) | collective-permute-done | bytes 278560 | tf_op jit(solution)/shard_map/ppermute | solution.py:74
  114.4 11.8 %collective-permute-done.13 = bf16[272,512]{1,0:T(8,128)(2,1)S(1)} collective-permute-done((bf16[272,512]{1,0:T(8,128)(2,1)}, bf16[272,512]{1,0:T(8,128)(2,1)S(1)}, u32[]{:S(2)}, u32[]{:S(2)}) %collective-permute-start.13) | collective-permute-done | bytes 278560 | tf_op jit(solution)/shard_map/ppermute | solution.py:74
  128.8 6.6 %collective-permute-done.14 = bf16[272,512]{1,0:T(8,128)(2,1)} collective-permute-done((bf16[272,512]{1,0:T(8,128)(2,1)S(1)}, bf16[272,512]{1,0:T(8,128)(2,1)}, u32[]{:S(2)}, u32[]{:S(2)}) %collective-permute-start.14) | collective-permute-done | bytes 278560 | tf_op jit(solution)/shard_map/ppermute | solution.py:74
  140.9 17.7 %collective-permute-done.15 = bf16[272,512]{1,0:T(8,128)(2,1)S(1)} collective-permute-done((bf16[272,512]{1,0:T(8,128)(2,1)S(1)}, bf16[272,512]{1,0:T(8,128)(2,1)S(1)}, u32[]{:S(2)}, u32[]{:S(2)}) %collective-permute-start.15) | collective-permute-done | bytes 278560 | tf_op jit(solution)/shard_map/ppermute | solution.py:74
  158.9 2.9 collective-permute-start.16
  163.5 9.5 %collective-permute-done.16 = bf16[272,512]{1,0:T(8,128)(2,1)S(1)} collective-permute-done((bf16[272,512]{1,0:T(8,128)(2,1)S(1)}, bf16[272,512]{1,0:T(8,128)(2,1)S(1)}, u32[]{:S(2)}, u32[]{:S(2)}) %collective-permute-start.16) | collective-permute-done | bytes 278560 | tf_op jit(solution)/shard_map/ppermute | solution.py:74
  178.3 3.3 fusion.243
  182.4 4.9 %multiply_convert_fusion.5 = (bf16[512,1024]{1,0:T(8,128)(2,1)S(1)}, f32[512,1024]{1,0:T(8,128)}) fusion(f32[1024]{0:T(1024)S(1)} %get-tuple-element.104, bf16[512,1024]{1,0:T(8,128)(2,1)S(1)} %add_convert_fusion.5, bf16[9,1024,1024]{2,1,0:T(8,128)(2,1)} %all-gather.2.cloned.1.call-done), kind=kOutput, calls=%fused_computation.104 | convolution fusion | flops 1078984704 | bytes 6295552 | tf_op jit(solution)/shard_map/id,de->ie/dot_general | solution.py:15
  187.5 3.2 fusion.244
  193.2 2.5 collective-permute-start.19
  195.7 3.9 add_convert_fusion.2
  199.6 12.8 %copy.90 = bf16[512,1024]{0,1:T(8,128)(2,1)S(1)} copy(bf16[512,1024]{1,0:T(8,128)(2,1)} %add_convert_fusion.2) | data formatting | bytes 2097152 | tf_op jit(solution)/shard_map/reshape | solution.py:218
  212.5 4.3 %fusion.76 = bf16[512,1024]{1,0:T(8,128)(2,1)} fusion(bf16[512,1024]{1,0:T(8,128)(2,1)S(1)} %add_convert_fusion.4, bf16[9,1024,1024]{2,1,0:T(8,128)(2,1)} %all-gather.2.cloned.1.call-done), kind=kOutput, calls=%fused_computation.150 | convolution fusion | flops 1074266112 | bytes 4194304 | tf_op jit(solution)/shard_map/id,de->ie/dot_general | solution.py:15
  218.3 5.1 %fusion.245 = (f32[8,512]{1,0:T(8,128)S(1)}, f32[8,512,512]{1,2,0:T(8,128)}) fusion(bf16[512,8,128]{0,2,1:T(8,128)(2,1)S(1)} %bitcast.347, bf16[512,8,128]{0,2,1:T(8,128)(2,1)S(1)} %bitcast.345), kind=kOutput, calls=%fused_computation.592 | convolution fusion | flops 543162880 | bytes 10502144 | tf_op jit(solution)/shard_map/sub | solution.py:225
  223.4 3.3 fusion.80
  236.9 2.7 multiply_convert_fusion.4
  239.6 3.3 collective-permute-done.20
  244.0 3.3 convert_reduce_fusion.2
  247.3 2.3 multiply_reduce_fusion.2
  256.4 6.0 %convert_reduce_fusion.4 = (f32[8,128]{1,0:T(8,128)}, bf16[8,128,512]{2,1,0:T(8,128)(2,1)S(1)}) fusion(bf16[512,8,128]{0,2,1:T(8,128)(2,1)} %bitcast.351, f32[8,512,512]{1,2,0:T(8,128)} %get-tuple-element.282, f32[8,512]{1,0:T(8,128)S(1)} %get-tuple-element.281), kind=kOutput, calls=%fused_computation.67 | convolution fusion | flops 542637056 | bytes 10506240 | tf_op jit(solution)/shard_map/hij,ihe->jhe/dot_general | solution.py:15
  262.5 4.4 %multiply_reduce_fusion = (f32[8,512]{1,0:T(8,128)S(1)}, f32[8,512,512]{1,2,0:T(8,128)S(1)}) fusion(f32[8,512,512]{1,2,0:T(8,128)} %get-tuple-element.282, f32[8,512]{1,0:T(8,128)S(1)} %get-tuple-element.281, bf16[512,8,128]{0,2,1:T(8,128)(2,1)S(1)} %bitcast.352, bf16[64,8,8,128]{3,2,1,0:T(8,128)(2,1)S(1)} %copy-done.94), kind=kOutput, calls=%fused_computation.2 | convolution fusion | flops 543158272 | bytes 18907136 | tf_op jit(solution)/shard_map/ihe,jhe->hij/dot_general | solution.py:15
  267.1 2.8 multiply_convert_fusion
  272.3 2.9 fusion.53
  275.2 3.1 fusion.55
  278.3 4.7 %multiply_reduce_fusion.3 = (f32[1024]{0:T(1024)}, f32[512]{0:T(512)S(1)}, f32[512]{0:T(512)S(1)}, f32[1024]{0:T(1024)}, f32[512,1024]{1,0:T(8,128)S(1)}) fusion(f32[512,1024]{1,0:T(8,128)S(1)} %copy-done.9, f32[512]{0:T(512)S(1)} %add_rsqrt_fusion.3, f32[512]{0:T(512)S(1)} %broadcast_multiply_fusion.13, f32[1024]{0:T(1024)S(1)} %get-tuple-element.102, ...), kind=kOutput, calls=%fused_computation.69 | convolution fusion | flops 1079505920 | bytes 11554816 | tf_op jit(solution)/shard_map/ie,de->id/dot_general | solution.py:15
  284.6 4.9 %convert_reduce_fusion.7 = (f32[1024]{0:T(1024)}, bf16[512,1024]{1,0:T(8,128)(2,1)S(1)}) fusion(f32[512,1024]{1,0:T(8,128)S(1)} %copy-done.92, f32[1024]{0:T(1024)S(1)} %copy-done.75, bf16[9,1024,1024]{2,1,0:T(8,128)(2,1)} %all-gather.2.cloned.1.call-done, f32[512,1024]{1,0:T(8,128)S(1)} %get-tuple-element.145), kind=kOutput, calls=%fused_computation.71 | convolution fusion | flops 1086323712 | bytes 7348224 | tf_op jit(solution)/shard_map/ie,de->id/dot_general | solution.py:15
  289.5 4.0 multiply_reduce_fusion.4
  294.3 3.8 convert_reduce_fusion.9
  299.9 3.0 add_convert_fusion
  317.4 3.0 copy.80
  325.5 4.0 collective-permute-done.24
  333.9 3.6 collective-permute-done.25
  347.4 2.9 collective-permute-done.26
  352.0 2.4 multiply_reduce_fusion.5
  359.1 2.3 concatenate.221
  373.9 5.8 %collective-permute-done.33 = f32[3,32,1024]{2,1,0:T(8,128)S(1)} collective-permute-done((f32[3,32,1024]{2,1,0:T(8,128)S(1)}, f32[3,32,1024]{2,1,0:T(8,128)S(1)}, u32[]{:S(2)}, u32[]{:S(2)}) %collective-permute-start.33) | collective-permute-done | bytes 393248 | tf_op jit(solution)/shard_map/ppermute | solution.py:74
  379.7 8.4 %collective-permute-done.31 = f32[3,32,1024]{2,1,0:T(8,128)S(1)} collective-permute-done((f32[3,32,1024]{2,1,0:T(8,128)S(1)}, f32[3,32,1024]{2,1,0:T(8,128)S(1)}, u32[]{:S(2)}, u32[]{:S(2)}) %collective-permute-start.31) | collective-permute-done | bytes 393248 | tf_op jit(solution)/shard_map/ppermute | solution.py:74
  388.1 8.1 %collective-permute-done.29 = f32[56,1792]{1,0:T(8,128)S(1)} collective-permute-done((f32[56,1792]{1,0:T(8,128)S(1)}, f32[56,1792]{1,0:T(8,128)S(1)}, u32[]{:S(2)}, u32[]{:S(2)}) %collective-permute-start.29) | collective-permute-done | bytes 401440 | tf_op jit(solution)/shard_map/ppermute | solution.py:74
  (489 shorter events, 132.1 us)
Async XLA Ops:
  7.2 12.1 %copy-start.86 = (bf16[2,261]{1,0:T(2,128)(2,1)S(1)}, bf16[2,261]{1,0:T(2,128)(2,1)}, u32[]{:S(2)}) copy-start(bf16[2,261]{1,0:T(2,128)(2,1)} %param.14) | copy-start | bytes 3136
  7.2 12.1 %copy-start = (bf16[2,261,1024]{2,0,1:T(2,128)(2,1)S(1)}, bf16[2,261,1024]{2,0,1:T(2,128)(2,1)}, u32[]{:S(2)}) copy-start(bf16[2,261,1024]{2,0,1:T(2,128)(2,1)} %param.8) | copy-start | bytes 3207172
  7.2 171.1 %all-gather.2.cloned.1.call-start = ((), (), s32[]{:S(2)}) async-start(), calls=%async_computation | async-start | bytes 19464192 | tf_op jit(solution)/shard_map/all_gather | solution.py:139
  11.8 17.8 %collective-permute-start.7 = (bf16[1,1,1,32,1792]{4,3,0,2,1:T(8,128)(2,1)S(1)}, bf16[1,1,1,32,1792]{4,3,0,2,1:T(8,128)(2,1)S(1)}, u32[]{:S(2)}, u32[]{:S(2)}) collective-permute-start(bf16[1,1,1,32,1792]{4,3,0,2,1:T(8,128)(2,1)S(1)} %bitcast.353), channel_id=1, source_target_pairs={{0,12},{1,13},{2,14},{3,15},{4,8},{5,9},{6,10},{7,11},{8,4},{9,5},... | collective-permute-start | bytes 344072 | tf_op jit(solution)/shard_map/ppermute | solution.py:74
  16.9 21.8 %collective-permute-start.6 = (bf16[1,1,1,32,1792]{4,3,0,2,1:T(8,128)(2,1)S(1)}, bf16[1,1,1,32,1792]{4,3,0,2,1:T(8,128)(2,1)S(1)}, u32[]{:S(2)}, u32[]{:S(2)}) collective-permute-start(bf16[1,1,1,32,1792]{4,3,0,2,1:T(8,128)(2,1)S(1)} %bitcast.354), channel_id=1, source_target_pairs={{0,8},{1,9},{2,10},{3,11},{4,12},{5,13},{6,14},{7,15},{8,0},{9,1},... | collective-permute-start | bytes 344072 | tf_op jit(solution)/shard_map/ppermute | solution.py:74
  16.9 10.2 %collective-permute-start.5 = (bf16[1,1,1,32,1792]{4,3,0,2,1:T(8,128)(2,1)S(1)}, bf16[1,1,1,32,1792]{4,3,0,2,1:T(8,128)(2,1)S(1)}, u32[]{:S(2)}, u32[]{:S(2)}) collective-permute-start(bf16[1,1,1,32,1792]{4,3,0,2,1:T(8,128)(2,1)S(1)} %bitcast.355), channel_id=1, source_target_pairs={{0,4},{1,5},{2,6},{3,7},{4,0},{5,1},{6,2},{7,3},{8,12},{9,13},{10,... | collective-permute-start | bytes 344072 | tf_op jit(solution)/shard_map/ppermute | solution.py:74
  17.6 4.3 %collective-permute-start = (bf16[32,1024]{1,0:T(8,128)(2,1)S(1)}, bf16[32,1024]{1,0:T(8,128)(2,1)S(1)}, u32[]{:S(2)}, u32[]{:S(2)}) collective-permute-start(bf16[32,1024]{1,0:T(8,128)(2,1)S(1)} %dynamic-slice_bitcast_fusion.21), channel_id=1, source_target_pairs={{0,1},{1,0},{2,3},{3,2},{4,5},{5,4},{6,7},{7,6},{8,9},{9,8},{10,11... | collective-permute-start | bytes 196616 | tf_op jit(solution)/shard_map/ppermute | solution.py:74
  21.9 22.5 %collective-permute-start.3 = (bf16[1,1,1,64,1024]{4,3,2,1,0:T(8,128)(2,1)S(1)}, bf16[1,1,1,64,1024]{4,3,2,1,0:T(8,128)(2,1)S(1)}, u32[]{:S(2)}, u32[]{:S(2)}) collective-permute-start(bf16[1,1,1,64,1024]{4,3,2,1,0:T(8,128)(2,1)S(1)} %maximum_bitcast_fusion.3), channel_id=1, source_target_pairs={{0,12},{1,13},{2,14},{3,15},{4,8},{5,9},{6,10},{7,11},{8,4},{9,5},... | collective-permute-start | bytes 393224 | tf_op jit(solution)/shard_map/ppermute | solution.py:74
  25.8 24.5 %collective-permute-start.2 = (bf16[1,1,1,64,1024]{4,3,2,1,0:T(8,128)(2,1)S(1)}, bf16[1,1,1,64,1024]{4,3,2,1,0:T(8,128)(2,1)S(1)}, u32[]{:S(2)}, u32[]{:S(2)}) collective-permute-start(bf16[1,1,1,64,1024]{4,3,2,1,0:T(8,128)(2,1)S(1)} %maximum_bitcast_fusion.3), channel_id=1, source_target_pairs={{0,8},{1,9},{2,10},{3,11},{4,12},{5,13},{6,14},{7,15},{8,0},{9,1},... | collective-permute-start | bytes 393224 | tf_op jit(solution)/shard_map/ppermute | solution.py:74
  27.1 15.8 %collective-permute-start.1 = (bf16[1,1,1,64,1024]{4,3,2,1,0:T(8,128)(2,1)S(1)}, bf16[1,1,1,64,1024]{4,3,2,1,0:T(8,128)(2,1)S(1)}, u32[]{:S(2)}, u32[]{:S(2)}) collective-permute-start(bf16[1,1,1,64,1024]{4,3,2,1,0:T(8,128)(2,1)S(1)} %maximum_bitcast_fusion.3), channel_id=1, source_target_pairs={{0,4},{1,5},{2,6},{3,7},{4,0},{5,1},{6,2},{7,3},{8,12},{9,13},{10,... | collective-permute-start | bytes 393224 | tf_op jit(solution)/shard_map/ppermute | solution.py:74
  38.9 21.4 %collective-permute-start.10 = (bf16[4,1,32,1792]{3,2,1,0:T(8,128)(2,1)S(1)}, bf16[4,1,32,1792]{3,2,1,0:T(8,128)(2,1)S(1)}, u32[]{:S(2)}, u32[]{:S(2)}) collective-permute-start(bf16[4,1,32,1792]{3,2,1,0:T(8,128)(2,1)S(1)} %maximum_bitcast_fusion.2), channel_id=1, source_target_pairs={{0,3},{1,2},{2,1},{3,0},{4,7},{5,6},{6,5},{7,4},{8,11},{9,10},{10,... | collective-permute-start | bytes 1376264 | tf_op jit(solution)/shard_map/ppermute | solution.py:74
  41.4 18.9 %collective-permute-start.9 = (bf16[4,1,32,1792]{3,2,1,0:T(8,128)(2,1)S(1)}, bf16[4,1,32,1792]{3,2,1,0:T(8,128)(2,1)S(1)}, u32[]{:S(2)}, u32[]{:S(2)}) collective-permute-start(bf16[4,1,32,1792]{3,2,1,0:T(8,128)(2,1)S(1)} %maximum_bitcast_fusion.2), channel_id=1, source_target_pairs={{0,2},{1,3},{2,0},{3,1},{4,6},{5,7},{6,4},{7,5},{8,10},{9,11},{10,... | collective-permute-start | bytes 1376264 | tf_op jit(solution)/shard_map/ppermute | solution.py:74
  43.0 17.2 %collective-permute-start.8 = (bf16[4,1,32,1792]{3,2,1,0:T(8,128)(2,1)S(1)}, bf16[4,1,32,1792]{3,2,1,0:T(8,128)(2,1)S(1)}, u32[]{:S(2)}, u32[]{:S(2)}) collective-permute-start(bf16[4,1,32,1792]{3,2,1,0:T(8,128)(2,1)S(1)} %maximum_bitcast_fusion.2), channel_id=1, source_target_pairs={{0,1},{1,0},{2,3},{3,2},{4,5},{5,4},{6,7},{7,6},{8,9},{9,8},{10,11... | collective-permute-start | bytes 1376264 | tf_op jit(solution)/shard_map/ppermute | solution.py:74
  61.9 16.7 %collective-permute-start.11 = (bf16[1,512,1792]{2,1,0:T(8,128)(2,1)}, bf16[1,512,1792]{2,1,0:T(8,128)(2,1)}, u32[]{:S(2)}, u32[]{:S(2)}) collective-permute-start(bf16[1,512,1792]{2,1,0:T(8,128)(2,1)} %bitcast.11), channel_id=1, source_target_pairs={{0,16},{16,0},{1,17},{17,1},{2,18},{18,2},{3,19},{19,3},{4,20},{20... | collective-permute-start | bytes 5505032 | tf_op jit(solution)/shard_map/ppermute | solution.py:77
  62.0 15.3 %collective-permute-start.4 = (bf16[4,1,64,1024]{3,2,0,1:T(8,128)(2,1)S(1)}, bf16[4,1,64,1024]{3,2,0,1:T(8,128)(2,1)S(1)}, u32[]{:S(2)}, u32[]{:S(2)}) collective-permute-start(bf16[4,1,64,1024]{3,2,0,1:T(8,128)(2,1)S(1)} %maximum_bitcast_fusion.1), channel_id=1, source_target_pairs={{0,2},{1,3},{2,0},{3,1},{4,6},{5,7},{6,4},{7,5},{8,10},{9,11},{10,... | collective-permute-start | bytes 1572872 | tf_op jit(solution)/shard_map/ppermute | solution.py:74
  78.6 99.7 %copy-start.1 = (f32[4,2,64,1024]{3,2,1,0:T(8,128)}, f32[4,2,64,1024]{3,2,1,0:T(8,128)S(1)}, u32[]{:S(2)}) copy-start(f32[4,2,64,1024]{3,2,1,0:T(8,128)S(1)} %copy.58) | copy-start | bytes 6291460
  87.5 94.9 %copy-start.74 = (f32[1024]{0:T(1024)}, f32[1024]{0:T(1024)S(1)}, u32[]{:S(2)}) copy-start(f32[1024]{0:T(1024)S(1)} %get-tuple-element.104) | copy-start | bytes 12292
  89.9 14.5 %collective-permute-start.12 = (bf16[272,512]{1,0:T(8,128)(2,1)S(1)}, bf16[272,512]{1,0:T(8,128)(2,1)S(1)}, u32[]{:S(2)}, u32[]{:S(2)}) collective-permute-start(bf16[272,512]{1,0:T(8,128)(2,1)S(1)} %fusion.84), channel_id=1, source_target_pairs={{0,1},{1,0},{2,3},{3,2},{4,5},{5,4},{6,7},{7,6},{8,9},{9,8},{10,11... | collective-permute-start | bytes 835592 | tf_op jit(solution)/shard_map/ppermute | solution.py:74
  92.1 15.2 %copy-start.37 = (bf16[2,261,1024]{2,1,0:T(8,128)(2,1)}, bf16[2,261,1024]{2,1,0:T(8,128)(2,1)S(1)}, u32[]{:S(2)}) copy-start(bf16[2,261,1024]{2,1,0:T(8,128)(2,1)S(1)} %fusion.14) | copy-start | bytes 3207172
  110.9 15.3 %collective-permute-start.13 = (bf16[272,512]{1,0:T(8,128)(2,1)}, bf16[272,512]{1,0:T(8,128)(2,1)S(1)}, u32[]{:S(2)}, u32[]{:S(2)}) collective-permute-start(bf16[272,512]{1,0:T(8,128)(2,1)} %dynamic-slice_bitcast_fusion.1), channel_id=1, source_target_pairs={{0,1},{1,0},{2,3},{3,2},{4,5},{5,4},{6,7},{7,6},{8,9},{9,8},{10,11... | collective-permute-start | bytes 835592 | tf_op jit(solution)/shard_map/ppermute | solution.py:74
  128.2 7.3 %collective-permute-start.14 = (bf16[272,512]{1,0:T(8,128)(2,1)S(1)}, bf16[272,512]{1,0:T(8,128)(2,1)}, u32[]{:S(2)}, u32[]{:S(2)}) collective-permute-start(bf16[272,512]{1,0:T(8,128)(2,1)S(1)} %fusion.136), channel_id=1, source_target_pairs={{0,2},{1,3},{2,0},{3,1},{4,6},{5,7},{6,4},{7,5},{8,10},{9,11},{10,... | collective-permute-start | bytes 835592 | tf_op jit(solution)/shard_map/ppermute | solution.py:74
  128.8 45.5 %copy-start.28 = (bf16[1024,768]{1,0:T(8,128)(2,1)S(1)}, bf16[1024,768]{1,0:T(8,128)(2,1)}, u32[]{:S(2)}) copy-start(bf16[1024,768]{1,0:T(8,128)(2,1)} %copy-done.27) | copy-start | bytes 4718596
  128.8 45.5 %copy-start.90 = (pred[272]{0:T(512)(128)(4,1)S(1)}, pred[272]{0:T(512)(128)(4,1)}, u32[]{:S(2)}) copy-start(pred[272]{0:T(512)(128)(4,1)} %iota_compare_fusion.11) | copy-start | bytes 820
  137.5 21.1 %collective-permute-start.15 = (bf16[272,512]{1,0:T(8,128)(2,1)S(1)}, bf16[272,512]{1,0:T(8,128)(2,1)S(1)}, u32[]{:S(2)}, u32[]{:S(2)}) collective-permute-start(bf16[272,512]{1,0:T(8,128)(2,1)S(1)} %fusion.128), channel_id=1, source_target_pairs={{0,4},{1,5},{2,6},{3,7},{4,0},{5,1},{6,2},{7,3},{8,12},{9,13},{10,... | collective-permute-start | bytes 835592 | tf_op jit(solution)/shard_map/ppermute | solution.py:74
  158.9 17.3 %copy-start.51 = (bf16[272,512]{1,0:T(8,128)(2,1)}, bf16[272,512]{1,0:T(8,128)(2,1)S(1)}, u32[]{:S(2)}) copy-start(bf16[272,512]{1,0:T(8,128)(2,1)S(1)} %fusion.132) | copy-start | bytes 835588
  158.9 14.1 %collective-permute-start.16 = (bf16[272,512]{1,0:T(8,128)(2,1)S(1)}, bf16[272,512]{1,0:T(8,128)(2,1)S(1)}, u32[]{:S(2)}, u32[]{:S(2)}) collective-permute-start(bf16[272,512]{1,0:T(8,128)(2,1)S(1)} %fusion.132), channel_id=1, source_target_pairs={{0,8},{1,9},{2,10},{3,11},{4,12},{5,13},{6,14},{7,15},{8,0},{9,1},... | collective-permute-start | bytes 835592 | tf_op jit(solution)/shard_map/ppermute | solution.py:74
  176.2 11.1 %collective-permute-start.17 = (bf16[32,1024]{1,0:T(8,128)(2,1)S(1)}, bf16[32,1024]{1,0:T(8,128)(2,1)S(1)}, u32[]{:S(2)}, u32[]{:S(2)}) collective-permute-start(bf16[32,1024]{1,0:T(8,128)(2,1)S(1)} %dynamic-slice_bitcast_fusion.20), channel_id=1, source_target_pairs={{0,1},{1,0},{2,3},{3,2},{4,5},{5,4},{6,7},{7,6},{8,9},{9,8},{10,11... | collective-permute-start | bytes 196616 | tf_op jit(solution)/shard_map/ppermute | solution.py:74
  178.3 120.8 %copy-start.68 = (bf16[512]{0:T(512)(128)(2,1)}, bf16[512]{0:T(512)(128)(2,1)S(1)}, u32[]{:S(2)}) copy-start(bf16[512]{0:T(512)(128)(2,1)S(1)} %get-tuple-element.128) | copy-start | bytes 3076
  187.4 5.0 %collective-permute-start.18 = (bf16[1,64,1024]{2,1,0:T(8,128)(2,1)S(1)}, bf16[1,64,1024]{2,1,0:T(8,128)(2,1)S(1)}, u32[]{:S(2)}, u32[]{:S(2)}) collective-permute-start(bf16[1,64,1024]{2,1,0:T(8,128)(2,1)S(1)} %maximum_bitcast_fusion.4), channel_id=1, source_target_pairs={{0,4},{1,5},{2,6},{3,7},{4,0},{5,1},{6,2},{7,3},{8,12},{9,13},{10,... | collective-permute-start | bytes 393224 | tf_op jit(solution)/shard_map/ppermute | solution.py:74
  192.0 20.5 %copy-start.25 = (bf16[512,1024]{1,0:T(8,128)(2,1)}, bf16[512,1024]{1,0:T(8,128)(2,1)S(1)}, u32[]{:S(2)}) copy-start(bf16[512,1024]{1,0:T(8,128)(2,1)S(1)} %add_convert_fusion.4) | copy-start | bytes 3145732
  193.2 35.5 %collective-permute-start.19 = (bf16[2,64,1024]{2,1,0:T(8,128)(2,1)}, bf16[2,64,1024]{2,1,0:T(8,128)(2,1)}, u32[]{:S(2)}, u32[]{:S(2)}) collective-permute-start(bf16[2,64,1024]{2,1,0:T(8,128)(2,1)} %pad_maximum_fusion.19), channel_id=1, source_target_pairs={{0,8},{1,9},{2,10},{3,11},{4,12},{5,13},{6,14},{7,15},{8,0},{9,1},... | collective-permute-start | bytes 786440 | tf_op jit(solution)/shard_map/ppermute | solution.py:74
  231.0 11.9 %collective-permute-start.20 = (bf16[4,64,1024]{2,1,0:T(8,128)(2,1)S(1)}, bf16[4,64,1024]{2,1,0:T(8,128)(2,1)S(1)}, u32[]{:S(2)}, u32[]{:S(2)}) collective-permute-start(bf16[4,64,1024]{2,1,0:T(8,128)(2,1)S(1)} %pad_maximum_fusion.10), channel_id=1, source_target_pairs={{0,2},{1,3},{2,0},{3,1},{4,6},{5,7},{6,4},{7,5},{8,10},{9,11},{10,... | collective-permute-start | bytes 1572872 | tf_op jit(solution)/shard_map/ppermute | solution.py:74
  256.4 10.4 %slice-start = ((s8[8388608]{0:T(1024)(128)(4,1)}), s8[4194304]{0:T(1024)(128)(4,1)S(1)}, s32[]{:S(2)}) async-start(s8[8388608]{0:T(1024)(128)(4,1)} %bitcast.339), calls=%async_computation.1 | async-start | bytes 8388608
  299.5 9.4 %collective-permute-start.22 = (bf16[272,512]{1,0:T(8,128)(2,1)S(1)}, bf16[272,512]{1,0:T(8,128)(2,1)S(1)}, u32[]{:S(2)}, u32[]{:S(2)}) collective-permute-start(bf16[272,512]{1,0:T(8,128)(2,1)S(1)} %select_select_fusion.2), channel_id=1, source_target_pairs={{0,1},{1,0},{2,3},{3,2},{4,5},{5,4},{6,7},{7,6},{8,9},{9,8},{10,11... | collective-permute-start | bytes 835592 | tf_op jit(solution)/shard_map/ppermute | solution.py:74
  302.9 5.2 %collective-permute-start.21 = (bf16[32,1024]{1,0:T(8,128)(2,1)S(1)}, bf16[32,1024]{1,0:T(8,128)(2,1)S(1)}, u32[]{:S(2)}, u32[]{:S(2)}) collective-permute-start(bf16[32,1024]{1,0:T(8,128)(2,1)S(1)} %constant_dynamic-slice_fusion.36), channel_id=1, source_target_pairs={{0,1},{1,0},{2,3},{3,2},{4,5},{5,4},{6,7},{7,6},{8,9},{9,8},{10,11... | collective-permute-start | bytes 196616 | tf_op jit(solution)/shard_map/ppermute | solution.py:74
  316.0 6.6 %collective-permute-start.23 = (bf16[272,512]{1,0:T(8,128)(2,1)S(1)}, bf16[272,512]{1,0:T(8,128)(2,1)S(1)}, u32[]{:S(2)}, u32[]{:S(2)}) collective-permute-start(bf16[272,512]{1,0:T(8,128)(2,1)S(1)} %dynamic-slice_bitcast_fusion), channel_id=1, source_target_pairs={{0,1},{1,0},{2,3},{3,2},{4,5},{5,4},{6,7},{7,6},{8,9},{9,8},{10,11... | collective-permute-start | bytes 835592 | tf_op jit(solution)/shard_map/ppermute | solution.py:74
  322.8 6.6 %collective-permute-start.24 = (bf16[272,512]{1,0:T(8,128)(2,1)S(1)}, bf16[272,512]{1,0:T(8,128)(2,1)S(1)}, u32[]{:S(2)}, u32[]{:S(2)}) collective-permute-start(bf16[272,512]{1,0:T(8,128)(2,1)S(1)} %fusion.140), channel_id=1, source_target_pairs={{0,2},{1,3},{2,0},{3,1},{4,6},{5,7},{6,4},{7,5},{8,10},{9,11},{10,... | collective-permute-start | bytes 835592 | tf_op jit(solution)/shard_map/ppermute | solution.py:74
  324.9 21.0 %collective-permute-start.34 = (f32[3,64,1024]{2,1,0:T(8,128)S(1)}, f32[3,64,1024]{2,1,0:T(8,128)S(1)}, u32[]{:S(2)}, u32[]{:S(2)}) collective-permute-start(f32[3,64,1024]{2,1,0:T(8,128)S(1)} %pad_maximum_fusion.7), channel_id=1, source_target_pairs={{0,16},{16,0},{1,17},{17,1},{2,18},{18,2},{3,19},{19,3},{4,20},{20... | collective-permute-start | bytes 2359304 | tf_op jit(solution)/shard_map/ppermute | solution.py:77
  330.9 6.6 %collective-permute-start.25 = (bf16[272,512]{1,0:T(8,128)(2,1)S(1)}, bf16[272,512]{1,0:T(8,128)(2,1)S(1)}, u32[]{:S(2)}, u32[]{:S(2)}) collective-permute-start(bf16[272,512]{1,0:T(8,128)(2,1)S(1)} %select_select_fusion.1), channel_id=1, source_target_pairs={{0,4},{1,5},{2,6},{3,7},{4,0},{5,1},{6,2},{7,3},{8,12},{9,13},{10,... | collective-permute-start | bytes 835592 | tf_op jit(solution)/shard_map/ppermute | solution.py:74
  333.9 32.3 %collective-permute-start.32 = (f32[3,64,1024]{2,1,0:T(8,128)}, f32[3,64,1024]{2,1,0:T(8,128)}, u32[]{:S(2)}, u32[]{:S(2)}) collective-permute-start(f32[3,64,1024]{2,1,0:T(8,128)} %pad_maximum_fusion.6), channel_id=1, source_target_pairs={{0,16},{16,0},{1,17},{17,1},{2,18},{18,2},{3,19},{19,3},{4,20},{20... | collective-permute-start | bytes 2359304 | tf_op jit(solution)/shard_map/ppermute | solution.py:77
  337.9 12.4 %collective-permute-start.26 = (bf16[272,512]{1,0:T(8,128)(2,1)S(1)}, bf16[272,512]{1,0:T(8,128)(2,1)S(1)}, u32[]{:S(2)}, u32[]{:S(2)}) collective-permute-start(bf16[272,512]{1,0:T(8,128)(2,1)S(1)} %select_select_fusion), channel_id=1, source_target_pairs={{0,8},{1,9},{2,10},{3,11},{4,12},{5,13},{6,14},{7,15},{8,0},{9,1},... | collective-permute-start | bytes 835592 | tf_op jit(solution)/shard_map/ppermute | solution.py:74
  345.8 24.3 %collective-permute-start.30 = (f32[3,64,1024]{2,1,0:T(8,128)}, f32[3,64,1024]{2,1,0:T(8,128)}, u32[]{:S(2)}, u32[]{:S(2)}) collective-permute-start(f32[3,64,1024]{2,1,0:T(8,128)} %pad_maximum_fusion.5), channel_id=1, source_target_pairs={{0,16},{16,0},{1,17},{17,1},{2,18},{18,2},{3,19},{19,3},{4,20},{20... | collective-permute-start | bytes 2359304 | tf_op jit(solution)/shard_map/ppermute | solution.py:77
  346.7 22.4 %collective-permute-start.35 = (f32[3,32,1024]{2,1,0:T(8,128)}, f32[3,32,1024]{2,1,0:T(8,128)}, u32[]{:S(2)}, u32[]{:S(2)}) collective-permute-start(f32[3,32,1024]{2,1,0:T(8,128)} %constant_dynamic-slice_fusion.2), channel_id=1, source_target_pairs={{0,1},{1,0},{2,3},{3,2},{4,5},{5,4},{6,7},{7,6},{8,9},{9,8},{10,11... | collective-permute-start | bytes 1179656 | tf_op jit(solution)/shard_map/ppermute | solution.py:74
  355.8 8.7 %collective-permute-start.27 = (f32[32,1024]{1,0:T(8,128)}, f32[32,1024]{1,0:T(8,128)}, u32[]{:S(2)}, u32[]{:S(2)}) collective-permute-start(f32[32,1024]{1,0:T(8,128)} %constant_dynamic-slice_fusion.19), channel_id=1, source_target_pairs={{0,1},{1,0},{2,3},{3,2},{4,5},{5,4},{6,7},{7,6},{8,9},{9,8},{10,11... | collective-permute-start | bytes 393224 | tf_op jit(solution)/shard_map/ppermute | solution.py:74
  364.4 7.7 %collective-permute-start.28 = (f32[88,1792]{1,0:T(8,128)S(1)}, f32[88,1792]{1,0:T(8,128)S(1)}, u32[]{:S(2)}, u32[]{:S(2)}) collective-permute-start(f32[88,1792]{1,0:T(8,128)S(1)} %fusion.111), channel_id=1, source_target_pairs={{0,16},{16,0},{1,17},{17,1},{2,18},{18,2},{3,19},{19,3},{4,20},{20... | collective-permute-start | bytes 1892360 | tf_op jit(solution)/shard_map/ppermute | solution.py:77
  367.6 12.1 %collective-permute-start.33 = (f32[3,32,1024]{2,1,0:T(8,128)S(1)}, f32[3,32,1024]{2,1,0:T(8,128)S(1)}, u32[]{:S(2)}, u32[]{:S(2)}) collective-permute-start(f32[3,32,1024]{2,1,0:T(8,128)S(1)} %constant_dynamic-slice_fusion.3), channel_id=1, source_target_pairs={{0,1},{1,0},{2,3},{3,2},{4,5},{5,4},{6,7},{7,6},{8,9},{9,8},{10,11... | collective-permute-start | bytes 1179656 | tf_op jit(solution)/shard_map/ppermute | solution.py:74
  371.5 16.6 %collective-permute-start.31 = (f32[3,32,1024]{2,1,0:T(8,128)S(1)}, f32[3,32,1024]{2,1,0:T(8,128)S(1)}, u32[]{:S(2)}, u32[]{:S(2)}) collective-permute-start(f32[3,32,1024]{2,1,0:T(8,128)S(1)} %constant_dynamic-slice_fusion.4), channel_id=1, source_target_pairs={{0,1},{1,0},{2,3},{3,2},{4,5},{5,4},{6,7},{7,6},{8,9},{9,8},{10,11... | collective-permute-start | bytes 1179656 | tf_op jit(solution)/shard_map/ppermute | solution.py:74
  372.4 23.8 %collective-permute-start.29 = (f32[56,1792]{1,0:T(8,128)S(1)}, f32[56,1792]{1,0:T(8,128)S(1)}, u32[]{:S(2)}, u32[]{:S(2)}) collective-permute-start(f32[56,1792]{1,0:T(8,128)S(1)} %pad_maximum_fusion.11), channel_id=1, source_target_pairs={{0,1},{1,0},{2,3},{3,2},{4,5},{5,4},{6,7},{7,6},{8,9},{9,8},{10,11... | collective-permute-start | bytes 1204232 | tf_op jit(solution)/shard_map/ppermute | solution.py:74
  (91 other events, 332.2 us)
Sparse Core Ops, SparseCore 0:
  10.9 153.6 all-gather.1

commit v2 on v1

--- a/solution.py
+++ b/solution.py
@@ -258,12 +258,16 @@
     def halves(x, which):
         return lax.dynamic_slice_in_dim(x, which * own_w, own_w, x.ndim - 2)
 
-    def settle(parts):
-        other = swap_core(jnp.stack([window(p, 1 - core) for p in parts]))
-        return jnp.stack([window(p, core) for p in parts]) + other
-
-    def settle_last(x):
-        return halves(x, parity) + swap(halves(x, 1 - parity), 1)
+    def settle(parts, extra=()):
+        return swap_core(jnp.concatenate([window(p, 1 - core) for p in parts] + list(extra), axis=0))
+
+    def settled(parts, other, extra=()):
+        return jnp.concatenate([window(p, core) for p in parts] + list(extra), axis=0) + other
+
+    def halved(x, count, which):
+        top = x[: count * part_rows].reshape(count, part_rows, -1)
+        top = halves(top, which).reshape(count * own_w, -1)
+        return jnp.concatenate([top, x[count * part_rows :]], axis=0)
 
     def sums(x):
         return jnp.sum(x.astype(f32), axis=0, keepdims=True)
@@ -327,50 +331,7 @@
     grad_vc = [jnp.sum(d_in_norm * unit_x, axis=(0, 2)), jnp.sum(d_in_norm, axis=(0, 2))]
     grad_vc = jnp.pad(jnp.stack(grad_vc), ((0, 0), (0, total_rows - channels)))
     other = after(other, grad_vc)
-    force_sum = mine.astype(f32) + other.astype(f32)
-    work = [
-        lambda t: [weight_grad(after(self_mix, t), round_seven), weight_grad(after(low_c, t), d_self_values)],
-        lambda t: [weight_grad(after(low_c, t), d_self_keys), weight_grad(after(low_c, t), d_self_query)],
-        lambda t: [
-            weight_grad(after(ffn_act, t), round_three),
-            weight_grad(after(low_b, t), d_ffn_pre),
-            weight_grad(after(attended, t), round_one),
-        ],
-    ]
-    ready = []
-    for step, bit in enumerate([2] + wide):
-        mine = write(force_sum.astype(b16), split_two(grad_vc[0]) + split_two(grad_vc[1]))
-        other = swap(mine, bit)
-        if step < len(work):
-            ready.append(work[step](mine))
-            other = after(other, *ready[-1])
-        force_sum = mine.astype(f32) + other.astype(f32)
-        grad_vc = jnp.stack([force_sum[channels] + force_sum[channels + 1], force_sum[channels + 2] + force_sum[channels + 3]])
-    while len(ready) < len(work):
-        ready.append(work[len(ready)](force_sum))
-    part7, part6 = ready[0]
-    part5, part4 = ready[1]
-    part3, part2, part1 = ready[2]
-    force_low = jnp.where(row < channels, force_sum * scale, 0.0).astype(b16)
-    d_query = matmul("ci,dc->id", force_low, v_key).astype(b16)
-    part0 = weight_grad(low_a, d_query)
-    d_norm_a = matmul("ie,de->id", d_query, square[0])
-    grad_lat = d_after_cross + norm_back(d_norm_a, unit_a, inv_a, vecf[0], 1)
-    grad_latents = own_rows(grad_lat)
-
-    part_q = matmul("ia,ci->ac", share(query), force_low)
-    part_att = matmul("ia,ci->ac", share(d_attended), mean_low)
-    pad_lanes = lanes - tall
-    wide_all = width + 2 * lanes
-
-    def gradients(which):
-        full = [window(part0, which)]
-        for part in (part_q, part_att):
-            full.append(jnp.pad(window(part, which), ((0, 0), (0, pad_lanes))))
-        return jnp.concatenate(full, axis=1)
-
-    late_vec = jnp.concatenate([sums(d_norm_a * unit_a), sums(d_norm_a), sums(d_query), jnp.pad(grad_vc, ((0, 0), (0, width - total_rows)))], axis=0)
-    early_vec = jnp.concatenate(
+    early_vec = lambda: jnp.concatenate(
         [
             sums(d_attended),
             sums(round_one),
@@ -387,10 +348,84 @@
             sums(d_norm_e),
             sums(d_out_pre),
             sums(round_nine),
+            jnp.zeros((1, width), f32),
         ],
         axis=0,
     )
-    vectors = jnp.concatenate([late_vec, early_vec, jnp.zeros((4, width), f32)], axis=0)
+    store = {"first": [part9, part8]}
+
+    def work_one(t):
+        store["first"] += [weight_grad(after(self_mix, t), round_seven), weight_grad(after(low_c, t), d_self_values)]
+        return store["first"][2:]
+
+    def work_two(t):
+        held = after(store["first"][0], t)
+        store["first"][0] = held
+        got = settle(store["first"])
+        store["second"] = [
+            weight_grad(after(low_c, t), d_self_keys),
+            weight_grad(after(low_c, t), d_self_query),
+            weight_grad(after(ffn_act, t), round_three),
+        ]
+        store["vec"] = early_vec()
+        store["first"] = settled(store["first"], got)
+        return store["second"] + [store["first"], store["vec"]]
+
+    def work_three(t):
+        mine = after(store["first"], t)
+        got = swap(halved(mine, 4, 1 - parity), 1)
+        other = settle([after(store["second"][0], t)] + store["second"][1:], [store["vec"]])
+        store["third"] = [weight_grad(after(low_b, t), d_ffn_pre), weight_grad(after(attended, t), round_one)]
+        store["second"] = settled(store["second"], other, [store["vec"]])
+        store["first"] = halved(mine, 4, parity) + got
+        return store["third"] + [store["first"], store["second"]]
+
+    def work_four(t):
+        mine = after(store["second"], t)
+        got = swap(halved(mine, 3, 1 - parity), 1)
+        other = settle([after(store["third"][0], t)] + store["third"][1:])
+        store["third"] = settled(store["third"], other)
+        store["second"] = halved(mine, 3, parity) + got
+        return [store["second"], store["third"]]
+
+    work = [work_one, work_two, work_three, work_four]
+    other = after(other, *work[0](force))
+    force_sum = mine.astype(f32) + other.astype(f32)
+    done = 1
+    for step, bit in enumerate([2] + wide):
+        mine = write(force_sum.astype(b16), split_two(grad_vc[0]) + split_two(grad_vc[1]))
+        other = swap(mine, bit)
+        if done < len(work):
+            other = after(other, *work[done](mine))
+            done += 1
+        force_sum = mine.astype(f32) + other.astype(f32)
+        grad_vc = jnp.stack([force_sum[channels] + force_sum[channels + 1], force_sum[channels + 2] + force_sum[channels + 3]])
+    while done < len(work):
+        work[done](force_sum)
+        done += 1
+    mine = after(store["third"], force_sum)
+    third_other = swap(halved(mine, 2, 1 - parity), 1)
+    third = halved(mine, 2, parity) + third_other
+    force_low = jnp.where(row < channels, force_sum * scale, 0.0).astype(b16)
+    d_query = matmul("ci,dc->id", force_low, v_key).astype(b16)
+    part0 = weight_grad(low_a, d_query)
+    d_norm_a = matmul("ie,de->id", d_query, square[0])
+    grad_lat = d_after_cross + norm_back(d_norm_a, unit_a, inv_a, vecf[0], 1)
+    grad_latents = own_rows(grad_lat)
+
+    part_q = matmul("ia,ci->ac", share(query), force_low)
+    part_att = matmul("ia,ci->ac", share(d_attended), mean_low)
+    pad_lanes = lanes - tall
+    wide_all = width + 2 * lanes
+
+    def gradients(which):
+        full = [window(part0, which)]
+        for part in (part_q, part_att):
+            full.append(jnp.pad(window(part, which), ((0, 0), (0, pad_lanes))))
+        return jnp.concatenate(full, axis=1)
+
+    late_vec = jnp.concatenate([sums(d_norm_a * unit_a), sums(d_norm_a), sums(d_query), jnp.pad(grad_vc, ((0, 0), (0, width - total_rows)))], axis=0)
+    vectors = jnp.concatenate([late_vec, jnp.zeros((3, width), f32)], axis=0)
     tail = jnp.pad(vectors, ((0, 0), (0, wide_all - width)))
     own = jnp.concatenate([gradients(core), tail], axis=0)
     own = own + swap_core(jnp.concatenate([gradients(1 - core), tail], axis=0))
@@ -403,12 +438,12 @@
     grad_input = jnp.stack([own[:own_w, width : width + channels], own[:own_w, width + lanes : width + lanes + channels]])
     tail = own[own_w:, :width]
     grad_vc = tail[3:5, :channels]
-    grad_vec = lax.dynamic_slice_in_dim(tail, core * n * own_w + place * own_w, own_w, 1)
-    grad_vec = jnp.concatenate([grad_vec[:3], grad_vec[5 : 2 + vec_d.shape[0]]], axis=0)
-    early = settle_last(settle([part7, part8, part9]))
-    heads_part = settle_last(settle([part4, part5, part6]))
-    mid = settle_last(settle([part1, part2, part3]))
-    grad_square = jnp.concatenate([late, mid, heads_part, early], axis=0)
+    vectors = jnp.concatenate([tail[:3], store["second"][3 * own_w :]], axis=0)
+    grad_vec = lax.dynamic_slice_in_dim(vectors, core * n * own_w + place * own_w, own_w, 1)[: vec_d.shape[0]]
+    nine, eight, seven, six = store["first"].reshape(4, own_w, width)
+    five, four, three = store["second"][: 3 * own_w].reshape(3, own_w, width)
+    two, one = third.reshape(2, own_w, width)
+    grad_square = jnp.stack([late[0], one, two, three, four, five, six, seven, eight, nine])
     return (latents_out, grad_latents, grad_pixels, grad_square, grad_input, grad_vec, grad_vc)
 
 

time: 411 us -> 430 us (1.046)
  local copies, waits for them, and re-layouts: 63 us -> 79.2 us
    concatenate x1 -> x3, local copies, waits for them, and re-layouts: 2.29 us -> 15 us  [the longest x1 7.17 us: settle(): jnp.concatenate([window(p, 1 - core) for p in parts] + list(extra), axis=0)]
    dynamic_slice x3 -> x14, local copies, waits for them, and re-layouts: 2.76 us -> 7.26 us  [window(): return lax.dynamic_slice_in_dim(part, which * aligned + inner, part_rows, 0)]
    unnamed x209 -> x294, local copies, waits for them, and re-layouts: 15.9 us -> 16.8 us
  transfers between devices with their start and end apart: 37 -> 37, of which waited for: 21 -> 20; matrix products, arithmetic and copies ran while one was open for 32% -> 32% of each run, Pallas kernels for 0% -> 0%
where the time goes in v2:
time: 430 us; the launch traced here: 425 us
  waiting for transfers between devices  138 us (32%)
  matrix products  103 us (24%)
  local copies, waits for them, and re-layouts  79.2 us (18%)
  other arithmetic  46.5 us (11%)
  starting transfers between devices  40.8 us (9%)
  between operations  16.9 us (4%)
    ppermute x31, waiting for transfers between devices, swap(): return lax.ppermute(x, 'ctx', [(i, i ^ bit) for i in range(n)])  138 us
    dot_general x47, matrix products, matmul(): return jnp.einsum(form, left, right, preferred_element_type=f32)  98.4 us
    ppermute x31, starting transfers between devices, swap(): return lax.ppermute(x, 'ctx', [(i, i ^ bit) for i in range(n)])  40.6 us
    unnamed x294, local copies, waits for them, and re-layouts  16.8 us
    reshape x3, local copies, waits for them, and re-layouts, heads(): return x.reshape(total_rows, H, head_size)  16.6 us
    dynamic_slice x11, local copies, waits for them, and re-layouts, share(): lax.dynamic_slice_in_dim(a, s * n * own_w + base, aligned, 1)  9.75 us
  transfers between devices with their start and end apart: 37, of which 20 were waited for; matrix products, arithmetic and copies ran while one was open for 32% of the time, Pallas kernels for 0%

profile of v2, /device:TPU:0, one launch (start us, length us, event | category | flops | bytes accessed | tf_op | source)
XLA Modules:
  0.0 425.1 jit_solution(3945080531477866107)
XLA Ops:
  11.8 5.1 %collective-permute-start.7 = (bf16[1,1,1,32,1792]{4,3,0,2,1:T(8,128)(2,1)S(1)}, bf16[1,1,1,32,1792]{4,3,0,2,1:T(8,128)(2,1)S(1)}, u32[]{:S(2)}, u32[]{:S(2)}) collective-permute-start(bf16[1,1,1,32,1792]{4,3,0,2,1:T(8,128)(2,1)S(1)} %bitcast.371), channel_id=1, source_target_pairs={{0,12},{1,13},{2,14},{3,15},{4,8},{5,9},{6,10},{7,11},{8,4},{9,5},... | collective-permute-start | bytes 344072 | tf_op jit(solution)/shard_map/ppermute | solution.py:74
  22.0 3.8 collective-permute-start.3
  27.2 2.5 collective-permute-start.1
  29.7 9.1 %collective-permute-done.6 = bf16[1,1,1,32,1792]{4,3,0,2,1:T(8,128)(2,1)S(1)} collective-permute-done((bf16[1,1,1,32,1792]{4,3,0,2,1:T(8,128)(2,1)S(1)}, bf16[1,1,1,32,1792]{4,3,0,2,1:T(8,128)(2,1)S(1)}, u32[]{:S(2)}, u32[]{:S(2)}) %collective-permute-start.6) | collective-permute-done | bytes 114720 | tf_op jit(solution)/shard_map/ppermute | solution.py:74
  38.9 2.6 collective-permute-start.10
  44.4 5.9 %collective-permute-done.2 = bf16[1,1,1,64,1024]{4,3,2,1,0:T(8,128)(2,1)S(1)} collective-permute-done((bf16[1,1,1,64,1024]{4,3,2,1,0:T(8,128)(2,1)S(1)}, bf16[1,1,1,64,1024]{4,3,2,1,0:T(8,128)(2,1)S(1)}, u32[]{:S(2)}, u32[]{:S(2)}) %collective-permute-start.2) | collective-permute-done | bytes 131104 | tf_op jit(solution)/shard_map/ppermute | solution.py:74
  50.3 9.9 %collective-permute-done.8 = bf16[4,1,32,1792]{3,2,1,0:T(8,128)(2,1)S(1)} collective-permute-done((bf16[4,1,32,1792]{3,2,1,0:T(8,128)(2,1)S(1)}, bf16[4,1,32,1792]{3,2,1,0:T(8,128)(2,1)S(1)}, u32[]{:S(2)}, u32[]{:S(2)}) %collective-permute-start.8) | collective-permute-done | bytes 458784 | tf_op jit(solution)/shard_map/ppermute | solution.py:74
  62.3 15.0 %collective-permute-done.4 = bf16[4,1,64,1024]{3,2,0,1:T(8,128)(2,1)S(1)} collective-permute-done((bf16[4,1,64,1024]{3,2,0,1:T(8,128)(2,1)S(1)}, bf16[4,1,64,1024]{3,2,0,1:T(8,128)(2,1)S(1)}, u32[]{:S(2)}, u32[]{:S(2)}) %collective-permute-start.4) | collective-permute-done | bytes 524320 | tf_op jit(solution)/shard_map/ppermute | solution.py:74
  78.6 3.1 broadcast_select_fusion.1
  82.2 5.3 %slice_reduce_fusion = (f32[1024]{0:T(1024)}, f32[1024]{0:T(1024)}, f32[1024]{0:T(1024)S(1)}, f32[1024]{0:T(1024)S(1)}, f32[1024]{0:T(1024)}, /*index=5*/f32[102...) fusion(f32[18,1024]{0,1:T(8,128)S(1)} %convert_bitcast_fusion), kind=kLoop, calls=%fused_computation.204 | loop fusion | bytes 147456 | tf_op jit(solution)/shard_map/slice | solution.py:235
  92.1 12.4 %collective-permute-done.12 = bf16[272,512]{1,0:T(8,128)(2,1)S(1)} collective-permute-done((bf16[272,512]{1,0:T(8,128)(2,1)S(1)}, bf16[272,512]{1,0:T(8,128)(2,1)S(1)}, u32[]{:S(2)}, u32[]{:S(2)}) %collective-permute-start.12) | collective-permute-done | bytes 278560 | tf_op jit(solution)/shard_map/ppermute | solution.py:74
  114.4 11.8 %collective-permute-done.13 = bf16[272,512]{1,0:T(8,128)(2,1)S(1)} collective-permute-done((bf16[272,512]{1,0:T(8,128)(2,1)}, bf16[272,512]{1,0:T(8,128)(2,1)S(1)}, u32[]{:S(2)}, u32[]{:S(2)}) %collective-permute-start.13) | collective-permute-done | bytes 278560 | tf_op jit(solution)/shard_map/ppermute | solution.py:74
  128.8 6.6 %collective-permute-done.14 = bf16[272,512]{1,0:T(8,128)(2,1)} collective-permute-done((bf16[272,512]{1,0:T(8,128)(2,1)S(1)}, bf16[272,512]{1,0:T(8,128)(2,1)}, u32[]{:S(2)}, u32[]{:S(2)}) %collective-permute-start.14) | collective-permute-done | bytes 278560 | tf_op jit(solution)/shard_map/ppermute | solution.py:74
  141.0 17.7 %collective-permute-done.15 = bf16[272,512]{1,0:T(8,128)(2,1)S(1)} collective-permute-done((bf16[272,512]{1,0:T(8,128)(2,1)S(1)}, bf16[272,512]{1,0:T(8,128)(2,1)S(1)}, u32[]{:S(2)}, u32[]{:S(2)}) %collective-permute-start.15) | collective-permute-done | bytes 278560 | tf_op jit(solution)/shard_map/ppermute | solution.py:74
  159.0 2.9 collective-permute-start.16
  163.6 9.5 %collective-permute-done.16 = bf16[272,512]{1,0:T(8,128)(2,1)S(1)} collective-permute-done((bf16[272,512]{1,0:T(8,128)(2,1)S(1)}, bf16[272,512]{1,0:T(8,128)(2,1)S(1)}, u32[]{:S(2)}, u32[]{:S(2)}) %collective-permute-start.16) | collective-permute-done | bytes 278560 | tf_op jit(solution)/shard_map/ppermute | solution.py:74
  177.4 3.3 fusion.255
  181.7 4.7 %multiply_convert_fusion.5 = (bf16[512,1024]{1,0:T(8,128)(2,1)S(1)}, f32[512,1024]{1,0:T(8,128)}) fusion(f32[1024]{0:T(1024)S(1)} %copy-done.108, bf16[512,1024]{1,0:T(8,128)(2,1)S(1)} %add_convert_fusion.5, bf16[9,1024,1024]{2,1,0:T(8,128)(2,1)} %all-gather.2.cloned.1.call-done), kind=kOutput, calls=%fused_computation.104 | convolution fusion | flops 1078984704 | bytes 6295552 | tf_op jit(solution)/shard_map/id,de->ie/dot_general | solution.py:15
  186.5 3.2 fusion.256
  192.2 2.6 collective-permute-start.19
  194.8 3.9 add_convert_fusion.2
  198.7 12.8 %copy.90 = bf16[512,1024]{0,1:T(8,128)(2,1)S(1)} copy(bf16[512,1024]{1,0:T(8,128)(2,1)} %add_convert_fusion.2) | data formatting | bytes 2097152 | tf_op jit(solution)/shard_map/reshape | solution.py:218
  211.6 4.3 %fusion.76 = bf16[512,1024]{1,0:T(8,128)(2,1)} fusion(bf16[512,1024]{1,0:T(8,128)(2,1)S(1)} %add_convert_fusion.4, bf16[9,1024,1024]{2,1,0:T(8,128)(2,1)} %all-gather.2.cloned.1.call-done), kind=kOutput, calls=%fused_computation.150 | convolution fusion | flops 1074266112 | bytes 4194304 | tf_op jit(solution)/shard_map/id,de->ie/dot_general | solution.py:15
  217.4 5.1 %fusion.257 = (f32[8,512]{1,0:T(8,128)S(1)}, f32[8,512,512]{1,2,0:T(8,128)}) fusion(bf16[512,8,128]{0,2,1:T(8,128)(2,1)S(1)} %bitcast.361, bf16[512,8,128]{0,2,1:T(8,128)(2,1)S(1)} %bitcast.359), kind=kOutput, calls=%fused_computation.614 | convolution fusion | flops 543162880 | bytes 10502144 | tf_op jit(solution)/shard_map/sub | solution.py:225
  222.5 3.3 fusion.80
  236.2 2.7 multiply_convert_fusion.4
  238.9 3.2 collective-permute-done.20
  243.2 3.3 convert_reduce_fusion.3
  246.5 2.3 multiply_reduce_fusion.4
  255.7 6.0 %convert_reduce_fusion.5 = (f32[8,128]{1,0:T(8,128)}, bf16[8,128,512]{2,1,0:T(8,128)(2,1)S(1)}) fusion(bf16[512,8,128]{0,2,1:T(8,128)(2,1)} %bitcast.369, f32[8,512,512]{1,2,0:T(8,128)} %get-tuple-element.298, f32[8,512]{1,0:T(8,128)S(1)} %get-tuple-element.297), kind=kOutput, calls=%fused_computation.71 | convolution fusion | flops 542637056 | bytes 10506240 | tf_op jit(solution)/shard_map/hij,ihe->jhe/dot_general | solution.py:15
  261.7 4.3 %multiply_reduce_fusion = (f32[8,512]{1,0:T(8,128)S(1)}, f32[8,512,512]{1,2,0:T(8,128)S(1)}) fusion(f32[8,512,512]{1,2,0:T(8,128)} %get-tuple-element.298, f32[8,512]{1,0:T(8,128)S(1)} %get-tuple-element.297, bf16[512,8,128]{0,2,1:T(8,128)(2,1)S(1)} %bitcast.370, bf16[64,8,8,128]{3,2,1,0:T(8,128)(2,1)S(1)} %copy-done.132), kind=kOutput, calls=%fused_computation.2 | convolution fusion | flops 543158272 | bytes 18907136 | tf_op jit(solution)/shard_map/ihe,jhe->hij/dot_general | solution.py:15
  266.3 2.8 multiply_convert_fusion
  271.5 2.9 fusion.53
  274.4 3.1 fusion.55
  277.5 4.7 %multiply_reduce_fusion.5 = (f32[1024]{0:T(1024)}, f32[512]{0:T(512)S(1)}, f32[512]{0:T(512)S(1)}, f32[1024]{0:T(1024)}, f32[512,1024]{1,0:T(8,128)S(1)}) fusion(f32[512,1024]{1,0:T(8,128)S(1)} %copy-done.11, f32[512]{0:T(512)S(1)} %add_rsqrt_fusion.3, f32[512]{0:T(512)S(1)} %broadcast_multiply_fusion.13, f32[1024]{0:T(1024)S(1)} %get-tuple-element.116, ...), kind=kOutput, calls=%fused_computation.73 | convolution fusion | flops 1079505920 | bytes 11554816 | tf_op jit(solution)/shard_map/ie,de->id/dot_general | solution.py:15
  283.8 4.8 %convert_reduce_fusion.8 = (f32[1024]{0:T(1024)}, bf16[512,1024]{1,0:T(8,128)(2,1)S(1)}) fusion(f32[512,1024]{1,0:T(8,128)S(1)} %copy-done.130, f32[1024]{0:T(1024)S(1)} %copy-done.109, bf16[9,1024,1024]{2,1,0:T(8,128)(2,1)} %all-gather.2.cloned.1.call-done, f32[512,1024]{1,0:T(8,128)S(1)} %get-tuple-element.159), kind=kOutput, calls=%fused_computation.75 | convolution fusion | flops 1086323712 | bytes 7348224 | tf_op jit(solution)/shard_map/ie,de->id/dot_general | solution.py:15
  288.7 4.4 %multiply_reduce_fusion.6 = (f32[1024]{0:T(1024)}, f32[512]{0:T(512)S(1)}, f32[512]{0:T(512)S(1)}, f32[1024]{0:T(1024)}, f32[512,1024]{1,0:T(8,128)S(1)}) fusion(f32[512,1024]{1,0:T(8,128)S(1)} %copy-done.8, f32[512]{0:T(512)S(1)} %add_rsqrt_fusion.4, f32[512]{0:T(512)S(1)} %broadcast_multiply_fusion.14, f32[1024]{0:T(1024)S(1)} %get-tuple-element.120, ...), kind=kOutput, calls=%fused_computation.76 | convolution fusion | flops 1078457344 | bytes 7360512 | tf_op jit(solution)/shard_map/ie,de->id/dot_general | solution.py:15
  294.0 4.5 %convert_reduce_fusion.10 = (f32[1024]{0:T(1024)}, bf16[512,1024]{1,0:T(8,128)(2,1)S(1)}) fusion(bf16[9,1024,1024]{2,1,0:T(8,128)(2,1)} %all-gather.2.cloned.1.call-done, f32[512,1024]{1,0:T(8,128)S(1)} %get-tuple-element.161), kind=kOutput, calls=%fused_computation.78 | convolution fusion | flops 1075837952 | bytes 5246976 | tf_op jit(solution)/shard_map/ie,de->id/dot_general | solution.py:15
  300.1 3.0 add_convert_fusion
  319.8 4.7 %collective-permute-done.23 = bf16[272,512]{1,0:T(8,128)(2,1)S(1)} collective-permute-done((bf16[272,512]{1,0:T(8,128)(2,1)S(1)}, bf16[272,512]{1,0:T(8,128)(2,1)S(1)}, u32[]{:S(2)}, u32[]{:S(2)}) %collective-permute-start.23) | collective-permute-done | bytes 278560 | tf_op jit(solution)/shard_map/ppermute | solution.py:74
  332.4 7.0 %concatenate.242 = f32[208,1024]{1,0:T(8,128)} concatenate(f32[64,1024]{1,0:T(8,128)} %constant_dynamic-slice_fusion.29, f32[64,1024]{1,0:T(8,128)} %get-tuple-element.204, f32[64,1024]{1,0:T(8,128)} %get-tuple-element.202, f32[1,1024]{1,0:T(1,128)} %bitcast.406, f32[1,1024]{1,0:T(1,128)S(1)} %bitcast.381, f32[1,1024]{1,0:T(1,128)} %bitcast.402, f32[1,1024]{1,0:T(1,128)} %bitcast.404, ...), dimensions={0} | concatenate | bytes 1703936 | tf_op jit(solution)/shard_map/concatenate | solution.py:265
  348.1 7.2 %concatenate.243 = f32[208,1024]{1,0:T(8,128)} concatenate(f32[64,1024]{1,0:T(8,128)} %constant_dynamic-slice_fusion.26, f32[64,1024]{1,0:T(8,128)} %get-tuple-element.203, f32[64,1024]{1,0:T(8,128)} %get-tuple-element.201, f32[1,1024]{1,0:T(1,128)} %bitcast.407, f32[1,1024]{1,0:T(1,128)S(1)} %bitcast.382, f32[1,1024]{1,0:T(1,128)S(1)} %bitcast.403, f32[1,1024]{1,0:T(1,128)} %bitcast.405, ...), dimensions={0} | concatenate | bytes 1703936 | tf_op jit(solution)/shard_map/concatenate | solution.py:262
  358.7 3.2 collective-permute-done.27
  368.6 9.7 %collective-permute-done.30 = f32[112,1024]{1,0:T(8,128)S(1)} collective-permute-done((f32[112,1024]{1,0:T(8,128)S(1)}, f32[112,1024]{1,0:T(8,128)S(1)}, u32[]{:S(2)}, u32[]{:S(2)}) %collective-permute-start.30) | collective-permute-done | bytes 458784 | tf_op jit(solution)/shard_map/ppermute | solution.py:74
  380.0 3.9 collective-permute-done.29
  397.8 3.0 copy.80
  405.0 5.1 %collective-permute-done.35 = f32[64,1024]{1,0:T(8,128)S(1)} collective-permute-done((f32[64,1024]{1,0:T(8,128)S(1)}, f32[64,1024]{1,0:T(8,128)S(1)}, u32[]{:S(2)}, u32[]{:S(2)}) %collective-permute-start.35) | collective-permute-done | bytes 262176 | tf_op jit(solution)/shard_map/ppermute | solution.py:74
  410.1 5.6 %collective-permute-done.34 = f32[40,1792]{1,0:T(8,128)S(1)} collective-permute-done((f32[40,1792]{1,0:T(8,128)S(1)}, f32[40,1792]{1,0:T(8,128)S(1)}, u32[]{:S(2)}, u32[]{:S(2)}) %collective-permute-start.34) | collective-permute-done | bytes 286752 | tf_op jit(solution)/shard_map/ppermute | solution.py:74
  (580 shorter events, 140.5 us)
Async XLA Ops:
  7.2 170.1 %all-gather.2.cloned.1.call-start = ((), (), s32[]{:S(2)}) async-start(), calls=%async_computation | async-start | bytes 19464192 | tf_op jit(solution)/shard_map/all_gather | solution.py:139
  11.8 17.9 %collective-permute-start.7 = (bf16[1,1,1,32,1792]{4,3,0,2,1:T(8,128)(2,1)S(1)}, bf16[1,1,1,32,1792]{4,3,0,2,1:T(8,128)(2,1)S(1)}, u32[]{:S(2)}, u32[]{:S(2)}) collective-permute-start(bf16[1,1,1,32,1792]{4,3,0,2,1:T(8,128)(2,1)S(1)} %bitcast.371), channel_id=1, source_target_pairs={{0,12},{1,13},{2,14},{3,15},{4,8},{5,9},{6,10},{7,11},{8,4},{9,5},... | collective-permute-start | bytes 344072 | tf_op jit(solution)/shard_map/ppermute | solution.py:74
  16.9 21.8 %collective-permute-start.6 = (bf16[1,1,1,32,1792]{4,3,0,2,1:T(8,128)(2,1)S(1)}, bf16[1,1,1,32,1792]{4,3,0,2,1:T(8,128)(2,1)S(1)}, u32[]{:S(2)}, u32[]{:S(2)}) collective-permute-start(bf16[1,1,1,32,1792]{4,3,0,2,1:T(8,128)(2,1)S(1)} %bitcast.372), channel_id=1, source_target_pairs={{0,8},{1,9},{2,10},{3,11},{4,12},{5,13},{6,14},{7,15},{8,0},{9,1},... | collective-permute-start | bytes 344072 | tf_op jit(solution)/shard_map/ppermute | solution.py:74
  16.9 10.2 %collective-permute-start.5 = (bf16[1,1,1,32,1792]{4,3,0,2,1:T(8,128)(2,1)S(1)}, bf16[1,1,1,32,1792]{4,3,0,2,1:T(8,128)(2,1)S(1)}, u32[]{:S(2)}, u32[]{:S(2)}) collective-permute-start(bf16[1,1,1,32,1792]{4,3,0,2,1:T(8,128)(2,1)S(1)} %bitcast.373), channel_id=1, source_target_pairs={{0,4},{1,5},{2,6},{3,7},{4,0},{5,1},{6,2},{7,3},{8,12},{9,13},{10,... | collective-permute-start | bytes 344072 | tf_op jit(solution)/shard_map/ppermute | solution.py:74
  17.6 4.3 %collective-permute-start = (bf16[32,1024]{1,0:T(8,128)(2,1)S(1)}, bf16[32,1024]{1,0:T(8,128)(2,1)S(1)}, u32[]{:S(2)}, u32[]{:S(2)}) collective-permute-start(bf16[32,1024]{1,0:T(8,128)(2,1)S(1)} %dynamic-slice_bitcast_fusion.3), channel_id=1, source_target_pairs={{0,1},{1,0},{2,3},{3,2},{4,5},{5,4},{6,7},{7,6},{8,9},{9,8},{10,11... | collective-permute-start | bytes 196616 | tf_op jit(solution)/shard_map/ppermute | solution.py:74
  19.9 289.2 %copy-start.73 = (pred[272]{0:T(512)(128)(4,1)}, pred[272]{0:T(512)(128)(4,1)S(1)}, u32[]{:S(2)}) copy-start(pred[272]{0:T(512)(128)(4,1)S(1)} %get-tuple-element.325) | copy-start | bytes 820
  19.9 289.2 %copy-start.75 = (pred[272]{0:T(512)(128)(4,1)}, pred[272]{0:T(512)(128)(4,1)S(1)}, u32[]{:S(2)}) copy-start(pred[272]{0:T(512)(128)(4,1)S(1)} %get-tuple-element.326) | copy-start | bytes 820
  22.0 22.5 %collective-permute-start.3 = (bf16[1,1,1,64,1024]{4,3,2,1,0:T(8,128)(2,1)S(1)}, bf16[1,1,1,64,1024]{4,3,2,1,0:T(8,128)(2,1)S(1)}, u32[]{:S(2)}, u32[]{:S(2)}) collective-permute-start(bf16[1,1,1,64,1024]{4,3,2,1,0:T(8,128)(2,1)S(1)} %maximum_bitcast_fusion.3), channel_id=1, source_target_pairs={{0,12},{1,13},{2,14},{3,15},{4,8},{5,9},{6,10},{7,11},{8,4},{9,5},... | collective-permute-start | bytes 393224 | tf_op jit(solution)/shard_map/ppermute | solution.py:74
  25.8 24.5 %collective-permute-start.2 = (bf16[1,1,1,64,1024]{4,3,2,1,0:T(8,128)(2,1)S(1)}, bf16[1,1,1,64,1024]{4,3,2,1,0:T(8,128)(2,1)S(1)}, u32[]{:S(2)}, u32[]{:S(2)}) collective-permute-start(bf16[1,1,1,64,1024]{4,3,2,1,0:T(8,128)(2,1)S(1)} %maximum_bitcast_fusion.3), channel_id=1, source_target_pairs={{0,8},{1,9},{2,10},{3,11},{4,12},{5,13},{6,14},{7,15},{8,0},{9,1},... | collective-permute-start | bytes 393224 | tf_op jit(solution)/shard_map/ppermute | solution.py:74
  27.2 15.8 %collective-permute-start.1 = (bf16[1,1,1,64,1024]{4,3,2,1,0:T(8,128)(2,1)S(1)}, bf16[1,1,1,64,1024]{4,3,2,1,0:T(8,128)(2,1)S(1)}, u32[]{:S(2)}, u32[]{:S(2)}) collective-permute-start(bf16[1,1,1,64,1024]{4,3,2,1,0:T(8,128)(2,1)S(1)} %maximum_bitcast_fusion.3), channel_id=1, source_target_pairs={{0,4},{1,5},{2,6},{3,7},{4,0},{5,1},{6,2},{7,3},{8,12},{9,13},{10,... | collective-permute-start | bytes 393224 | tf_op jit(solution)/shard_map/ppermute | solution.py:74
  38.9 21.4 %collective-permute-start.10 = (bf16[4,1,32,1792]{3,2,1,0:T(8,128)(2,1)S(1)}, bf16[4,1,32,1792]{3,2,1,0:T(8,128)(2,1)S(1)}, u32[]{:S(2)}, u32[]{:S(2)}) collective-permute-start(bf16[4,1,32,1792]{3,2,1,0:T(8,128)(2,1)S(1)} %maximum_bitcast_fusion.2), channel_id=1, source_target_pairs={{0,3},{1,2},{2,1},{3,0},{4,7},{5,6},{6,5},{7,4},{8,11},{9,10},{10,... | collective-permute-start | bytes 1376264 | tf_op jit(solution)/shard_map/ppermute | solution.py:74
  41.4 18.9 %collective-permute-start.9 = (bf16[4,1,32,1792]{3,2,1,0:T(8,128)(2,1)S(1)}, bf16[4,1,32,1792]{3,2,1,0:T(8,128)(2,1)S(1)}, u32[]{:S(2)}, u32[]{:S(2)}) collective-permute-start(bf16[4,1,32,1792]{3,2,1,0:T(8,128)(2,1)S(1)} %maximum_bitcast_fusion.2), channel_id=1, source_target_pairs={{0,2},{1,3},{2,0},{3,1},{4,6},{5,7},{6,4},{7,5},{8,10},{9,11},{10,... | collective-permute-start | bytes 1376264 | tf_op jit(solution)/shard_map/ppermute | solution.py:74
  43.0 17.2 %collective-permute-start.8 = (bf16[4,1,32,1792]{3,2,1,0:T(8,128)(2,1)S(1)}, bf16[4,1,32,1792]{3,2,1,0:T(8,128)(2,1)S(1)}, u32[]{:S(2)}, u32[]{:S(2)}) collective-permute-start(bf16[4,1,32,1792]{3,2,1,0:T(8,128)(2,1)S(1)} %maximum_bitcast_fusion.2), channel_id=1, source_target_pairs={{0,1},{1,0},{2,3},{3,2},{4,5},{5,4},{6,7},{7,6},{8,9},{9,8},{10,11... | collective-permute-start | bytes 1376264 | tf_op jit(solution)/shard_map/ppermute | solution.py:74
  61.9 16.7 %collective-permute-start.11 = (bf16[1,512,1792]{2,1,0:T(8,128)(2,1)}, bf16[1,512,1792]{2,1,0:T(8,128)(2,1)}, u32[]{:S(2)}, u32[]{:S(2)}) collective-permute-start(bf16[1,512,1792]{2,1,0:T(8,128)(2,1)} %bitcast.11), channel_id=1, source_target_pairs={{0,16},{16,0},{1,17},{17,1},{2,18},{18,2},{3,19},{19,3},{4,20},{20... | collective-permute-start | bytes 5505032 | tf_op jit(solution)/shard_map/ppermute | solution.py:77
  62.1 15.2 %collective-permute-start.4 = (bf16[4,1,64,1024]{3,2,0,1:T(8,128)(2,1)S(1)}, bf16[4,1,64,1024]{3,2,0,1:T(8,128)(2,1)S(1)}, u32[]{:S(2)}, u32[]{:S(2)}) collective-permute-start(bf16[4,1,64,1024]{3,2,0,1:T(8,128)(2,1)S(1)} %maximum_bitcast_fusion.1), channel_id=1, source_target_pairs={{0,2},{1,3},{2,0},{3,1},{4,6},{5,7},{6,4},{7,5},{8,10},{9,11},{10,... | collective-permute-start | bytes 1572872 | tf_op jit(solution)/shard_map/ppermute | solution.py:74
  62.2 237.2 %copy-start.77 = (pred[272]{0:T(512)(128)(4,1)}, pred[272]{0:T(512)(128)(4,1)S(1)}, u32[]{:S(2)}) copy-start(pred[272]{0:T(512)(128)(4,1)S(1)} %get-tuple-element.323) | copy-start | bytes 820
  62.2 237.2 %copy-start.80 = (pred[272]{0:T(512)(128)(4,1)}, pred[272]{0:T(512)(128)(4,1)S(1)}, u32[]{:S(2)}) copy-start(pred[272]{0:T(512)(128)(4,1)S(1)} %get-tuple-element.324) | copy-start | bytes 820
  62.3 45.0 %copy-start.87 = (pred[2,1024]{1,0:T(4,128)(4,1)}, pred[2,1024]{1,0:T(4,128)(4,1)S(1)}, u32[]{:S(2)}) copy-start(pred[2,1024]{1,0:T(4,128)(4,1)S(1)} %broadcast_compare_fusion) | copy-start | bytes 6148
  78.6 98.7 %copy-start.1 = (f32[4,2,64,1024]{3,2,1,0:T(8,128)}, f32[4,2,64,1024]{3,2,1,0:T(8,128)S(1)}, u32[]{:S(2)}) copy-start(f32[4,2,64,1024]{3,2,1,0:T(8,128)S(1)} %copy.58) | copy-start | bytes 6291460
  89.9 14.5 %collective-permute-start.12 = (bf16[272,512]{1,0:T(8,128)(2,1)S(1)}, bf16[272,512]{1,0:T(8,128)(2,1)S(1)}, u32[]{:S(2)}, u32[]{:S(2)}) collective-permute-start(bf16[272,512]{1,0:T(8,128)(2,1)S(1)} %fusion.84), channel_id=1, source_target_pairs={{0,1},{1,0},{2,3},{3,2},{4,5},{5,4},{6,7},{7,6},{8,9},{9,8},{10,11... | collective-permute-start | bytes 835592 | tf_op jit(solution)/shard_map/ppermute | solution.py:74
  110.9 15.3 %collective-permute-start.13 = (bf16[272,512]{1,0:T(8,128)(2,1)}, bf16[272,512]{1,0:T(8,128)(2,1)S(1)}, u32[]{:S(2)}, u32[]{:S(2)}) collective-permute-start(bf16[272,512]{1,0:T(8,128)(2,1)} %dynamic-slice_bitcast_fusion.1), channel_id=1, source_target_pairs={{0,1},{1,0},{2,3},{3,2},{4,5},{5,4},{6,7},{7,6},{8,9},{9,8},{10,11... | collective-permute-start | bytes 835592 | tf_op jit(solution)/shard_map/ppermute | solution.py:74
  128.2 7.3 %collective-permute-start.14 = (bf16[272,512]{1,0:T(8,128)(2,1)S(1)}, bf16[272,512]{1,0:T(8,128)(2,1)}, u32[]{:S(2)}, u32[]{:S(2)}) collective-permute-start(bf16[272,512]{1,0:T(8,128)(2,1)S(1)} %fusion.137), channel_id=1, source_target_pairs={{0,2},{1,3},{2,0},{3,1},{4,6},{5,7},{6,4},{7,5},{8,10},{9,11},{10,... | collective-permute-start | bytes 835592 | tf_op jit(solution)/shard_map/ppermute | solution.py:74
  128.8 45.0 %copy-start.34 = (bf16[1024,768]{1,0:T(8,128)(2,1)S(1)}, bf16[1024,768]{1,0:T(8,128)(2,1)}, u32[]{:S(2)}) copy-start(bf16[1024,768]{1,0:T(8,128)(2,1)} %copy-done.33) | copy-start | bytes 4718596
  128.8 45.0 %copy-start.127 = (pred[272]{0:T(512)(128)(4,1)S(1)}, pred[272]{0:T(512)(128)(4,1)}, u32[]{:S(2)}) copy-start(pred[272]{0:T(512)(128)(4,1)} %iota_compare_fusion.11) | copy-start | bytes 820
  137.5 21.2 %collective-permute-start.15 = (bf16[272,512]{1,0:T(8,128)(2,1)S(1)}, bf16[272,512]{1,0:T(8,128)(2,1)S(1)}, u32[]{:S(2)}, u32[]{:S(2)}) collective-permute-start(bf16[272,512]{1,0:T(8,128)(2,1)S(1)} %fusion.129), channel_id=1, source_target_pairs={{0,4},{1,5},{2,6},{3,7},{4,0},{5,1},{6,2},{7,3},{8,12},{9,13},{10,... | collective-permute-start | bytes 835592 | tf_op jit(solution)/shard_map/ppermute | solution.py:74
  159.0 14.1 %collective-permute-start.16 = (bf16[272,512]{1,0:T(8,128)(2,1)S(1)}, bf16[272,512]{1,0:T(8,128)(2,1)S(1)}, u32[]{:S(2)}, u32[]{:S(2)}) collective-permute-start(bf16[272,512]{1,0:T(8,128)(2,1)S(1)} %fusion.133), channel_id=1, source_target_pairs={{0,8},{1,9},{2,10},{3,11},{4,12},{5,13},{6,14},{7,15},{8,0},{9,1},... | collective-permute-start | bytes 835592 | tf_op jit(solution)/shard_map/ppermute | solution.py:74
  173.8 125.6 %copy-start.104 = (bf16[512]{0:T(512)(128)(2,1)}, bf16[512]{0:T(512)(128)(2,1)S(1)}, u32[]{:S(2)}) copy-start(bf16[512]{0:T(512)(128)(2,1)S(1)} %get-tuple-element.140) | copy-start | bytes 3076
  175.8 10.6 %collective-permute-start.17 = (bf16[32,1024]{1,0:T(8,128)(2,1)S(1)}, bf16[32,1024]{1,0:T(8,128)(2,1)S(1)}, u32[]{:S(2)}, u32[]{:S(2)}) collective-permute-start(bf16[32,1024]{1,0:T(8,128)(2,1)S(1)} %dynamic-slice_bitcast_fusion.2), channel_id=1, source_target_pairs={{0,1},{1,0},{2,3},{3,2},{4,5},{5,4},{6,7},{7,6},{8,9},{9,8},{10,11... | collective-permute-start | bytes 196616 | tf_op jit(solution)/shard_map/ppermute | solution.py:74
  177.3 122.1 %copy-start.100 = (bf16[512]{0:T(512)(128)(2,1)}, bf16[512]{0:T(512)(128)(2,1)S(1)}, u32[]{:S(2)}) copy-start(bf16[512]{0:T(512)(128)(2,1)S(1)} %get-tuple-element.142) | copy-start | bytes 3076
  177.3 122.1 %copy-start.102 = (bf16[512]{0:T(512)(128)(2,1)}, bf16[512]{0:T(512)(128)(2,1)S(1)}, u32[]{:S(2)}) copy-start(bf16[512]{0:T(512)(128)(2,1)S(1)} %get-tuple-element.143) | copy-start | bytes 3076
  186.4 5.0 %collective-permute-start.18 = (bf16[1,64,1024]{2,1,0:T(8,128)(2,1)S(1)}, bf16[1,64,1024]{2,1,0:T(8,128)(2,1)S(1)}, u32[]{:S(2)}, u32[]{:S(2)}) collective-permute-start(bf16[1,64,1024]{2,1,0:T(8,128)(2,1)S(1)} %maximum_bitcast_fusion.4), channel_id=1, source_target_pairs={{0,4},{1,5},{2,6},{3,7},{4,0},{5,1},{6,2},{7,3},{8,12},{9,13},{10,... | collective-permute-start | bytes 393224 | tf_op jit(solution)/shard_map/ppermute | solution.py:74
  192.2 35.6 %collective-permute-start.19 = (bf16[2,64,1024]{2,1,0:T(8,128)(2,1)}, bf16[2,64,1024]{2,1,0:T(8,128)(2,1)}, u32[]{:S(2)}, u32[]{:S(2)}) collective-permute-start(bf16[2,64,1024]{2,1,0:T(8,128)(2,1)} %pad_maximum_fusion.19), channel_id=1, source_target_pairs={{0,8},{1,9},{2,10},{3,11},{4,12},{5,13},{6,14},{7,15},{8,0},{9,1},... | collective-permute-start | bytes 786440 | tf_op jit(solution)/shard_map/ppermute | solution.py:74
  230.1 12.1 %collective-permute-start.20 = (bf16[4,64,1024]{2,1,0:T(8,128)(2,1)S(1)}, bf16[4,64,1024]{2,1,0:T(8,128)(2,1)S(1)}, u32[]{:S(2)}, u32[]{:S(2)}) collective-permute-start(bf16[4,64,1024]{2,1,0:T(8,128)(2,1)S(1)} %pad_maximum_fusion.9), channel_id=1, source_target_pairs={{0,2},{1,3},{2,0},{3,1},{4,6},{5,7},{6,4},{7,5},{8,10},{9,11},{10,... | collective-permute-start | bytes 1572872 | tf_op jit(solution)/shard_map/ppermute | solution.py:74
  299.7 9.3 %collective-permute-start.22 = (bf16[272,512]{1,0:T(8,128)(2,1)S(1)}, bf16[272,512]{1,0:T(8,128)(2,1)S(1)}, u32[]{:S(2)}, u32[]{:S(2)}) collective-permute-start(bf16[272,512]{1,0:T(8,128)(2,1)S(1)} %select_select_fusion.2), channel_id=1, source_target_pairs={{0,1},{1,0},{2,3},{3,2},{4,5},{5,4},{6,7},{7,6},{8,9},{9,8},{10,11... | collective-permute-start | bytes 835592 | tf_op jit(solution)/shard_map/ppermute | solution.py:74
  303.1 5.3 %collective-permute-start.21 = (bf16[32,1024]{1,0:T(8,128)(2,1)S(1)}, bf16[32,1024]{1,0:T(8,128)(2,1)S(1)}, u32[]{:S(2)}, u32[]{:S(2)}) collective-permute-start(bf16[32,1024]{1,0:T(8,128)(2,1)S(1)} %constant_dynamic-slice_fusion.56), channel_id=1, source_target_pairs={{0,1},{1,0},{2,3},{3,2},{4,5},{5,4},{6,7},{7,6},{8,9},{9,8},{10,11... | collective-permute-start | bytes 196616 | tf_op jit(solution)/shard_map/ppermute | solution.py:74
  318.0 6.6 %collective-permute-start.23 = (bf16[272,512]{1,0:T(8,128)(2,1)S(1)}, bf16[272,512]{1,0:T(8,128)(2,1)S(1)}, u32[]{:S(2)}, u32[]{:S(2)}) collective-permute-start(bf16[272,512]{1,0:T(8,128)(2,1)S(1)} %dynamic-slice_bitcast_fusion), channel_id=1, source_target_pairs={{0,1},{1,0},{2,3},{3,2},{4,5},{5,4},{6,7},{7,6},{8,9},{9,8},{10,11... | collective-permute-start | bytes 835592 | tf_op jit(solution)/shard_map/ppermute | solution.py:74
  324.8 17.1 %collective-permute-start.24 = (bf16[272,512]{1,0:T(8,128)(2,1)S(1)}, bf16[272,512]{1,0:T(8,128)(2,1)S(1)}, u32[]{:S(2)}, u32[]{:S(2)}) collective-permute-start(bf16[272,512]{1,0:T(8,128)(2,1)S(1)} %fusion.141), channel_id=1, source_target_pairs={{0,2},{1,3},{2,0},{3,1},{4,6},{5,7},{6,4},{7,5},{8,10},{9,11},{10,... | collective-permute-start | bytes 835592 | tf_op jit(solution)/shard_map/ppermute | solution.py:74
  327.0 12.4 %collective-permute-start.25 = (f32[256,1024]{1,0:T(8,128)}, f32[256,1024]{1,0:T(8,128)S(1)}, u32[]{:S(2)}, u32[]{:S(2)}) collective-permute-start(f32[256,1024]{1,0:T(8,128)} %pad_maximum_fusion.2), channel_id=1, source_target_pairs={{0,16},{16,0},{1,17},{17,1},{2,18},{18,2},{3,19},{19,3},{4,20},{20... | collective-permute-start | bytes 3145736 | tf_op jit(solution)/shard_map/ppermute | solution.py:77
  342.3 21.5 %collective-permute-start.26 = (bf16[272,512]{1,0:T(8,128)(2,1)S(1)}, bf16[272,512]{1,0:T(8,128)(2,1)}, u32[]{:S(2)}, u32[]{:S(2)}) collective-permute-start(bf16[272,512]{1,0:T(8,128)(2,1)S(1)} %select_select_fusion.1), channel_id=1, source_target_pairs={{0,4},{1,5},{2,6},{3,7},{4,0},{5,1},{6,2},{7,3},{8,12},{9,13},{10,... | collective-permute-start | bytes 835592 | tf_op jit(solution)/shard_map/ppermute | solution.py:74
  347.4 14.4 %collective-permute-start.27 = (f32[128,1024]{1,0:T(8,128)}, f32[128,1024]{1,0:T(8,128)}, u32[]{:S(2)}, u32[]{:S(2)}) collective-permute-start(f32[128,1024]{1,0:T(8,128)} %bitcast.63), channel_id=1, source_target_pairs={{0,1},{1,0},{2,3},{3,2},{4,5},{5,4},{6,7},{7,6},{8,9},{9,8},{10,11... | collective-permute-start | bytes 1572872 | tf_op jit(solution)/shard_map/ppermute | solution.py:74
  355.3 8.5 %collective-permute-start.28 = (f32[208,1024]{1,0:T(8,128)}, f32[208,1024]{1,0:T(8,128)S(1)}, u32[]{:S(2)}, u32[]{:S(2)}) collective-permute-start(f32[208,1024]{1,0:T(8,128)} %concatenate.243), channel_id=1, source_target_pairs={{0,16},{16,0},{1,17},{17,1},{2,18},{18,2},{3,19},{19,3},{4,20},{20... | collective-permute-start | bytes 2555912 | tf_op jit(solution)/shard_map/ppermute | solution.py:77
  366.4 11.9 %collective-permute-start.30 = (f32[112,1024]{1,0:T(8,128)S(1)}, f32[112,1024]{1,0:T(8,128)S(1)}, u32[]{:S(2)}, u32[]{:S(2)}) collective-permute-start(f32[112,1024]{1,0:T(8,128)S(1)} %pad_maximum_fusion.5), channel_id=1, source_target_pairs={{0,1},{1,0},{2,3},{3,2},{4,5},{5,4},{6,7},{7,6},{8,9},{9,8},{10,11... | collective-permute-start | bytes 1376264 | tf_op jit(solution)/shard_map/ppermute | solution.py:74
  367.2 11.9 %collective-permute-start.31 = (f32[128,1024]{1,0:T(8,128)S(1)}, f32[128,1024]{1,0:T(8,128)S(1)}, u32[]{:S(2)}, u32[]{:S(2)}) collective-permute-start(f32[128,1024]{1,0:T(8,128)S(1)} %pad_maximum_fusion.10), channel_id=1, source_target_pairs={{0,16},{16,0},{1,17},{17,1},{2,18},{18,2},{3,19},{19,3},{4,20},{20... | collective-permute-start | bytes 1572872 | tf_op jit(solution)/shard_map/ppermute | solution.py:77
  367.9 16.0 %collective-permute-start.29 = (bf16[272,512]{1,0:T(8,128)(2,1)S(1)}, bf16[272,512]{1,0:T(8,128)(2,1)S(1)}, u32[]{:S(2)}, u32[]{:S(2)}) collective-permute-start(bf16[272,512]{1,0:T(8,128)(2,1)S(1)} %select_select_fusion), channel_id=1, source_target_pairs={{0,8},{1,9},{2,10},{3,11},{4,12},{5,13},{6,14},{7,15},{8,0},{9,1},... | collective-permute-start | bytes 835592 | tf_op jit(solution)/shard_map/ppermute | solution.py:74
  390.6 11.0 %collective-permute-start.32 = (f32[32,1024]{1,0:T(8,128)}, f32[32,1024]{1,0:T(8,128)}, u32[]{:S(2)}, u32[]{:S(2)}) collective-permute-start(f32[32,1024]{1,0:T(8,128)} %constant_dynamic-slice_fusion.17), channel_id=1, source_target_pairs={{0,1},{1,0},{2,3},{3,2},{4,5},{5,4},{6,7},{7,6},{8,9},{9,8},{10,11... | collective-permute-start | bytes 393224 | tf_op jit(solution)/shard_map/ppermute | solution.py:74
  396.3 6.3 %collective-permute-start.33 = (f32[72,1792]{1,0:T(8,128)S(1)}, f32[72,1792]{1,0:T(8,128)S(1)}, u32[]{:S(2)}, u32[]{:S(2)}) collective-permute-start(f32[72,1792]{1,0:T(8,128)S(1)} %fusion.114), channel_id=1, source_target_pairs={{0,16},{16,0},{1,17},{17,1},{2,18},{18,2},{3,19},{19,3},{4,20},{20... | collective-permute-start | bytes 1548296 | tf_op jit(solution)/shard_map/ppermute | solution.py:77
  400.9 9.2 %collective-permute-start.35 = (f32[64,1024]{1,0:T(8,128)S(1)}, f32[64,1024]{1,0:T(8,128)S(1)}, u32[]{:S(2)}, u32[]{:S(2)}) collective-permute-start(f32[64,1024]{1,0:T(8,128)S(1)} %bitcast.374), channel_id=1, source_target_pairs={{0,1},{1,0},{2,3},{3,2},{4,5},{5,4},{6,7},{7,6},{8,9},{9,8},{10,11... | collective-permute-start | bytes 786440 | tf_op jit(solution)/shard_map/ppermute | solution.py:74
  402.8 12.9 %collective-permute-start.34 = (f32[40,1792]{1,0:T(8,128)S(1)}, f32[40,1792]{1,0:T(8,128)S(1)}, u32[]{:S(2)}, u32[]{:S(2)}) collective-permute-start(f32[40,1792]{1,0:T(8,128)S(1)} %pad_maximum_fusion.11), channel_id=1, source_target_pairs={{0,1},{1,0},{2,3},{3,2},{4,5},{5,4},{6,7},{7,6},{8,9},{9,8},{10,11... | collective-permute-start | bytes 860168 | tf_op jit(solution)/shard_map/ppermute | solution.py:74
  (130 other events, 584.2 us)
Sparse Core Ops, SparseCore 0:
  10.9 153.7 all-gather.1

commit v3 on v1

v3 whole, which is shorter than its diff:
```python
import math

import jax
import jax.numpy as jnp
from jax import lax
from jax.experimental import pallas as pl
from jax.experimental.pallas import tpu as pltpu
from jax.sharding import PartitionSpec as P

H = 8
epsilon = 1e-05
f32 = jnp.float32
b16 = jnp.bfloat16


def matmul(form, left, right):
    return jnp.einsum(form, left, right, preferred_element_type=f32)


def layer_norm(value, gain, shift, axis):
    center = value - jnp.mean(value, axis=axis, keepdims=True)
    spread = jnp.mean(center * center, axis=axis, keepdims=True)
    inverse = lax.rsqrt(spread + epsilon)
    unit = center * inverse
    return (unit * gain + shift, unit, inverse)


def norm_back(grad, unit, inverse, gain, axis):
    scaled = grad * gain
    inner = (
        scaled
        - jnp.mean(scaled, axis=axis, keepdims=True)
        - unit * jnp.mean(scaled * unit, axis=axis, keepdims=True)
    )
    return inner * inverse


def split_two(value):
    high = value.astype(b16)
    low = (value - high.astype(f32)).astype(b16)
    return high, low


def after(value, *needed):
    return lax.optimization_barrier((value,) + needed)[0]


def pick(array, index):
    return lax.dynamic_index_in_dim(array, index, 0, keepdims=False)


def latent_part(attended, lat, vectors, planes, numbers, part_rows, aligned, scale_self):
    total, width = lat.shape
    head = width // H
    extra = vectors.shape[0]
    out_rows = 9 * part_rows + extra
    shares = 2 * aligned
    stacked = shares + 16
    chunk = 32
    block = 256
    part = 128
    cubic = 0.044715
    root = math.sqrt(2.0 / math.pi)

    def kernel(
        num, att, lat_ref, vec, planes_ref, final, d_att, stream_out, keep, send,
        w, cot, low_b, act_b, low_c, q, k, v, mix, low_e, act_e, weights,
        unit_b, unit_c, unit_e, pre_b, pre_e, inv_b, inv_c, inv_e, stream, t, r, small, lhs, sems,
    ):
        parity, core, inner = num[0], num[1], num[4]

        def load(plane, slot, sem):
            return pltpu.make_async_copy(planes_ref.at[plane], w.at[slot], sems.at[sem])

        cot_copy = pltpu.make_async_copy(
            planes_ref.at[9 + parity, pl.ds(pl.multiple_of(core * total, total), total), :], cot, sems.at[11]
        )
        copies = [load(i, i, i) for i in range(7)]
        for copy in copies:
            copy.start()
        cot_copy.start()
        row_eight, row_nine = load(7, 0, 7), load(8, 1, 8)
        again_two, again_one = load(1, 1, 9), load(0, 0, 10)

        lhs[pl.ds(shares, 16), :] = jnp.ones((16, total), b16)

        def each(size, body, carry=None):
            def step(i, c):
                return body(pl.ds(pl.multiple_of(i * size, size), size), c)

            return lax.fori_loop(0, total // size, step, 0 if carry is None else carry)

        def product(a, slot, flip):
            dims = (((1,), (1 if flip else 0,)), ((), ()))
            return lax.dot_general(a, w[slot], dims, preferred_element_type=f32)

        def into_t(a_ref, slot, flip=False, add=False):
            def body(rows, c):
                o = product(a_ref[rows, :], slot, flip)
                t[rows, :] = t[rows, :] + o if add else o
                return c

            each(block, body)

        def into_low(a_ref, slot, out, flip=False, bias=None):
            def body(rows, c):
                o = product(a_ref[rows, :], slot, flip)
                if bias is not None:
                    o = o + vec[bias : bias + 1, :]
                out[rows, :] = o.astype(b16)
                return c

            each(block, body)

        def row_of(i):
            return vec[i : i + 1, :]

        def residual(before, bias, unit, inv, low, gain):
            def body(rows, c):
                x = before[rows, :].astype(f32) + t[rows, :] + row_of(bias)
                stream[rows, :] = x
                center = x - jnp.mean(x, axis=1, keepdims=True)
                inverse = lax.rsqrt(jnp.mean(center * center, axis=1, keepdims=True) + epsilon)
                u = center * inverse
                unit[rows, :] = u
                inv[rows, :] = jnp.broadcast_to(inverse, (chunk, 128))
                low[rows, :] = (u * row_of(gain) + row_of(gain + 1)).astype(b16)
                return c

            each(chunk, body)

        def activate(bias, pre, act):
            def body(rows, c):
                x = t[rows, :] + row_of(bias)
                pre[rows, :] = x
                act[rows, :] = (0.5 * x * (1.0 + jnp.tanh(root * (x + cubic * (x * x * x))))).astype(b16)
                return c

            each(chunk, body)

        def activate_back(pre):
            def body(rows, c):
                x = pre[rows, :]
                square = x * x
                h = jnp.tanh(root * (x + cubic * (square * x)))
                slope = 0.5 * (1.0 + h) + 0.5 * x * (1.0 - h * h) * (root * (1.0 + 3.0 * cubic * square))
                r[rows, :] = (t[rows, :] * slope).astype(b16)
                return c

            each(chunk, body)

        def norm_grad(before, unit, inv, gain, place):
            def body(rows, c):
                g, u = t[rows, :], unit[rows, :]
                scaled = g * row_of(gain)
                inner_grad = (
                    scaled
                    - jnp.mean(scaled, axis=1, keepdims=True)
                    - u * jnp.mean(scaled * u, axis=1, keepdims=True)
                )
                x = before[rows, :].astype(f32) + inner_grad * inv[rows, 0:1]
                stream[rows, :] = x
                r[rows, :] = x.astype(b16)
                first = c[0] + jnp.sum((g * u).reshape(chunk // 8, 8, width), axis=0)
                second = c[1] + jnp.sum(g.reshape(chunk // 8, 8, width), axis=0)
                return first, second

            zero = jnp.zeros((8, width), f32)
            first, second = each(chunk, body, (zero, zero))
            put_sum(place, jnp.sum(first, axis=0, keepdims=True))
            put_sum(place + 1, jnp.sum(second, axis=0, keepdims=True))

        def put_sum(place, value):
            keep[pl.ds(9 * part_rows + place, 1), :] = value
            send[pl.ds(9 * part_rows + place, 1), :] = value

        def gradient(index, a_ref, r_ref, place=None):
            for s in range(2):
                columns = a_ref[:, pl.ds(pl.multiple_of(num[2 + s], 128), aligned)]
                lhs[pl.ds(s * aligned, aligned), :] = columns.T
            t[pl.ds(0, stacked), :] = jnp.dot(lhs[...], r_ref[...], preferred_element_type=f32)
            near = pl.multiple_of(core * aligned + inner, 8)
            far = pl.multiple_of((1 - core) * aligned + inner, 8)
            keep[pl.ds(index * part_rows, part_rows), :] = t[pl.ds(near, part_rows), :]
            send[pl.ds(index * part_rows, part_rows), :] = t[pl.ds(far, part_rows), :]
            if place is not None:
                put_sum(place, t[pl.ds(shares, 1), :])

        for place in (keep, send):
            place[pl.ds(9 * part_rows, extra), :] = jnp.zeros((extra, width), f32)

        copies[0].wait()
        into_t(att, 0)
        row_eight.start()
        residual(lat_ref, 4, unit_b, inv_b, low_b, 5)
        copies[1].wait()
        into_t(low_b, 1)
        row_nine.start()
        activate(7, pre_b, act_b)
        copies[2].wait()
        into_t(act_b, 2)
        residual(stream, 8, unit_c, inv_c, low_c, 9)
        copies[3].wait()
        into_low(low_c, 3, q, bias=11)
        copies[4].wait()
        into_low(low_c, 4, k)
        copies[5].wait()
        into_low(low_c, 5, v, bias=12)
        for h in range(H):
            cols = slice(h * head, (h + 1) * head)

            def attend(rows, c):
                s = scale_self * lax.dot_general(
                    q[rows, cols], k[:, cols], (((1,), (1,)), ((), ())), preferred_element_type=f32
                )
                e = jnp.exp(s - jnp.max(s, axis=1, keepdims=True))
                low = (e / jnp.sum(e, axis=1, keepdims=True)).astype(b16)
                weights[h, rows, :] = low
                mix[rows, cols] = jnp.dot(low, v[:, cols], preferred_element_type=f32).astype(b16)
                return c

            each(part, attend)
        copies[6].wait()
        into_t(mix, 6)
        residual(stream, 13, unit_e, inv_e, low_e, 14)
        row_eight.wait()
        into_t(low_e, 0)
        activate(16, pre_e, act_e)
        row_nine.wait()
        into_t(act_e, 1)

        def finish(rows, c):
            final[rows, :] = (stream[rows, :] + t[rows, :] + row_of(17)).astype(b16)
            return c

        each(chunk, finish)

        cot_copy.wait()
        into_t(cot, 1, flip=True)
        again_two.start()
        activate_back(pre_e)
        gradient(8, act_e, cot, 17)
        gradient(7, low_e, r, 16)
        into_t(r, 0, flip=True)
        again_one.start()
        norm_grad(cot, unit_e, inv_e, 14, 14)
        gradient(6, mix, r, 13)
        into_low(r, 6, d_att, flip=True)
        for h in range(H):
            cols = slice(h * head, (h + 1) * head)
            turned = (((0,), (0,)), ((), ()))
            small[...] = lax.dot_general(weights[h], d_att[:, cols], turned, preferred_element_type=f32).astype(b16)

            def attend_back(rows, c):
                d_weight = lax.dot_general(
                    d_att[rows, cols], v[:, cols], (((1,), (1,)), ((), ())), preferred_element_type=f32
                )
                weight = weights[h, rows, :].astype(f32)
                d_scores = weight * (d_weight - jnp.sum(d_weight * weight, axis=1, keepdims=True))
                d_scores = d_scores.astype(b16)
                weights[h, rows, :] = d_scores
                d_query = jnp.dot(d_scores, k[:, cols], preferred_element_type=f32) * scale_self
                d_att[rows, cols] = d_query.astype(b16)
                return c

            each(part, attend_back)
            d_keys = lax.dot_general(weights[h], q[:, cols], turned, preferred_element_type=f32) * scale_self
            k[:, cols] = d_keys.astype(b16)
            v[:, cols] = small[...]
        gradient(5, low_c, v, 12)
        gradient(4, low_c, k)
        gradient(3, low_c, d_att, 11)
        into_t(d_att, 3, flip=True)
        into_t(k, 4, flip=True, add=True)
        into_t(v, 5, flip=True, add=True)
        norm_grad(stream, unit_c, inv_c, 9, 9)
        gradient(2, act_b, r, 8)
        into_t(r, 2, flip=True)
        activate_back(pre_b)
        gradient(1, low_b, r, 7)
        again_two.wait()
        into_t(r, 1, flip=True)
        norm_grad(stream, unit_b, inv_b, 5, 5)
        gradient(0, att, r, 4)
        again_one.wait()
        into_low(r, 0, d_att, flip=True)
        put_sum(3, jnp.dot(jnp.ones((16, total), b16), d_att[...], preferred_element_type=f32)[0:1, :])

        def leave(rows, c):
            stream_out[rows, :] = stream[rows, :]
            return c

        each(chunk, leave)

    whole = pl.BlockSpec(memory_space=pltpu.VMEM)
    low = pltpu.VMEM((total, width), b16)
    high = pltpu.VMEM((total, width), f32)
    narrow = pltpu.VMEM((total, 128), f32)
    return pl.pallas_call(
        kernel,
        name="latent_part",
        in_specs=[pl.BlockSpec(memory_space=pltpu.SMEM), whole, whole, whole, pl.BlockSpec(memory_space=pl.ANY)],
        out_specs=[whole] * 5,
        out_shape=[
            jax.ShapeDtypeStruct((total, width), b16),
            jax.ShapeDtypeStruct((total, width), b16),
            jax.ShapeDtypeStruct((total, width), f32),
            jax.ShapeDtypeStruct((out_rows, width), f32),
            jax.ShapeDtypeStruct((out_rows, width), f32),
        ],
        scratch_shapes=[
            pltpu.VMEM((7, width, width), b16),
            low, low, low, low, low, low, low, low, low, low,
            pltpu.VMEM((H, total, total), b16),
            high, high, high, high, high, narrow, narrow, narrow, high, high, low,
            pltpu.VMEM((total, head), b16),
            pltpu.VMEM((stacked, total), b16),
            pltpu.SemaphoreType.DMA((12,)),
        ],
        compiler_params=pltpu.CompilerParams(vmem_limit_bytes=62 * 1024 * 1024),
    )(numbers, attended, lat, vectors, planes)


def body(pixels, lengths, latents, w_square, w_input, vec_d, vec_c, cotangent):
    n = lax.axis_size("ctx")
    bits_all = n.bit_length() - 1
    rows = latents.shape[1]
    width = latents.shape[2]
    own_w = w_square.shape[1]
    channels = pixels.shape[1]
    slots = pixels.shape[2]
    total_rows = rows * n
    head_size = width // H
    scale = 1.0 / math.sqrt(width)
    scale_self = 1.0 / math.sqrt(head_size)
    core = lax.axis_index("seq")
    place = lax.axis_index("ctx")
    parity = place & 1
    pair = place >> 1
    wide = [4 << i for i in range(bits_all - 2)]

    def swap(x, bit):
        return lax.ppermute(x, "ctx", [(i, i ^ bit) for i in range(n)])

    def swap_core(x):
        return lax.ppermute(x, "seq", [(0, 1), (1, 0)])

    def ordered(mine, other, flag, axis):
        first = jnp.where(flag == 0, mine, other)
        second = jnp.where(flag == 0, other, mine)
        return jnp.concatenate([first, second], axis=axis)

    def quad(x, low, high, axis):
        one, two, three = swap(x, low), swap(x, high), swap(x, low | high)
        bit_low, bit_high = (place // low) & 1, (place // high) & 1
        near = ordered(x, one, bit_low, axis)
        far = ordered(two, three, bit_low, axis)
        return ordered(near, far, bit_high, axis)

    def both(x):
        return ordered(x, swap_core(x), core, 1)

    def gather_wide(x):
        rest = list(wide)
        x = x[None]
        while len(rest) > 1:
            x = quad(x[None], rest[0], rest[1], 0)
            x = x.reshape((-1,) + x.shape[2:])
            rest = rest[2:]
        for bit in rest:
            x = ordered(x[None], swap(x[None], bit), (place // bit) & 1, 0)
            x = x.reshape((-1,) + x.shape[2:])
        return x

    lanes = 384
    packed = jnp.concatenate(
        [
            w_square[0],
            jnp.pad(w_input[0], ((0, 0), (0, lanes - channels))),
            w_input[1],
            vec_d.T,
            jnp.zeros((own_w, lanes - channels - vec_d.shape[0]), b16),
        ],
        axis=1,
    )
    packed = gather_wide(packed[None])[:, 0]
    packed = quad(packed[:, None], 1, 2, 1)
    packed = both(packed.reshape(1, n * own_w, -1))[0]
    square_first = packed[:, :width]
    packed = lax.optimization_barrier(packed[:, width:])
    tall = (channels + 6 + 15) // 16 * 16
    v_key = packed[:, :tall]
    v_val = jnp.where(jnp.arange(tall) < channels, packed[:, lanes : lanes + tall], jnp.zeros((), b16))
    vecf = packed[:, lanes + channels : lanes + channels + vec_d.shape[0]].T.astype(f32)
    lat = ordered(pick(latents, parity), swap(pick(latents, 1 - parity), 1), parity, 0)
    lat = gather_wide(lat[None])
    lat = ordered(lat, swap(lat, 2), (place // 2) & 1, 1).reshape(total_rows, width)
    planes = lax.all_gather(jnp.concatenate([w_square[1:], cotangent], axis=0), ("seq", "ctx"), axis=1, tiled=True)

    latent = lat.astype(f32)
    norm_a, unit_a, inv_a = layer_norm(latent, vecf[0], vecf[1], 1)
    low_a = norm_a.astype(b16)
    query = (matmul("id,de->ie", low_a, square_first) + vecf[2]).astype(b16)
    gate = (matmul("dc,id->ci", v_key, query) * scale).astype(b16)
    gates = ordered(gate[None], swap(gate, 1)[None], parity, 0)

    gain_in = vec_c.astype(f32)
    norm_x, unit_x, inv_x = layer_norm(pixels.astype(f32), gain_in[0][:, None], gain_in[1][:, None], 1)
    low_x = jnp.pad(norm_x.astype(b16), ((0, 0), (0, tall - channels), (0, 0)))
    position = place * slots + jnp.arange(slots, dtype=jnp.int32)
    valid = (position[None, :] < lengths[:, None])[:, None, :]
    scores = matmul("qci,qcj->qij", gates, low_x)
    top = jnp.max(jnp.where(valid, scores, -1e30), axis=2)
    top_hi, top_lo = split_two(top)
    shift = top_hi.astype(f32) + top_lo.astype(f32)
    expo = jnp.where(valid, jnp.exp(scores - shift[..., None]), 0.0)
    total_hi, total_lo = split_two(jnp.sum(expo, axis=2))
    mixed = matmul("qij,qcj->qci", expo.astype(b16), low_x).astype(b16)
    row = jnp.arange(tall)[:, None]

    def write(v, parts):
        for k, part in enumerate(parts):
            v = jnp.where(row == channels + k, part[..., None, :], v)
        return v

    pay = write(mixed, [top_hi, top_lo, total_hi, total_lo])

    def opened(p):
        s = p[channels : channels + 4].astype(f32)
        return p.astype(f32), s[0] + s[1], s[2] + s[3]

    def merge(a, b):
        va, ta, la = opened(a)
        vb, tb, lb = opened(b)
        t = jnp.maximum(ta, tb)
        ea = jnp.exp(ta - t)
        eb = jnp.exp(tb - t)
        return va * ea + vb * eb, t, la * ea + lb * eb

    def closed(v, t, l):
        return write(v.astype(b16), split_two(t) + split_two(l))

    state = merge(pick(pay, parity), swap(pick(pay, 1 - parity), 1))
    for bit in [2] + wide:
        mine = closed(*state)
        state = merge(mine, swap(mine, bit))
    mix_sum, top_all, total_all = state
    mean_x = jnp.where(row < channels, mix_sum / total_all, 0.0)
    mean_low = mean_x.astype(b16)

    attended = (matmul("ci,dc->id", mean_low, v_val) + vecf[3]).astype(b16)
    part_rows = 2 * own_w
    aligned = max(part_rows, 128)
    base = pair * part_rows // aligned * aligned
    inner = pair * part_rows - base
    vectors = jnp.pad(vecf, ((0, 24 - vecf.shape[0]), (0, 0)))
    numbers = jnp.stack([parity, core, base, n * own_w + base, inner]).astype(jnp.int32)
    final, d_attended, d_after_cross, keep, send = latent_part(
        attended, lat, vectors, planes, numbers, part_rows, aligned, scale_self
    )

    def own_rows(array):
        mine = lax.dynamic_slice_in_dim(array, place * rows, rows, 0)
        theirs = lax.dynamic_slice_in_dim(array, (place ^ 1) * rows, rows, 0)
        return ordered(mine[None], swap(theirs, 1)[None], parity, 0)

    latents_out = own_rows(final)

    def share(a):
        return jnp.concatenate([lax.dynamic_slice_in_dim(a, s * n * own_w + base, aligned, 1) for s in range(2)], axis=1)

    def weight_grad(a, r):
        return matmul("ia,ie->ae", share(a), r)

    def window(part, which):
        return lax.dynamic_slice_in_dim(part, which * aligned + inner, part_rows, 0)

    def halves(x, which):
        return lax.dynamic_slice_in_dim(x, which * own_w, own_w, x.ndim - 2)

    def halved(x, which):
        top = halves(x[: 9 * part_rows].reshape(9, part_rows, width), which).reshape(9 * own_w, width)
        return jnp.concatenate([top, x[9 * part_rows :]], axis=0)

    def sums(x):
        return jnp.sum(x.astype(f32), axis=0, keepdims=True)

    pull = matmul("dc,id->ci", v_val, d_attended).astype(b16)
    delta = jnp.sum(pull.astype(f32) * mean_x, axis=0)
    pieces = split_two(top_all) + split_two(total_all) + split_two(delta)
    sent = write(pull, pieces)
    other = swap(sent, 1)
    core_sums = swap_core(after(send, sent))
    sents = ordered(sent[None], other[None], parity, 0)
    pulls = sents
    side = sents[:, channels : channels + 6].astype(f32)
    top_q = side[:, 0] + side[:, 1]
    total_q = side[:, 2] + side[:, 3]
    delta_q = side[:, 4] + side[:, 5]
    scores_again = matmul("qci,qcj->qij", gates, low_x)
    weight = jnp.where(valid, jnp.exp(scores_again - top_q[..., None]), 0.0) / total_q[..., None]
    d_weight = matmul("qci,qcj->qij", pulls, low_x)
    d_scores = (weight * (d_weight - delta_q[..., None])).astype(b16)
    weight_low = weight.astype(b16)
    force = matmul("qij,qcj->qci", d_scores, low_x).astype(b16)
    mine = pick(force, parity)
    other = swap(pick(force, 1 - parity), 1)
    held = after(d_scores, force)
    d_in_norm = (matmul("qci,qij->qcj", gates, held) + matmul("qci,qij->qcj", pulls, weight_low))[:, :channels]
    grad_pixels = norm_back(d_in_norm, unit_x, inv_x, gain_in[0][:, None], 1)
    grad_vc = [jnp.sum(d_in_norm * unit_x, axis=(0, 2)), jnp.sum(d_in_norm, axis=(0, 2))]
    grad_vc = jnp.pad(jnp.stack(grad_vc), ((0, 0), (0, total_rows - channels)))
    other = after(other, grad_vc)
    force_sum = mine.astype(f32) + other.astype(f32)
    chip_sums = None
    for bit in [2] + wide:
        mine = write(force_sum.astype(b16), split_two(grad_vc[0]) + split_two(grad_vc[1]))
        other = swap(mine, bit)
        if chip_sums is None:
            core_sums = after(keep, mine) + core_sums
            chip_sums = swap(halved(core_sums, 1 - parity), 1)
            part_att = matmul("ia,ci->ac", share(d_attended), mean_low)
            other = after(other, part_att)
        force_sum = mine.astype(f32) + other.astype(f32)
        grad_vc = jnp.stack([force_sum[channels] + force_sum[channels + 1], force_sum[channels + 2] + force_sum[channels + 3]])
    force_low = jnp.where(row < channels, force_sum * scale, 0.0).astype(b16)
    d_query = matmul("ci,dc->id", force_low, v_key).astype(b16)
    part0 = weight_grad(low_a, d_query)
    d_norm_a = matmul("ie,de->id", d_query, square_first)
    grad_lat = d_after_cross + norm_back(d_norm_a, unit_a, inv_a, vecf[0], 1)
    grad_latents = own_rows(grad_lat)

    part_q = matmul("ia,ci->ac", share(query), force_low)
    pad_lanes = lanes - tall
    wide_all = width + 2 * lanes

    def gradients(which):
        full = [window(part0, which)]
        for part in (part_q, part_att):
            full.append(jnp.pad(window(part, which), ((0, 0), (0, pad_lanes))))
        return jnp.concatenate(full, axis=1)

    late_vec = jnp.concatenate([sums(d_norm_a * unit_a), sums(d_norm_a), sums(d_query), jnp.pad(grad_vc, ((0, 0), (0, width - total_rows)))], axis=0)
    vectors = jnp.concatenate([late_vec, jnp.zeros((3, width), f32)], axis=0)
    tail = jnp.pad(vectors, ((0, 0), (0, wide_all - width)))
    own = jnp.concatenate([gradients(core), tail], axis=0)
    own = own + swap_core(jnp.concatenate([gradients(1 - core), tail], axis=0))

    def reduced(which):
        return jnp.concatenate([halves(own[:part_rows], which), own[part_rows:]], axis=0)

    own = reduced(parity) + swap(reduced(1 - parity), 1)
    late = own[None, :own_w, :width]
    chip_sums = halved(core_sums, parity) + chip_sums
    grad_input = jnp.stack([own[:own_w, width : width + channels], own[:own_w, width + lanes : width + lanes + channels]])
    tail = own[own_w:, :width]
    grad_vc = tail[3:5, :channels]
    vectors = jnp.concatenate([tail[:3], chip_sums[9 * own_w + 3 :]], axis=0)
    grad_vec = lax.dynamic_slice_in_dim(vectors, core * n * own_w + place * own_w, own_w, 1)[: vec_d.shape[0]]
    grad_square = jnp.concatenate([late, chip_sums[: 9 * own_w].reshape(9, own_w, width)], axis=0)
    return (latents_out, grad_latents, grad_pixels, grad_square, grad_input, grad_vec, grad_vc)


def solution(mesh):
    placed = (
        P("seq", None, "ctx"),
        P("seq"),
        P("seq", "ctx", None),
        P(None, ("seq", "ctx"), None),
        P(None, ("seq", "ctx"), None),
        P(None, ("seq", "ctx")),
        P(),
        P("seq", "ctx", None),
    )
    return jax.shard_map(
        body,
        mesh=mesh,
        in_specs=placed,
        out_specs=(
            P("seq", "ctx", None),
            P("seq", "ctx", None),
            P("seq", None, "ctx"),
            P(None, ("seq", "ctx"), None),
            P(None, ("seq", "ctx"), None),
            P(None, ("seq", "ctx")),
            P(),
        ),
        check_vma=False,
    )
```

time: 411 us -> 412 us (level)
  Pallas kernels: 0 us -> 94.1 us
  matrix products: 103 us -> 25.1 us
  waiting for transfers between devices: 141 us -> 189 us
  local copies, waits for them, and re-layouts: 63 us -> 24.7 us
  other arithmetic: 42.8 us -> 29 us
  starting transfers between devices: 40.2 us -> 31 us
    pallas_call x0 -> x1, Pallas kernels: none -> 94.1 us  [latent_part(): pl.pallas_call(kernel, name='latent_part', in_specs=[pl.BlockSpec(memory_...]
    dot_general x47 -> x15, matrix products: 98.1 us -> 25.1 us  [matmul(): return jnp.einsum(form, left, right, preferred_element_type=f32)]
    ppermute x31 -> x25, waiting for transfers between devices: 141 us -> 186 us  [swap(): return lax.ppermute(x, 'ctx', [(i, i ^ bit) for i in range(n)])]
    reshape x3 -> x1, local copies, waits for them, and re-layouts: 16.6 us -> 2.79 us  [body(): packed = both(packed.reshape(1, n * own_w, -1))[0]]
    unnamed x209 -> x145, local copies, waits for them, and re-layouts: 15.9 us -> 6.79 us
    ppermute x31 -> x25, starting transfers between devices: 40 us -> 30.9 us  [swap(): return lax.ppermute(x, 'ctx', [(i, i ^ bit) for i in range(n)])]
    dynamic_slice x11 -> x3, local copies, waits for them, and re-layouts: 8.7 us -> 3.44 us  [share(): lax.dynamic_slice_in_dim(a, s * n * own_w + base, aligned, 1)]
    sub x1 -> x0, matrix products: 5.13 us -> none  [body(): self_scores - jnp.max(self_scores, axis=2, keepdims=True)]
  transfers between devices with their start and end apart: 37 -> 29, of which waited for: 21 -> 20; matrix products, arithmetic and copies ran while one was open for 32% -> 17% of each run, Pallas kernels for 0% -> 0%
where the time goes in v3:
time: 412 us; the launch traced here: 409 us
  waiting for transfers between devices  189 us (46%)
  Pallas kernels  94.1 us (23%)
  starting transfers between devices  31 us (8%)
  other arithmetic  29 us (7%)
  matrix products  25.1 us (6%)
  local copies, waits for them, and re-layouts  24.7 us (6%)
  between operations  15.9 us (4%)
    ppermute x25, waiting for transfers between devices, swap(): return lax.ppermute(x, 'ctx', [(i, i ^ bit) for i in range(n)])  186 us
    pallas_call x1, Pallas kernels, latent_part(): pl.pallas_call(kernel, name='latent_part', in_specs=[pl.BlockSpec(memory_...  94.1 us
    ppermute x25, starting transfers between devices, swap(): return lax.ppermute(x, 'ctx', [(i, i ^ bit) for i in range(n)])  30.9 us
    dot_general x15, matrix products, matmul(): return jnp.einsum(form, left, right, preferred_element_type=f32)  25.1 us
  transfers between devices with their start and end apart: 29, of which 20 were waited for; matrix products, arithmetic and copies ran while one was open for 17% of the time, Pallas kernels for 0%

profile of v3, /device:TPU:0, one launch (start us, length us, event | category | flops | bytes accessed | tf_op | source)
XLA Modules:
  0.0 409.0 jit_solution(18355639298089040234)
XLA Ops:
  8.5 1.9 pad_maximum_fusion.7
  11.4 5.1 %collective-permute-start.2 = (bf16[1,1,1,32,1792]{4,3,0,2,1:T(8,128)(2,1)S(1)}, bf16[1,1,1,32,1792]{4,3,0,2,1:T(8,128)(2,1)S(1)}, u32[]{:S(2)}, u32[]{:S(2)}) collective-permute-start(bf16[1,1,1,32,1792]{4,3,0,2,1:T(8,128)(2,1)S(1)} %bitcast.136), channel_id=1, source_target_pairs={{0,12},{1,13},{2,14},{3,15},{4,8},{5,9},{6,10},{7,11},{8,4},{9,5},... | collective-permute-start | bytes 344072 | tf_op jit(solution)/shard_map/ppermute | solution.py:343
  17.2 1.7 collective-permute-start.7
  21.6 3.8 collective-permute-start.10
  25.4 2.5 collective-permute-start.8
  27.9 10.5 %collective-permute-done.1 = bf16[1,1,1,32,1792]{4,3,0,2,1:T(8,128)(2,1)S(1)} collective-permute-done((bf16[1,1,1,32,1792]{4,3,0,2,1:T(8,128)(2,1)S(1)}, bf16[1,1,1,32,1792]{4,3,0,2,1:T(8,128)(2,1)S(1)}, u32[]{:S(2)}, u32[]{:S(2)}) %collective-permute-start.1) | collective-permute-done | bytes 114720 | tf_op jit(solution)/shard_map/ppermute | solution.py:343
  38.6 2.5 collective-permute-start.5
  42.5 1.5 collective-permute-start.3
  44.0 8.7 %collective-permute-done.9 = bf16[1,1,1,64,1024]{4,3,2,1,0:T(8,128)(2,1)S(1)} collective-permute-done((bf16[1,1,1,64,1024]{4,3,2,1,0:T(8,128)(2,1)S(1)}, bf16[1,1,1,64,1024]{4,3,2,1,0:T(8,128)(2,1)S(1)}, u32[]{:S(2)}, u32[]{:S(2)}) %collective-permute-start.9) | collective-permute-done | bytes 131104 | tf_op jit(solution)/shard_map/ppermute | solution.py:343
  52.7 4.7 %collective-permute-done.3 = bf16[4,1,32,1792]{3,2,1,0:T(8,128)(2,1)S(1)} collective-permute-done((bf16[4,1,32,1792]{3,2,1,0:T(8,128)(2,1)S(1)}, bf16[4,1,32,1792]{3,2,1,0:T(8,128)(2,1)S(1)}, u32[]{:S(2)}, u32[]{:S(2)}) %collective-permute-start.3) | collective-permute-done | bytes 458784 | tf_op jit(solution)/shard_map/ppermute | solution.py:343
  58.0 2.8 copy.38
  62.1 20.5 %collective-permute-done.11 = bf16[4,1,64,1024]{3,2,0,1:T(8,128)(2,1)S(1)} collective-permute-done((bf16[4,1,64,1024]{3,2,0,1:T(8,128)(2,1)S(1)}, bf16[4,1,64,1024]{3,2,0,1:T(8,128)(2,1)S(1)}, u32[]{:S(2)}, u32[]{:S(2)}) %collective-permute-start.11) | collective-permute-done | bytes 524320 | tf_op jit(solution)/shard_map/ppermute | solution.py:343
  83.7 2.3 broadcast_select_fusion.1
  90.3 1.5 collective-permute-start.12
  92.3 6.7 %collective-permute-done.12 = bf16[272,512]{1,0:T(8,128)(2,1)S(1)} collective-permute-done((bf16[272,512]{1,0:T(8,128)(2,1)S(1)}, bf16[272,512]{1,0:T(8,128)(2,1)S(1)}, u32[]{:S(2)}, u32[]{:S(2)}) %collective-permute-start.12) | collective-permute-done | bytes 278560 | tf_op jit(solution)/shard_map/ppermute | solution.py:343
  99.1 1.4 select_reduce_fusion
  103.8 1.4 collective-permute-start.13
  105.8 13.0 %collective-permute-done.13 = bf16[272,512]{1,0:T(8,128)(2,1)S(1)} collective-permute-done((bf16[272,512]{1,0:T(8,128)(2,1)S(1)}, bf16[272,512]{1,0:T(8,128)(2,1)S(1)}, u32[]{:S(2)}, u32[]{:S(2)}) %collective-permute-start.13) | collective-permute-done | bytes 278560 | tf_op jit(solution)/shard_map/ppermute | solution.py:343
  120.7 13.8 %collective-permute-done.14 = bf16[272,512]{1,0:T(8,128)(2,1)S(1)} collective-permute-done((bf16[272,512]{1,0:T(8,128)(2,1)S(1)}, bf16[272,512]{1,0:T(8,128)(2,1)S(1)}, u32[]{:S(2)}, u32[]{:S(2)}) %collective-permute-start.14) | collective-permute-done | bytes 278560 | tf_op jit(solution)/shard_map/ppermute | solution.py:343
  135.5 1.4 collective-permute-start.15
  137.7 14.8 %collective-permute-done.15 = bf16[272,512]{1,0:T(8,128)(2,1)S(1)} collective-permute-done((bf16[272,512]{1,0:T(8,128)(2,1)S(1)}, bf16[272,512]{1,0:T(8,128)(2,1)S(1)}, u32[]{:S(2)}, u32[]{:S(2)}) %collective-permute-start.15) | collective-permute-done | bytes 278560 | tf_op jit(solution)/shard_map/ppermute | solution.py:343
  153.4 1.7 constant_dynamic-slice_fusion.11
  155.8 27.8 %collective-permute-done.16 = bf16[272,512]{1,0:T(8,128)(2,1)S(1)} collective-permute-done((bf16[272,512]{1,0:T(8,128)(2,1)S(1)}, bf16[272,512]{1,0:T(8,128)(2,1)S(1)}, u32[]{:S(2)}, u32[]{:S(2)}) %collective-permute-start.16) | collective-permute-done | bytes 278560 | tf_op jit(solution)/shard_map/ppermute | solution.py:343
  183.7 3.0 add_convert_fusion.att
  186.7 3.5 all-gather.2.cloned.1.call-done.planes_ref
  190.2 94.1 %latent_part.1 = (bf16[512,1024]{1,0:T(8,128)(2,1)}, bf16[512,1024]{1,0:T(8,128)(2,1)}, f32[512,1024]{1,0:T(8,128)}, f32[600,1024]{1,0:T(8,128)}, f32[600,1024]{1,0:T(8,128)}) custom-call(s32[5]{0:T(128)} %stack.46.num, bf16[512,1024]{1,0:T(8,128)(2,1)} %add_convert_fusion.att, bf16[512,1024]{1,0:T(8,128)(2,1)} %bitcast.130, f32[24,1024]{1,0:T(8,128)} %pad.39.vec, ...), custom_call_target="tpu_custom_call" | custom-call | tf_op jit(solution)/shard_map/latent_part/pallas_call | solution.py:299
  284.3 1.5 constant_dynamic-slice_fusion.18
  285.8 1.5 collective-permute-start.17
  288.4 2.0 multiply_reduce_fusion.4
  294.0 6.3 %collective-permute-done.18 = bf16[272,512]{1,0:T(8,128)(2,1)} collective-permute-done((bf16[272,512]{1,0:T(8,128)(2,1)}, bf16[272,512]{1,0:T(8,128)(2,1)}, u32[]{:S(2)}, u32[]{:S(2)}) %collective-permute-start.18) | collective-permute-done | bytes 278560 | tf_op jit(solution)/shard_map/ppermute | solution.py:343
  300.3 1.3 select_bitcast_fusion.1
  301.8 3.6 fusion.19
  305.5 2.3 multiply_convert_fusion
  310.3 1.4 fusion.11
  311.8 5.7 %collective-permute-done.19 = bf16[272,512]{1,0:T(8,128)(2,1)S(1)} collective-permute-done((bf16[272,512]{1,0:T(8,128)(2,1)S(1)}, bf16[272,512]{1,0:T(8,128)(2,1)S(1)}, u32[]{:S(2)}, u32[]{:S(2)}) %collective-permute-start.19) | collective-permute-done | bytes 278560 | tf_op jit(solution)/shard_map/ppermute | solution.py:343
  320.1 4.5 %collective-permute-done.20 = bf16[272,512]{1,0:T(8,128)(2,1)S(1)} collective-permute-done((bf16[272,512]{1,0:T(8,128)(2,1)S(1)}, bf16[272,512]{1,0:T(8,128)(2,1)S(1)}, u32[]{:S(2)}, u32[]{:S(2)}) %collective-permute-start.20) | collective-permute-done | bytes 278560 | tf_op jit(solution)/shard_map/ppermute | solution.py:343
  325.1 6.5 %collective-permute-done.21 = bf16[272,512]{1,0:T(8,128)(2,1)S(1)} collective-permute-done((bf16[272,512]{1,0:T(8,128)(2,1)S(1)}, bf16[272,512]{1,0:T(8,128)(2,1)S(1)}, u32[]{:S(2)}, u32[]{:S(2)}) %collective-permute-start.21) | collective-permute-done | bytes 278560 | tf_op jit(solution)/shard_map/ppermute | solution.py:343
  332.8 3.0 copy.48
  335.8 7.7 %collective-permute-done.22 = bf16[272,512]{1,0:T(8,128)(2,1)S(1)} collective-permute-done((bf16[272,512]{1,0:T(8,128)(2,1)S(1)}, bf16[272,512]{1,0:T(8,128)(2,1)S(1)}, u32[]{:S(2)}, u32[]{:S(2)}) %collective-permute-start.22) | collective-permute-done | bytes 278560 | tf_op jit(solution)/shard_map/ppermute | solution.py:343
  343.5 1.9 convert_reduce_fusion.2
  345.4 3.6 multiply_reduce_fusion
  349.1 1.4 fusion.85
  351.7 1.3 concatenate.182
  357.7 2.3 multiply_add_fusion
  360.9 1.6 collective-permute-start.25
  364.1 2.4 collective-permute-done.23
  367.2 5.4 %collective-permute-done.25 = f32[40,1792]{1,0:T(8,128)S(1)} collective-permute-done((f32[40,1792]{1,0:T(8,128)S(1)}, f32[40,1792]{1,0:T(8,128)S(1)}, u32[]{:S(2)}, u32[]{:S(2)}) %collective-permute-start.25) | collective-permute-done | bytes 286752 | tf_op jit(solution)/shard_map/ppermute | solution.py:343
  373.9 25.6 %collective-permute-done.27 = f32[312,1024]{1,0:T(8,128)S(1)} collective-permute-done((f32[312,1024]{1,0:T(8,128)S(1)}, f32[312,1024]{1,0:T(8,128)S(1)}, u32[]{:S(2)}, u32[]{:S(2)}) %collective-permute-start.27) | collective-permute-done | bytes 1277984 | tf_op jit(solution)/shard_map/ppermute | solution.py:343
  (320 shorter events, 47.7 us)
Async XLA Ops:
  7.2 10.0 %copy-start.23 = (bf16[2,32,1024]{2,1,0:T(8,128)(2,1)S(1)}, bf16[2,32,1024]{2,1,0:T(8,128)(2,1)}, u32[]{:S(2)}) copy-start(bf16[2,32,1024]{2,1,0:T(8,128)(2,1)} %param.10) | copy-start | bytes 393220
  7.2 11.7 %copy-start.62 = (bf16[2,261]{1,0:T(2,128)(2,1)S(1)}, bf16[2,261]{1,0:T(2,128)(2,1)}, u32[]{:S(2)}) copy-start(bf16[2,261]{1,0:T(2,128)(2,1)} %param.14) | copy-start | bytes 3136
  7.2 12.3 %copy-start = (bf16[2,261,1024]{2,0,1:T(2,128)(2,1)S(1)}, bf16[2,261,1024]{2,0,1:T(2,128)(2,1)}, u32[]{:S(2)}) copy-start(bf16[2,261,1024]{2,0,1:T(2,128)(2,1)} %param.8) | copy-start | bytes 3207172
  7.2 183.0 %all-gather.2.cloned.1.call-start = ((), (), s32[]{:S(2)}) async-start(), calls=%async_computation | async-start | bytes 23789568 | tf_op jit(solution)/shard_map/all_gather | solution.py:398
  11.4 16.5 %collective-permute-start.2 = (bf16[1,1,1,32,1792]{4,3,0,2,1:T(8,128)(2,1)S(1)}, bf16[1,1,1,32,1792]{4,3,0,2,1:T(8,128)(2,1)S(1)}, u32[]{:S(2)}, u32[]{:S(2)}) collective-permute-start(bf16[1,1,1,32,1792]{4,3,0,2,1:T(8,128)(2,1)S(1)} %bitcast.136), channel_id=1, source_target_pairs={{0,12},{1,13},{2,14},{3,15},{4,8},{5,9},{6,10},{7,11},{8,4},{9,5},... | collective-permute-start | bytes 344072 | tf_op jit(solution)/shard_map/ppermute | solution.py:343
  16.6 21.9 %collective-permute-start.1 = (bf16[1,1,1,32,1792]{4,3,0,2,1:T(8,128)(2,1)S(1)}, bf16[1,1,1,32,1792]{4,3,0,2,1:T(8,128)(2,1)S(1)}, u32[]{:S(2)}, u32[]{:S(2)}) collective-permute-start(bf16[1,1,1,32,1792]{4,3,0,2,1:T(8,128)(2,1)S(1)} %bitcast.137), channel_id=1, source_target_pairs={{0,8},{1,9},{2,10},{3,11},{4,12},{5,13},{6,14},{7,15},{8,0},{9,1},... | collective-permute-start | bytes 344072 | tf_op jit(solution)/shard_map/ppermute | solution.py:343
  16.6 8.8 %collective-permute-start = (bf16[1,1,1,32,1792]{4,3,0,2,1:T(8,128)(2,1)S(1)}, bf16[1,1,1,32,1792]{4,3,0,2,1:T(8,128)(2,1)S(1)}, u32[]{:S(2)}, u32[]{:S(2)}) collective-permute-start(bf16[1,1,1,32,1792]{4,3,0,2,1:T(8,128)(2,1)S(1)} %bitcast.138), channel_id=1, source_target_pairs={{0,4},{1,5},{2,6},{3,7},{4,0},{5,1},{6,2},{7,3},{8,12},{9,13},{10,... | collective-permute-start | bytes 344072 | tf_op jit(solution)/shard_map/ppermute | solution.py:343
  17.2 4.3 %collective-permute-start.7 = (bf16[32,1024]{1,0:T(8,128)(2,1)S(1)}, bf16[32,1024]{1,0:T(8,128)(2,1)S(1)}, u32[]{:S(2)}, u32[]{:S(2)}) collective-permute-start(bf16[32,1024]{1,0:T(8,128)(2,1)S(1)} %dynamic-slice_bitcast_fusion.2), channel_id=1, source_target_pairs={{0,1},{1,0},{2,3},{3,2},{4,5},{5,4},{6,7},{7,6},{8,9},{9,8},{10,11... | collective-permute-start | bytes 196616 | tf_op jit(solution)/shard_map/ppermute | solution.py:343
  21.6 22.4 %collective-permute-start.10 = (bf16[1,1,1,64,1024]{4,3,2,1,0:T(8,128)(2,1)S(1)}, bf16[1,1,1,64,1024]{4,3,2,1,0:T(8,128)(2,1)S(1)}, u32[]{:S(2)}, u32[]{:S(2)}) collective-permute-start(bf16[1,1,1,64,1024]{4,3,2,1,0:T(8,128)(2,1)S(1)} %maximum_bitcast_fusion.3), channel_id=1, source_target_pairs={{0,12},{1,13},{2,14},{3,15},{4,8},{5,9},{6,10},{7,11},{8,4},{9,5},... | collective-permute-start | bytes 393224 | tf_op jit(solution)/shard_map/ppermute | solution.py:343
  25.4 27.3 %collective-permute-start.9 = (bf16[1,1,1,64,1024]{4,3,2,1,0:T(8,128)(2,1)S(1)}, bf16[1,1,1,64,1024]{4,3,2,1,0:T(8,128)(2,1)S(1)}, u32[]{:S(2)}, u32[]{:S(2)}) collective-permute-start(bf16[1,1,1,64,1024]{4,3,2,1,0:T(8,128)(2,1)S(1)} %maximum_bitcast_fusion.3), channel_id=1, source_target_pairs={{0,8},{1,9},{2,10},{3,11},{4,12},{5,13},{6,14},{7,15},{8,0},{9,1},... | collective-permute-start | bytes 393224 | tf_op jit(solution)/shard_map/ppermute | solution.py:343
  25.4 17.1 %collective-permute-start.8 = (bf16[1,1,1,64,1024]{4,3,2,1,0:T(8,128)(2,1)S(1)}, bf16[1,1,1,64,1024]{4,3,2,1,0:T(8,128)(2,1)S(1)}, u32[]{:S(2)}, u32[]{:S(2)}) collective-permute-start(bf16[1,1,1,64,1024]{4,3,2,1,0:T(8,128)(2,1)S(1)} %maximum_bitcast_fusion.3), channel_id=1, source_target_pairs={{0,4},{1,5},{2,6},{3,7},{4,0},{5,1},{6,2},{7,3},{8,12},{9,13},{10,... | collective-permute-start | bytes 393224 | tf_op jit(solution)/shard_map/ppermute | solution.py:343
  38.6 18.9 %collective-permute-start.5 = (bf16[4,1,32,1792]{3,2,1,0:T(8,128)(2,1)S(1)}, bf16[4,1,32,1792]{3,2,1,0:T(8,128)(2,1)S(1)}, u32[]{:S(2)}, u32[]{:S(2)}) collective-permute-start(bf16[4,1,32,1792]{3,2,1,0:T(8,128)(2,1)S(1)} %maximum_bitcast_fusion.2), channel_id=1, source_target_pairs={{0,3},{1,2},{2,1},{3,0},{4,7},{5,6},{6,5},{7,4},{8,11},{9,10},{10,... | collective-permute-start | bytes 1376264 | tf_op jit(solution)/shard_map/ppermute | solution.py:343
  41.1 16.4 %collective-permute-start.4 = (bf16[4,1,32,1792]{3,2,1,0:T(8,128)(2,1)S(1)}, bf16[4,1,32,1792]{3,2,1,0:T(8,128)(2,1)S(1)}, u32[]{:S(2)}, u32[]{:S(2)}) collective-permute-start(bf16[4,1,32,1792]{3,2,1,0:T(8,128)(2,1)S(1)} %maximum_bitcast_fusion.2), channel_id=1, source_target_pairs={{0,2},{1,3},{2,0},{3,1},{4,6},{5,7},{6,4},{7,5},{8,10},{9,11},{10,... | collective-permute-start | bytes 1376264 | tf_op jit(solution)/shard_map/ppermute | solution.py:343
  42.5 14.9 %collective-permute-start.3 = (bf16[4,1,32,1792]{3,2,1,0:T(8,128)(2,1)S(1)}, bf16[4,1,32,1792]{3,2,1,0:T(8,128)(2,1)S(1)}, u32[]{:S(2)}, u32[]{:S(2)}) collective-permute-start(bf16[4,1,32,1792]{3,2,1,0:T(8,128)(2,1)S(1)} %maximum_bitcast_fusion.2), channel_id=1, source_target_pairs={{0,1},{1,0},{2,3},{3,2},{4,5},{5,4},{6,7},{7,6},{8,9},{9,8},{10,11... | collective-permute-start | bytes 1376264 | tf_op jit(solution)/shard_map/ppermute | solution.py:343
  60.7 22.9 %collective-permute-start.6 = (bf16[1,512,1792]{1,2,0:T(8,128)(2,1)}, bf16[1,512,1792]{1,2,0:T(8,128)(2,1)}, u32[]{:S(2)}, u32[]{:S(2)}) collective-permute-start(bf16[1,512,1792]{1,2,0:T(8,128)(2,1)} %copy.38), channel_id=1, source_target_pairs={{0,16},{16,0},{1,17},{17,1},{2,18},{18,2},{3,19},{19,3},{4,20},{20... | collective-permute-start | bytes 5505032 | tf_op jit(solution)/shard_map/ppermute | solution.py:346
  60.9 21.7 %collective-permute-start.11 = (bf16[4,1,64,1024]{3,2,0,1:T(8,128)(2,1)S(1)}, bf16[4,1,64,1024]{3,2,0,1:T(8,128)(2,1)S(1)}, u32[]{:S(2)}, u32[]{:S(2)}) collective-permute-start(bf16[4,1,64,1024]{3,2,0,1:T(8,128)(2,1)S(1)} %maximum_bitcast_fusion.1), channel_id=1, source_target_pairs={{0,2},{1,3},{2,0},{3,1},{4,6},{5,7},{6,4},{7,5},{8,10},{9,11},{10,... | collective-permute-start | bytes 1572872 | tf_op jit(solution)/shard_map/ppermute | solution.py:343
  62.0 39.6 %copy-start.37 = (pred[272]{0:T(512)(128)(4,1)}, pred[272]{0:T(512)(128)(4,1)S(1)}, u32[]{:S(2)}) copy-start(pred[272]{0:T(512)(128)(4,1)S(1)} %get-tuple-element.182) | copy-start | bytes 820
  62.0 39.6 %copy-start.41 = (pred[272]{0:T(512)(128)(4,1)}, pred[272]{0:T(512)(128)(4,1)S(1)}, u32[]{:S(2)}) copy-start(pred[272]{0:T(512)(128)(4,1)S(1)} %get-tuple-element.183) | copy-start | bytes 820
  62.0 39.6 %copy-start.49 = (pred[2,1024]{1,0:T(4,128)(4,1)}, pred[2,1024]{1,0:T(4,128)(4,1)S(1)}, u32[]{:S(2)}) copy-start(pred[2,1024]{1,0:T(4,128)(4,1)S(1)} %broadcast_compare_fusion) | copy-start | bytes 6148
  62.1 29.8 %copy-start.21 = (f32[2,1024]{1,0:T(2,128)}, f32[2,1024]{1,0:T(2,128)S(1)}, u32[]{:S(2)}) copy-start(f32[2,1024]{1,0:T(2,128)S(1)} %add_rsqrt_fusion) | copy-start | bytes 24580
  90.3 8.7 %collective-permute-start.12 = (bf16[272,512]{1,0:T(8,128)(2,1)S(1)}, bf16[272,512]{1,0:T(8,128)(2,1)S(1)}, u32[]{:S(2)}, u32[]{:S(2)}) collective-permute-start(bf16[272,512]{1,0:T(8,128)(2,1)S(1)} %fusion.34), channel_id=1, source_target_pairs={{0,1},{1,0},{2,3},{3,2},{4,5},{5,4},{6,7},{7,6},{8,9},{9,8},{10,11... | collective-permute-start | bytes 835592 | tf_op jit(solution)/shard_map/ppermute | solution.py:343
  103.8 48.8 %copy-start.38 = (pred[272]{0:T(512)(128)(4,1)S(1)}, pred[272]{0:T(512)(128)(4,1)}, u32[]{:S(2)}) copy-start(pred[272]{0:T(512)(128)(4,1)} %copy-done.37) | copy-start | bytes 820
  103.8 48.8 %copy-start.42 = (pred[272]{0:T(512)(128)(4,1)S(1)}, pred[272]{0:T(512)(128)(4,1)}, u32[]{:S(2)}) copy-start(pred[272]{0:T(512)(128)(4,1)} %copy-done.41) | copy-start | bytes 820
  103.8 15.0 %collective-permute-start.13 = (bf16[272,512]{1,0:T(8,128)(2,1)S(1)}, bf16[272,512]{1,0:T(8,128)(2,1)S(1)}, u32[]{:S(2)}, u32[]{:S(2)}) collective-permute-start(bf16[272,512]{1,0:T(8,128)(2,1)S(1)} %dynamic-slice_bitcast_fusion.1), channel_id=1, source_target_pairs={{0,1},{1,0},{2,3},{3,2},{4,5},{5,4},{6,7},{7,6},{8,9},{9,8},{10,11... | collective-permute-start | bytes 835592 | tf_op jit(solution)/shard_map/ppermute | solution.py:343
  118.8 64.9 %copy-start.59 = (f32[1,1024]{1,0:T(1,128)S(1)}, f32[1,1024]{1,0:T(1,128)}, u32[]{:S(2)}) copy-start(f32[1,1024]{1,0:T(1,128)} %get-tuple-element.167) | copy-start | bytes 12292
  119.8 14.7 %collective-permute-start.14 = (bf16[272,512]{1,0:T(8,128)(2,1)S(1)}, bf16[272,512]{1,0:T(8,128)(2,1)S(1)}, u32[]{:S(2)}, u32[]{:S(2)}) collective-permute-start(bf16[272,512]{1,0:T(8,128)(2,1)S(1)} %fusion.76), channel_id=1, source_target_pairs={{0,2},{1,3},{2,0},{3,1},{4,6},{5,7},{6,4},{7,5},{8,10},{9,11},{10,... | collective-permute-start | bytes 835592 | tf_op jit(solution)/shard_map/ppermute | solution.py:343
  120.1 66.7 %copy-start.66 = (pred[272]{0:T(512)(128)(4,1)}, pred[272]{0:T(512)(128)(4,1)S(1)}, u32[]{:S(2)}) copy-start(pred[272]{0:T(512)(128)(4,1)S(1)} %iota_compare_fusion.11) | copy-start | bytes 820
  135.5 16.9 %collective-permute-start.15 = (bf16[272,512]{1,0:T(8,128)(2,1)S(1)}, bf16[272,512]{1,0:T(8,128)(2,1)S(1)}, u32[]{:S(2)}, u32[]{:S(2)}) collective-permute-start(bf16[272,512]{1,0:T(8,128)(2,1)S(1)} %fusion.68), channel_id=1, source_target_pairs={{0,4},{1,5},{2,6},{3,7},{4,0},{5,1},{6,2},{7,3},{8,12},{9,13},{10,... | collective-permute-start | bytes 835592 | tf_op jit(solution)/shard_map/ppermute | solution.py:343
  152.9 30.7 %collective-permute-start.16 = (bf16[272,512]{1,0:T(8,128)(2,1)S(1)}, bf16[272,512]{1,0:T(8,128)(2,1)S(1)}, u32[]{:S(2)}, u32[]{:S(2)}) collective-permute-start(bf16[272,512]{1,0:T(8,128)(2,1)S(1)} %fusion.72), channel_id=1, source_target_pairs={{0,8},{1,9},{2,10},{3,11},{4,12},{5,13},{6,14},{7,15},{8,0},{9,1},... | collective-permute-start | bytes 835592 | tf_op jit(solution)/shard_map/ppermute | solution.py:343
  183.6 106.8 %copy-start.55 = (bf16[512]{0:T(512)(128)(2,1)}, bf16[512]{0:T(512)(128)(2,1)S(1)}, u32[]{:S(2)}) copy-start(bf16[512]{0:T(512)(128)(2,1)S(1)} %get-tuple-element.70) | copy-start | bytes 3076
  183.6 106.8 %copy-start.56 = (bf16[512]{0:T(512)(128)(2,1)}, bf16[512]{0:T(512)(128)(2,1)S(1)}, u32[]{:S(2)}) copy-start(bf16[512]{0:T(512)(128)(2,1)S(1)} %get-tuple-element.71) | copy-start | bytes 3076
  183.7 106.7 %copy-start.51 = (bf16[512]{0:T(512)(128)(2,1)}, bf16[512]{0:T(512)(128)(2,1)S(1)}, u32[]{:S(2)}) copy-start(bf16[512]{0:T(512)(128)(2,1)S(1)} %get-tuple-element.72) | copy-start | bytes 3076
  183.7 106.7 %copy-start.52 = (bf16[512]{0:T(512)(128)(2,1)}, bf16[512]{0:T(512)(128)(2,1)S(1)}, u32[]{:S(2)}) copy-start(bf16[512]{0:T(512)(128)(2,1)S(1)} %get-tuple-element.73) | copy-start | bytes 3076
  190.2 98.1 %copy-start.65 = (bf16[272,512]{1,0:T(8,128)(2,1)S(1)}, bf16[272,512]{1,0:T(8,128)(2,1)}, u32[]{:S(2)}) copy-start(bf16[272,512]{1,0:T(8,128)(2,1)} %copy-done.64) | copy-start | bytes 835588
  190.2 98.1 %copy-start.67 = (pred[272]{0:T(512)(128)(4,1)S(1)}, pred[272]{0:T(512)(128)(4,1)}, u32[]{:S(2)}) copy-start(pred[272]{0:T(512)(128)(4,1)} %copy-done.66) | copy-start | bytes 820
  285.8 32.7 %collective-permute-start.17 = (bf16[32,1024]{1,0:T(8,128)(2,1)}, bf16[32,1024]{1,0:T(8,128)(2,1)}, u32[]{:S(2)}, u32[]{:S(2)}) collective-permute-start(bf16[32,1024]{1,0:T(8,128)(2,1)} %constant_dynamic-slice_fusion.18), channel_id=1, source_target_pairs={{0,1},{1,0},{2,3},{3,2},{4,5},{5,4},{6,7},{7,6},{8,9},{9,8},{10,11... | collective-permute-start | bytes 196616 | tf_op jit(solution)/shard_map/ppermute | solution.py:343
  291.5 8.9 %collective-permute-start.18 = (bf16[272,512]{1,0:T(8,128)(2,1)}, bf16[272,512]{1,0:T(8,128)(2,1)}, u32[]{:S(2)}, u32[]{:S(2)}) collective-permute-start(bf16[272,512]{1,0:T(8,128)(2,1)} %select_select_fusion.2), channel_id=1, source_target_pairs={{0,1},{1,0},{2,3},{3,2},{4,5},{5,4},{6,7},{7,6},{8,9},{9,8},{10,11... | collective-permute-start | bytes 835592 | tf_op jit(solution)/shard_map/ppermute | solution.py:343
  294.0 68.4 %collective-permute-start.26 = (f32[600,1024]{1,0:T(8,128)}, f32[600,1024]{1,0:T(8,128)S(1)}, u32[]{:S(2)}, u32[]{:S(2)}) collective-permute-start(f32[600,1024]{1,0:T(8,128)} %get-tuple-element.26), channel_id=1, source_target_pairs={{0,16},{16,0},{1,17},{17,1},{2,18},{18,2},{3,19},{19,3},{4,20},{20... | collective-permute-start | bytes 7372808 | tf_op jit(solution)/shard_map/ppermute | solution.py:346
  309.7 7.8 %collective-permute-start.19 = (bf16[272,512]{1,0:T(8,128)(2,1)S(1)}, bf16[272,512]{1,0:T(8,128)(2,1)S(1)}, u32[]{:S(2)}, u32[]{:S(2)}) collective-permute-start(bf16[272,512]{1,0:T(8,128)(2,1)S(1)} %dynamic-slice_bitcast_fusion), channel_id=1, source_target_pairs={{0,1},{1,0},{2,3},{3,2},{4,5},{5,4},{6,7},{7,6},{8,9},{9,8},{10,11... | collective-permute-start | bytes 835592 | tf_op jit(solution)/shard_map/ppermute | solution.py:343
  317.7 6.9 %collective-permute-start.20 = (bf16[272,512]{1,0:T(8,128)(2,1)S(1)}, bf16[272,512]{1,0:T(8,128)(2,1)S(1)}, u32[]{:S(2)}, u32[]{:S(2)}) collective-permute-start(bf16[272,512]{1,0:T(8,128)(2,1)S(1)} %fusion.80), channel_id=1, source_target_pairs={{0,2},{1,3},{2,0},{3,1},{4,6},{5,7},{6,4},{7,5},{8,10},{9,11},{10,... | collective-permute-start | bytes 835592 | tf_op jit(solution)/shard_map/ppermute | solution.py:343
  325.0 6.6 %collective-permute-start.21 = (bf16[272,512]{1,0:T(8,128)(2,1)S(1)}, bf16[272,512]{1,0:T(8,128)(2,1)S(1)}, u32[]{:S(2)}, u32[]{:S(2)}) collective-permute-start(bf16[272,512]{1,0:T(8,128)(2,1)S(1)} %select_select_fusion.1), channel_id=1, source_target_pairs={{0,4},{1,5},{2,6},{3,7},{4,0},{5,1},{6,2},{7,3},{8,12},{9,13},{10,... | collective-permute-start | bytes 835592 | tf_op jit(solution)/shard_map/ppermute | solution.py:343
  332.0 11.5 %collective-permute-start.22 = (bf16[272,512]{1,0:T(8,128)(2,1)S(1)}, bf16[272,512]{1,0:T(8,128)(2,1)S(1)}, u32[]{:S(2)}, u32[]{:S(2)}) collective-permute-start(bf16[272,512]{1,0:T(8,128)(2,1)S(1)} %select_select_fusion), channel_id=1, source_target_pairs={{0,8},{1,9},{2,10},{3,11},{4,12},{5,13},{6,14},{7,15},{8,0},{9,1},... | collective-permute-start | bytes 835592 | tf_op jit(solution)/shard_map/ppermute | solution.py:343
  332.8 10.7 %copy-start.68 = (pred[272]{0:T(512)(128)(4,1)S(1)}, pred[272]{0:T(512)(128)(4,1)}, u32[]{:S(2)}) copy-start(pred[272]{0:T(512)(128)(4,1)} %copy-done.66) | copy-start | bytes 820
  332.8 12.6 %copy-start.4 = (bf16[1024,1792]{0,1:T(8,128)(2,1)S(1)}, bf16[1024,1792]{0,1:T(8,128)(2,1)}, u32[]{:S(2)}) copy-start(bf16[1024,1792]{0,1:T(8,128)(2,1)} %copy-done.3) | copy-start | bytes 11010052
  356.2 4.4 %collective-permute-start.24 = (f32[72,1792]{1,0:T(8,128)S(1)}, f32[72,1792]{1,0:T(8,128)S(1)}, u32[]{:S(2)}, u32[]{:S(2)}) collective-permute-start(f32[72,1792]{1,0:T(8,128)S(1)} %fusion.55), channel_id=1, source_target_pairs={{0,16},{16,0},{1,17},{17,1},{2,18},{18,2},{3,19},{19,3},{4,20},{20... | collective-permute-start | bytes 1548296 | tf_op jit(solution)/shard_map/ppermute | solution.py:346
  360.1 6.4 %collective-permute-start.23 = (f32[32,1024]{1,0:T(8,128)S(1)}, f32[32,1024]{1,0:T(8,128)S(1)}, u32[]{:S(2)}, u32[]{:S(2)}) collective-permute-start(f32[32,1024]{1,0:T(8,128)S(1)} %constant_dynamic-slice_fusion.15), channel_id=1, source_target_pairs={{0,1},{1,0},{2,3},{3,2},{4,5},{5,4},{6,7},{7,6},{8,9},{9,8},{10,11... | collective-permute-start | bytes 393224 | tf_op jit(solution)/shard_map/ppermute | solution.py:343
  360.9 11.8 %collective-permute-start.25 = (f32[40,1792]{1,0:T(8,128)S(1)}, f32[40,1792]{1,0:T(8,128)S(1)}, u32[]{:S(2)}, u32[]{:S(2)}) collective-permute-start(f32[40,1792]{1,0:T(8,128)S(1)} %pad_maximum_fusion.10), channel_id=1, source_target_pairs={{0,1},{1,0},{2,3},{3,2},{4,5},{5,4},{6,7},{7,6},{8,9},{9,8},{10,11... | collective-permute-start | bytes 860168 | tf_op jit(solution)/shard_map/ppermute | solution.py:343
  363.5 36.1 %collective-permute-start.27 = (f32[312,1024]{1,0:T(8,128)S(1)}, f32[312,1024]{1,0:T(8,128)S(1)}, u32[]{:S(2)}, u32[]{:S(2)}) collective-permute-start(f32[312,1024]{1,0:T(8,128)S(1)} %pad_maximum_fusion.1), channel_id=1, source_target_pairs={{0,1},{1,0},{2,3},{3,2},{4,5},{5,4},{6,7},{7,6},{8,9},{9,8},{10,11... | collective-permute-start | bytes 3833864 | tf_op jit(solution)/shard_map/ppermute | solution.py:343
  (50 other events, 179.5 us)
Sparse Core Ops, SparseCore 0:
  11.0 179.2 all-gather.1

commit v4 on v3

--- a/solution.py
+++ b/solution.py
@@ -49,7 +49,7 @@
     return lax.dynamic_index_in_dim(array, index, 0, keepdims=False)
 
 
-def latent_part(attended, lat, vectors, planes, numbers, part_rows, aligned, scale_self):
+def latent_part(attended, lat, vectors, planes, cotangent, numbers, part_rows, aligned, scale_self):
     total, width = lat.shape
     head = width // H
     extra = vectors.shape[0]
@@ -63,18 +63,16 @@
     root = math.sqrt(2.0 / math.pi)
 
     def kernel(
-        num, att, lat_ref, vec, planes_ref, final, d_att, stream_out, keep, send,
+        num, att, lat_ref, vec, planes_ref, cot_ref, final, d_att, stream_out, keep, send,
         w, cot, low_b, act_b, low_c, q, k, v, mix, low_e, act_e, weights,
         unit_b, unit_c, unit_e, pre_b, pre_e, inv_b, inv_c, inv_e, stream, t, r, small, lhs, sems,
     ):
-        parity, core, inner = num[0], num[1], num[4]
+        core, inner = num[0], num[3]
 
         def load(plane, slot, sem):
             return pltpu.make_async_copy(planes_ref.at[plane], w.at[slot], sems.at[sem])
 
-        cot_copy = pltpu.make_async_copy(
-            planes_ref.at[9 + parity, pl.ds(pl.multiple_of(core * total, total), total), :], cot, sems.at[11]
-        )
+        cot_copy = pltpu.make_async_copy(cot_ref, cot, sems.at[11])
         copies = [load(i, i, i) for i in range(7)]
         for copy in copies:
             copy.start()
@@ -176,7 +174,7 @@
 
         def gradient(index, a_ref, r_ref, place=None):
             for s in range(2):
-                columns = a_ref[:, pl.ds(pl.multiple_of(num[2 + s], 128), aligned)]
+                columns = a_ref[:, pl.ds(pl.multiple_of(num[1 + s], 128), aligned)]
                 lhs[pl.ds(s * aligned, aligned), :] = columns.T
             t[pl.ds(0, stacked), :] = jnp.dot(lhs[...], r_ref[...], preferred_element_type=f32)
             near = pl.multiple_of(core * aligned + inner, 8)
@@ -299,7 +297,7 @@
     return pl.pallas_call(
         kernel,
         name="latent_part",
-        in_specs=[pl.BlockSpec(memory_space=pltpu.SMEM), whole, whole, whole, pl.BlockSpec(memory_space=pl.ANY)],
+        in_specs=[pl.BlockSpec(memory_space=pltpu.SMEM), whole, whole, whole] + [pl.BlockSpec(memory_space=pl.ANY)] * 2,
         out_specs=[whole] * 5,
         out_shape=[
             jax.ShapeDtypeStruct((total, width), b16),
@@ -318,7 +316,7 @@
             pltpu.SemaphoreType.DMA((12,)),
         ],
         compiler_params=pltpu.CompilerParams(vmem_limit_bytes=62 * 1024 * 1024),
-    )(numbers, attended, lat, vectors, planes)
+    )(numbers, attended, lat, vectors, planes, cotangent)
 
 
 def body(pixels, lengths, latents, w_square, w_input, vec_d, vec_c, cotangent):
@@ -371,6 +369,16 @@
             x = ordered(x[None], swap(x[None], bit), (place // bit) & 1, 0)
             x = x.reshape((-1,) + x.shape[2:])
         return x
+
+    def own_steps(array):
+        other = yield swap(pick(array, 1 - parity), 1)
+        x = ordered(pick(array, parity), other, parity, 0)[None]
+        for bit in wide:
+            other = yield swap(x, bit)
+            x = ordered(x, other, (place // bit) & 1, 0)
+        other = yield swap(x, 2)
+        x = ordered(x[:, None], other[:, None], (place // 2) & 1, 1)
+        return x.reshape(total_rows, width)
 
     lanes = 384
     packed = jnp.concatenate(
@@ -395,14 +403,28 @@
     lat = ordered(pick(latents, parity), swap(pick(latents, 1 - parity), 1), parity, 0)
     lat = gather_wide(lat[None])
     lat = ordered(lat, swap(lat, 2), (place // 2) & 1, 1).reshape(total_rows, width)
-    planes = lax.all_gather(jnp.concatenate([w_square[1:], cotangent], axis=0), ("seq", "ctx"), axis=1, tiled=True)
+    planes = lax.all_gather(w_square[1:], ("seq", "ctx"), axis=1, tiled=True)
 
     latent = lat.astype(f32)
     norm_a, unit_a, inv_a = layer_norm(latent, vecf[0], vecf[1], 1)
     low_a = norm_a.astype(b16)
     query = (matmul("id,de->ie", low_a, square_first) + vecf[2]).astype(b16)
     gate = (matmul("dc,id->ci", v_key, query) * scale).astype(b16)
-    gates = ordered(gate[None], swap(gate, 1)[None], parity, 0)
+    steps = own_steps(after(cotangent, gate))
+    hanging = [next(steps)]
+    gathered = []
+
+    def pace(value):
+        if not hanging:
+            return value
+        value, other = lax.optimization_barrier((value, hanging.pop()))
+        try:
+            hanging.append(steps.send(other))
+        except StopIteration as stop:
+            gathered.append(stop.value)
+        return value
+
+    gates = ordered(gate[None], pace(swap(gate, 1))[None], parity, 0)
 
     gain_in = vec_c.astype(f32)
     norm_x, unit_x, inv_x = layer_norm(pixels.astype(f32), gain_in[0][:, None], gain_in[1][:, None], 1)
@@ -440,10 +462,13 @@
     def closed(v, t, l):
         return write(v.astype(b16), split_two(t) + split_two(l))
 
-    state = merge(pick(pay, parity), swap(pick(pay, 1 - parity), 1))
+    state = merge(pick(pay, parity), pace(swap(pick(pay, 1 - parity), 1)))
     for bit in [2] + wide:
         mine = closed(*state)
-        state = merge(mine, swap(mine, bit))
+        state = merge(mine, pace(swap(mine, bit)))
+    while hanging:
+        pace(state[0])
+    cot = gathered[0]
     mix_sum, top_all, total_all = state
     mean_x = jnp.where(row < channels, mix_sum / total_all, 0.0)
     mean_low = mean_x.astype(b16)
@@ -454,9 +479,9 @@
     base = pair * part_rows // aligned * aligned
     inner = pair * part_rows - base
     vectors = jnp.pad(vecf, ((0, 24 - vecf.shape[0]), (0, 0)))
-    numbers = jnp.stack([parity, core, base, n * own_w + base, inner]).astype(jnp.int32)
+    numbers = jnp.stack([core, base, n * own_w + base, inner]).astype(jnp.int32)
     final, d_attended, d_after_cross, keep, send = latent_part(
-        attended, lat, vectors, planes, numbers, part_rows, aligned, scale_self
+        attended, lat, vectors, planes, cot, numbers, part_rows, aligned, scale_self
     )
 
     def own_rows(array):
@@ -518,9 +543,12 @@
         other = swap(mine, bit)
         if chip_sums is None:
             core_sums = after(keep, mine) + core_sums
-            chip_sums = swap(halved(core_sums, 1 - parity), 1)
+            other, core_sums = lax.optimization_barrier((other, core_sums))
+            chip_sums = swap(halved(core_sums, 1 - parity).astype(b16), 1)
             part_att = matmul("ia,ci->ac", share(d_attended), mean_low)
             other = after(other, part_att)
+        elif bit == wide[-1]:
+            other, chip_sums = lax.optimization_barrier((other, chip_sums))
         force_sum = mine.astype(f32) + other.astype(f32)
         grad_vc = jnp.stack([force_sum[channels] + force_sum[channels + 1], force_sum[channels + 2] + force_sum[channels + 3]])
     force_low = jnp.where(row < channels, force_sum * scale, 0.0).astype(b16)
@@ -551,7 +579,7 @@
 
     own = reduced(parity) + swap(reduced(1 - parity), 1)
     late = own[None, :own_w, :width]
-    chip_sums = halved(core_sums, parity) + chip_sums
+    chip_sums = halved(core_sums, parity) + chip_sums.astype(f32)
     grad_input = jnp.stack([own[:own_w, width : width + channels], own[:own_w, width + lanes : width + lanes + channels]])
     tail = own[own_w:, :width]
     grad_vc = tail[3:5, :channels]

time: 412 us -> 373 us (0.905)
  waiting for transfers between devices: 189 us -> 140 us
  local copies, waits for them, and re-layouts: 24.7 us -> 30.5 us
  starting transfers between devices: 31 us -> 36.2 us
    ppermute x25 -> x29, waiting for transfers between devices: 186 us -> 140 us  [swap(): return lax.ppermute(x, 'ctx', [(i, i ^ bit) for i in range(n)])]
    ppermute x25 -> x29, starting transfers between devices: 30.9 us -> 36.1 us  [swap(): return lax.ppermute(x, 'ctx', [(i, i ^ bit) for i in range(n)])]
    unnamed x145 -> x123, local copies, waits for them, and re-layouts: 6.79 us -> 9.51 us
  transfers between devices with their start and end apart: 29 -> 33, of which waited for: 20 -> 21; matrix products, arithmetic and copies ran while one was open for 17% -> 16% of each run, Pallas kernels for 0% -> 0%
where the time goes in v4:
time: 373 us; the launch traced here: 370 us
  waiting for transfers between devices  140 us (38%)
  Pallas kernels  93 us (25%)
  starting transfers between devices  36.2 us (10%)
  local copies, waits for them, and re-layouts  30.5 us (8%)
  other arithmetic  30.1 us (8%)
  matrix products  23.7 us (6%)
  between operations  15.7 us (4%)
    ppermute x29, waiting for transfers between devices, swap(): return lax.ppermute(x, 'ctx', [(i, i ^ bit) for i in range(n)])  140 us
    pallas_call x1, Pallas kernels, latent_part(): pl.pallas_call(kernel, name='latent_part', in_specs=[pl.BlockSpec(memory_...  93 us
    ppermute x29, starting transfers between devices, swap(): return lax.ppermute(x, 'ctx', [(i, i ^ bit) for i in range(n)])  36.1 us
    dot_general x15, matrix products, matmul(): return jnp.einsum(form, left, right, preferred_element_type=f32)  23.7 us
    unnamed x123, local copies, waits for them, and re-layouts  9.51 us
  transfers between devices with their start and end apart: 33, of which 21 were waited for; matrix products, arithmetic and copies ran while one was open for 16% of the time, Pallas kernels for 0%

profile of v4, /device:TPU:0, one launch (start us, length us, event | category | flops | bytes accessed | tf_op | source)
XLA Modules:
  0.0 369.6 jit_solution(5620046054674972291)
XLA Ops:
  7.3 2.0 slice.335
  11.8 5.1 %collective-permute-start.2 = (bf16[1,1,1,32,1792]{4,3,0,2,1:T(8,128)(2,1)S(1)}, bf16[1,1,1,32,1792]{4,3,0,2,1:T(8,128)(2,1)S(1)}, u32[]{:S(2)}, u32[]{:S(2)}) collective-permute-start(bf16[1,1,1,32,1792]{4,3,0,2,1:T(8,128)(2,1)S(1)} %bitcast.153), channel_id=1, source_target_pairs={{0,12},{1,13},{2,14},{3,15},{4,8},{5,9},{6,10},{7,11},{8,4},{9,5},... | collective-permute-start | bytes 344072 | tf_op jit(solution)/shard_map/ppermute | solution.py:341
  17.6 1.7 collective-permute-start.7
  20.5 1.4 collective-permute-done.7
  21.9 3.8 %collective-permute-start.10 = (bf16[1,1,1,64,1024]{4,3,2,1,0:T(8,128)(2,1)S(1)}, bf16[1,1,1,64,1024]{4,3,2,1,0:T(8,128)(2,1)S(1)}, u32[]{:S(2)}, u32[]{:S(2)}) collective-permute-start(bf16[1,1,1,64,1024]{4,3,2,1,0:T(8,128)(2,1)S(1)} %maximum_bitcast_fusion.3), channel_id=1, source_target_pairs={{0,12},{1,13},{2,14},{3,15},{4,8},{5,9},{6,10},{7,11},{8,4},{9,5},... | collective-permute-start | bytes 393224 | tf_op jit(solution)/shard_map/ppermute | solution.py:341
  25.8 1.3 collective-permute-done
  27.1 2.5 collective-permute-start.8
  29.6 9.1 %collective-permute-done.1 = bf16[1,1,1,32,1792]{4,3,0,2,1:T(8,128)(2,1)S(1)} collective-permute-done((bf16[1,1,1,32,1792]{4,3,0,2,1:T(8,128)(2,1)S(1)}, bf16[1,1,1,32,1792]{4,3,0,2,1:T(8,128)(2,1)S(1)}, u32[]{:S(2)}, u32[]{:S(2)}) %collective-permute-start.1) | collective-permute-done | bytes 114720 | tf_op jit(solution)/shard_map/ppermute | solution.py:341
  38.9 2.5 collective-permute-start.5
  43.0 1.4 collective-permute-start.3
  44.4 5.9 %collective-permute-done.9 = bf16[1,1,1,64,1024]{4,3,2,1,0:T(8,128)(2,1)S(1)} collective-permute-done((bf16[1,1,1,64,1024]{4,3,2,1,0:T(8,128)(2,1)S(1)}, bf16[1,1,1,64,1024]{4,3,2,1,0:T(8,128)(2,1)S(1)}, u32[]{:S(2)}, u32[]{:S(2)}) %collective-permute-start.9) | collective-permute-done | bytes 131104 | tf_op jit(solution)/shard_map/ppermute | solution.py:341
  50.3 9.9 %collective-permute-done.3 = bf16[4,1,32,1792]{3,2,1,0:T(8,128)(2,1)S(1)} collective-permute-done((bf16[4,1,32,1792]{3,2,1,0:T(8,128)(2,1)S(1)}, bf16[4,1,32,1792]{3,2,1,0:T(8,128)(2,1)S(1)}, u32[]{:S(2)}, u32[]{:S(2)}) %collective-permute-start.3) | collective-permute-done | bytes 458784 | tf_op jit(solution)/shard_map/ppermute | solution.py:341
  60.5 1.4 pad_maximum_fusion
  61.9 4.3 %copy.40 = bf16[1,512,1792]{1,2,0:T(8,128)(2,1)} copy(bf16[1,512,1792]{2,1,0:T(8,128)(2,1)} %bitcast.146) | data formatting | bytes 3670016 | tf_op jit(solution)/shard_map/reshape | solution.py:396
  66.4 1.4 fusion.9
  67.8 12.8 %collective-permute-done.11 = bf16[4,1,64,1024]{3,2,0,1:T(8,128)(2,1)S(1)} collective-permute-done((bf16[4,1,64,1024]{3,2,0,1:T(8,128)(2,1)S(1)}, bf16[4,1,64,1024]{3,2,0,1:T(8,128)(2,1)S(1)}, u32[]{:S(2)}, u32[]{:S(2)}) %collective-permute-start.11) | collective-permute-done | bytes 524320 | tf_op jit(solution)/shard_map/ppermute | solution.py:341
  81.9 1.5 fusion.16
  83.5 2.3 broadcast_select_fusion.1
  90.6 2.5 collective-permute-start.12
  93.8 15.3 %collective-permute-done.13 = bf16[32,1024]{1,0:T(8,128)(2,1)S(1)} collective-permute-done((bf16[32,1024]{1,0:T(8,128)(2,1)S(1)}, bf16[32,1024]{1,0:T(8,128)(2,1)S(1)}, u32[]{:S(2)}, u32[]{:S(2)}) %collective-permute-start.13) | collective-permute-done | bytes 65568 | tf_op jit(solution)/shard_map/ppermute | solution.py:341
  109.1 1.4 select_reduce_fusion
  114.5 1.9 collective-permute-start.14
  117.9 4.2 %collective-permute-done.15 = bf16[1,64,1024]{2,1,0:T(8,128)(2,1)S(1)} collective-permute-done((bf16[1,64,1024]{2,1,0:T(8,128)(2,1)S(1)}, bf16[1,64,1024]{2,1,0:T(8,128)(2,1)S(1)}, u32[]{:S(2)}, u32[]{:S(2)}) %collective-permute-start.15) | collective-permute-done | bytes 131104 | tf_op jit(solution)/shard_map/ppermute | solution.py:341
  122.1 7.4 %collective-permute-done.14 = bf16[272,512]{1,0:T(8,128)(2,1)S(1)} collective-permute-done((bf16[272,512]{1,0:T(8,128)(2,1)S(1)}, bf16[272,512]{1,0:T(8,128)(2,1)S(1)}, u32[]{:S(2)}, u32[]{:S(2)}) %collective-permute-start.14) | collective-permute-done | bytes 278560 | tf_op jit(solution)/shard_map/ppermute | solution.py:341
  132.4 17.6 %collective-permute-done.17 = bf16[2,64,1024]{2,1,0:T(8,128)(2,1)S(1)} collective-permute-done((bf16[2,64,1024]{2,1,0:T(8,128)(2,1)S(1)}, bf16[2,64,1024]{2,1,0:T(8,128)(2,1)S(1)}, u32[]{:S(2)}, u32[]{:S(2)}) %collective-permute-start.17) | collective-permute-done | bytes 262176 | tf_op jit(solution)/shard_map/ppermute | solution.py:341
  150.1 4.4 %collective-permute-start.19 = (bf16[4,64,1024]{2,1,0:T(8,128)(2,1)S(1)}, bf16[4,64,1024]{2,1,0:T(8,128)(2,1)S(1)}, u32[]{:S(2)}, u32[]{:S(2)}) collective-permute-start(bf16[4,64,1024]{2,1,0:T(8,128)(2,1)S(1)} %pad_maximum_fusion.9), channel_id=1, source_target_pairs={{0,2},{1,3},{2,0},{3,1},{4,6},{5,7},{6,4},{7,5},{8,10},{9,11},{10,... | collective-permute-start | bytes 1572872 | tf_op jit(solution)/shard_map/ppermute | solution.py:341
  155.0 1.7 constant_dynamic-slice_fusion.10
  157.3 8.7 %collective-permute-done.18 = bf16[272,512]{1,0:T(8,128)(2,1)S(1)} collective-permute-done((bf16[272,512]{1,0:T(8,128)(2,1)S(1)}, bf16[272,512]{1,0:T(8,128)(2,1)S(1)}, u32[]{:S(2)}, u32[]{:S(2)}) %collective-permute-start.18) | collective-permute-done | bytes 278560 | tf_op jit(solution)/shard_map/ppermute | solution.py:341
  168.5 12.3 %collective-permute-done.20 = bf16[272,512]{1,0:T(8,128)(2,1)S(1)} collective-permute-done((bf16[272,512]{1,0:T(8,128)(2,1)S(1)}, bf16[272,512]{1,0:T(8,128)(2,1)S(1)}, u32[]{:S(2)}, u32[]{:S(2)}) %collective-permute-start.20) | collective-permute-done | bytes 278560 | tf_op jit(solution)/shard_map/ppermute | solution.py:341
  181.6 2.9 add_convert_fusion.att
  184.5 93.0 %latent_part.1 = (bf16[512,1024]{1,0:T(8,128)(2,1)}, bf16[512,1024]{1,0:T(8,128)(2,1)}, f32[512,1024]{1,0:T(8,128)}, f32[600,1024]{1,0:T(8,128)}, f32[600,1024]{1,0:T(8,128)}) custom-call(s32[4]{0:T(128)} %pad_add_fusion.num, bf16[512,1024]{1,0:T(8,128)(2,1)} %add_convert_fusion.att, bf16[512,1024]{1,0:T(8,128)(2,1)} %bitcast.145, f32[24,1024]{1,0:T(8,128)} %pad.39.vec, ...), custom_call_target="tpu_custom_call" | custom-call | tf_op jit(solution)/shard_map/latent_part/pallas_call | solution.py:297
  277.5 1.5 constant_dynamic-slice_fusion.17
  279.0 1.4 collective-permute-start.21
  281.4 2.1 multiply_reduce_fusion.4
  287.0 5.4 %collective-permute-done.22 = bf16[272,512]{1,0:T(8,128)(2,1)S(1)} collective-permute-done((bf16[272,512]{1,0:T(8,128)(2,1)S(1)}, bf16[272,512]{1,0:T(8,128)(2,1)S(1)}, u32[]{:S(2)}, u32[]{:S(2)}) %collective-permute-start.22) | collective-permute-done | bytes 278560 | tf_op jit(solution)/shard_map/ppermute | solution.py:341
  293.5 4.2 %multiply_convert_fusion = bf16[2,512,1024]{2,1,0:T(8,128)(2,1)S(1)} fusion(f32[2,512]{1,0:T(2,128)S(1)} %bitcast.174, f32[2,512]{1,0:T(2,128)S(1)} %bitcast.172, f32[2,512,1024]{2,1,0:T(8,128)} %copy-done.8, f32[2,512]{1,0:T(2,128)S(1)} %bitcast.170, pred[2,1024]{1,0:T(4,128)(4,1)S(1)} %copy-done.42, bf16[2,261,1024]{2,1,0:T(8,128)(2,1)} %fusion.9, ...), kind=kOutput, calls=%fused_computation | convolution fusion | flops 576995328 | bytes 7931904 | tf_op jit(solution)/shard_map/qci,qcj->qij/dot_general | solution.py:17
  303.4 2.7 collective-permute-done.23
  306.3 1.6 collective-permute-start.24
  309.4 3.6 collective-permute-done.24
  314.6 5.4 %collective-permute-done.26 = bf16[272,512]{1,0:T(8,128)(2,1)S(1)} collective-permute-done((bf16[272,512]{1,0:T(8,128)(2,1)S(1)}, bf16[272,512]{1,0:T(8,128)(2,1)S(1)}, u32[]{:S(2)}, u32[]{:S(2)}) %collective-permute-start.26) | collective-permute-done | bytes 278560 | tf_op jit(solution)/shard_map/ppermute | solution.py:341
  321.9 3.0 copy.51
  325.0 6.6 %collective-permute-done.27 = bf16[272,512]{1,0:T(8,128)(2,1)S(1)} collective-permute-done((bf16[272,512]{1,0:T(8,128)(2,1)S(1)}, bf16[272,512]{1,0:T(8,128)(2,1)S(1)}, u32[]{:S(2)}, u32[]{:S(2)}) %collective-permute-start.27) | collective-permute-done | bytes 278560 | tf_op jit(solution)/shard_map/ppermute | solution.py:341
  332.5 2.6 convert_reduce_fusion.2
  335.3 3.6 multiply_reduce_fusion
  345.0 2.3 multiply_add_fusion
  348.2 1.5 collective-permute-start.31
  349.7 4.1 %collective-permute-done.29 = f32[32,1024]{1,0:T(8,128)S(1)} collective-permute-done((f32[32,1024]{1,0:T(8,128)S(1)}, f32[32,1024]{1,0:T(8,128)S(1)}, u32[]{:S(2)}, u32[]{:S(2)}) %collective-permute-start.29) | collective-permute-done | bytes 131104 | tf_op jit(solution)/shard_map/ppermute | solution.py:341
  354.5 4.9 %collective-permute-done.31 = f32[40,1792]{1,0:T(8,128)S(1)} collective-permute-done((f32[40,1792]{1,0:T(8,128)S(1)}, f32[40,1792]{1,0:T(8,128)S(1)}, u32[]{:S(2)}, u32[]{:S(2)}) %collective-permute-start.31) | collective-permute-done | bytes 286752 | tf_op jit(solution)/shard_map/ppermute | solution.py:341
  (320 shorter events, 53.7 us)
Async XLA Ops:
  7.2 12.2 %copy-start = (bf16[2,261,1024]{2,0,1:T(2,128)(2,1)S(1)}, bf16[2,261,1024]{2,0,1:T(2,128)(2,1)}, u32[]{:S(2)}) copy-start(bf16[2,261,1024]{2,0,1:T(2,128)(2,1)} %param.8) | copy-start | bytes 3207172
  7.2 12.7 %copy-start.53 = (s32[2]{0:T(128)S(1)}, s32[2]{0:T(128)}, u32[]{:S(2)}) copy-start(s32[2]{0:T(128)} %param.9) | copy-start | bytes 28
  7.2 177.3 %all-gather.2.cloned.1.call-start = ((), (), s32[]{:S(2)}) async-start(), calls=%async_computation | async-start | bytes 19464192 | tf_op jit(solution)/shard_map/all_gather | solution.py:406
  11.8 17.8 %collective-permute-start.2 = (bf16[1,1,1,32,1792]{4,3,0,2,1:T(8,128)(2,1)S(1)}, bf16[1,1,1,32,1792]{4,3,0,2,1:T(8,128)(2,1)S(1)}, u32[]{:S(2)}, u32[]{:S(2)}) collective-permute-start(bf16[1,1,1,32,1792]{4,3,0,2,1:T(8,128)(2,1)S(1)} %bitcast.153), channel_id=1, source_target_pairs={{0,12},{1,13},{2,14},{3,15},{4,8},{5,9},{6,10},{7,11},{8,4},{9,5},... | collective-permute-start | bytes 344072 | tf_op jit(solution)/shard_map/ppermute | solution.py:341
  16.9 21.8 %collective-permute-start.1 = (bf16[1,1,1,32,1792]{4,3,0,2,1:T(8,128)(2,1)S(1)}, bf16[1,1,1,32,1792]{4,3,0,2,1:T(8,128)(2,1)S(1)}, u32[]{:S(2)}, u32[]{:S(2)}) collective-permute-start(bf16[1,1,1,32,1792]{4,3,0,2,1:T(8,128)(2,1)S(1)} %bitcast.154), channel_id=1, source_target_pairs={{0,8},{1,9},{2,10},{3,11},{4,12},{5,13},{6,14},{7,15},{8,0},{9,1},... | collective-permute-start | bytes 344072 | tf_op jit(solution)/shard_map/ppermute | solution.py:341
  16.9 10.2 %collective-permute-start = (bf16[1,1,1,32,1792]{4,3,0,2,1:T(8,128)(2,1)S(1)}, bf16[1,1,1,32,1792]{4,3,0,2,1:T(8,128)(2,1)S(1)}, u32[]{:S(2)}, u32[]{:S(2)}) collective-permute-start(bf16[1,1,1,32,1792]{4,3,0,2,1:T(8,128)(2,1)S(1)} %bitcast.155), channel_id=1, source_target_pairs={{0,4},{1,5},{2,6},{3,7},{4,0},{5,1},{6,2},{7,3},{8,12},{9,13},{10,... | collective-permute-start | bytes 344072 | tf_op jit(solution)/shard_map/ppermute | solution.py:341
  17.6 4.3 %collective-permute-start.7 = (bf16[32,1024]{1,0:T(8,128)(2,1)S(1)}, bf16[32,1024]{1,0:T(8,128)(2,1)S(1)}, u32[]{:S(2)}, u32[]{:S(2)}) collective-permute-start(bf16[32,1024]{1,0:T(8,128)(2,1)S(1)} %dynamic-slice_bitcast_fusion.3), channel_id=1, source_target_pairs={{0,1},{1,0},{2,3},{3,2},{4,5},{5,4},{6,7},{7,6},{8,9},{9,8},{10,11... | collective-permute-start | bytes 196616 | tf_op jit(solution)/shard_map/ppermute | solution.py:341
  19.3 264.3 %copy-start.27 = (pred[272]{0:T(512)(128)(4,1)}, pred[272]{0:T(512)(128)(4,1)S(1)}, u32[]{:S(2)}) copy-start(pred[272]{0:T(512)(128)(4,1)S(1)} %get-tuple-element.215) | copy-start | bytes 820
  20.0 91.6 %copy-start.41 = (pred[2,1024]{1,0:T(4,128)(4,1)}, pred[2,1024]{1,0:T(4,128)(4,1)S(1)}, u32[]{:S(2)}) copy-start(pred[2,1024]{1,0:T(4,128)(4,1)S(1)} %broadcast_compare_fusion) | copy-start | bytes 6148
  21.9 22.5 %collective-permute-start.10 = (bf16[1,1,1,64,1024]{4,3,2,1,0:T(8,128)(2,1)S(1)}, bf16[1,1,1,64,1024]{4,3,2,1,0:T(8,128)(2,1)S(1)}, u32[]{:S(2)}, u32[]{:S(2)}) collective-permute-start(bf16[1,1,1,64,1024]{4,3,2,1,0:T(8,128)(2,1)S(1)} %maximum_bitcast_fusion.3), channel_id=1, source_target_pairs={{0,12},{1,13},{2,14},{3,15},{4,8},{5,9},{6,10},{7,11},{8,4},{9,5},... | collective-permute-start | bytes 393224 | tf_op jit(solution)/shard_map/ppermute | solution.py:341
  25.8 24.5 %collective-permute-start.9 = (bf16[1,1,1,64,1024]{4,3,2,1,0:T(8,128)(2,1)S(1)}, bf16[1,1,1,64,1024]{4,3,2,1,0:T(8,128)(2,1)S(1)}, u32[]{:S(2)}, u32[]{:S(2)}) collective-permute-start(bf16[1,1,1,64,1024]{4,3,2,1,0:T(8,128)(2,1)S(1)} %maximum_bitcast_fusion.3), channel_id=1, source_target_pairs={{0,8},{1,9},{2,10},{3,11},{4,12},{5,13},{6,14},{7,15},{8,0},{9,1},... | collective-permute-start | bytes 393224 | tf_op jit(solution)/shard_map/ppermute | solution.py:341
  27.1 15.9 %collective-permute-start.8 = (bf16[1,1,1,64,1024]{4,3,2,1,0:T(8,128)(2,1)S(1)}, bf16[1,1,1,64,1024]{4,3,2,1,0:T(8,128)(2,1)S(1)}, u32[]{:S(2)}, u32[]{:S(2)}) collective-permute-start(bf16[1,1,1,64,1024]{4,3,2,1,0:T(8,128)(2,1)S(1)} %maximum_bitcast_fusion.3), channel_id=1, source_target_pairs={{0,4},{1,5},{2,6},{3,7},{4,0},{5,1},{6,2},{7,3},{8,12},{9,13},{10,... | collective-permute-start | bytes 393224 | tf_op jit(solution)/shard_map/ppermute | solution.py:341
  38.9 21.4 %collective-permute-start.5 = (bf16[4,1,32,1792]{3,2,1,0:T(8,128)(2,1)S(1)}, bf16[4,1,32,1792]{3,2,1,0:T(8,128)(2,1)S(1)}, u32[]{:S(2)}, u32[]{:S(2)}) collective-permute-start(bf16[4,1,32,1792]{3,2,1,0:T(8,128)(2,1)S(1)} %maximum_bitcast_fusion.2), channel_id=1, source_target_pairs={{0,3},{1,2},{2,1},{3,0},{4,7},{5,6},{6,5},{7,4},{8,11},{9,10},{10,... | collective-permute-start | bytes 1376264 | tf_op jit(solution)/shard_map/ppermute | solution.py:341
  41.4 18.8 %collective-permute-start.4 = (bf16[4,1,32,1792]{3,2,1,0:T(8,128)(2,1)S(1)}, bf16[4,1,32,1792]{3,2,1,0:T(8,128)(2,1)S(1)}, u32[]{:S(2)}, u32[]{:S(2)}) collective-permute-start(bf16[4,1,32,1792]{3,2,1,0:T(8,128)(2,1)S(1)} %maximum_bitcast_fusion.2), channel_id=1, source_target_pairs={{0,2},{1,3},{2,0},{3,1},{4,6},{5,7},{6,4},{7,5},{8,10},{9,11},{10,... | collective-permute-start | bytes 1376264 | tf_op jit(solution)/shard_map/ppermute | solution.py:341
  43.0 17.2 %collective-permute-start.3 = (bf16[4,1,32,1792]{3,2,1,0:T(8,128)(2,1)S(1)}, bf16[4,1,32,1792]{3,2,1,0:T(8,128)(2,1)S(1)}, u32[]{:S(2)}, u32[]{:S(2)}) collective-permute-start(bf16[4,1,32,1792]{3,2,1,0:T(8,128)(2,1)S(1)} %maximum_bitcast_fusion.2), channel_id=1, source_target_pairs={{0,1},{1,0},{2,3},{3,2},{4,5},{5,4},{6,7},{7,6},{8,9},{9,8},{10,11... | collective-permute-start | bytes 1376264 | tf_op jit(solution)/shard_map/ppermute | solution.py:341
  66.2 17.3 %collective-permute-start.6 = (bf16[1,512,1792]{1,2,0:T(8,128)(2,1)}, bf16[1,512,1792]{1,2,0:T(8,128)(2,1)}, u32[]{:S(2)}, u32[]{:S(2)}) collective-permute-start(bf16[1,512,1792]{1,2,0:T(8,128)(2,1)} %copy.40), channel_id=1, source_target_pairs={{0,16},{16,0},{1,17},{17,1},{2,18},{18,2},{3,19},{19,3},{4,20},{20... | collective-permute-start | bytes 5505032 | tf_op jit(solution)/shard_map/ppermute | solution.py:344
  66.3 14.4 %collective-permute-start.11 = (bf16[4,1,64,1024]{3,2,0,1:T(8,128)(2,1)S(1)}, bf16[4,1,64,1024]{3,2,0,1:T(8,128)(2,1)S(1)}, u32[]{:S(2)}, u32[]{:S(2)}) collective-permute-start(bf16[4,1,64,1024]{3,2,0,1:T(8,128)(2,1)S(1)} %maximum_bitcast_fusion.1), channel_id=1, source_target_pairs={{0,2},{1,3},{2,0},{3,1},{4,6},{5,7},{6,4},{7,5},{8,10},{9,11},{10,... | collective-permute-start | bytes 1572872 | tf_op jit(solution)/shard_map/ppermute | solution.py:341
  66.4 217.3 %copy-start.30 = (pred[272]{0:T(512)(128)(4,1)}, pred[272]{0:T(512)(128)(4,1)S(1)}, u32[]{:S(2)}) copy-start(pred[272]{0:T(512)(128)(4,1)S(1)} %iota_compare_fusion.10) | copy-start | bytes 820
  89.6 19.5 %copy-start.14 = (bf16[2,261,1024]{2,1,0:T(8,128)(2,1)S(1)}, bf16[2,261,1024]{2,1,0:T(8,128)(2,1)}, u32[]{:S(2)}) copy-start(bf16[2,261,1024]{2,1,0:T(8,128)(2,1)} %fusion.9) | copy-start | bytes 3207172
  90.6 18.5 %collective-permute-start.12 = (bf16[272,512]{1,0:T(8,128)(2,1)S(1)}, bf16[272,512]{1,0:T(8,128)(2,1)S(1)}, u32[]{:S(2)}, u32[]{:S(2)}) collective-permute-start(bf16[272,512]{1,0:T(8,128)(2,1)S(1)} %fusion.33), channel_id=1, source_target_pairs={{0,1},{1,0},{2,3},{3,2},{4,5},{5,4},{6,7},{7,6},{8,9},{9,8},{10,11... | collective-permute-start | bytes 835592 | tf_op jit(solution)/shard_map/ppermute | solution.py:341
  93.1 190.6 %copy-start.33 = (pred[272]{0:T(512)(128)(4,1)}, pred[272]{0:T(512)(128)(4,1)S(1)}, u32[]{:S(2)}) copy-start(pred[272]{0:T(512)(128)(4,1)S(1)} %iota_compare_fusion.9) | copy-start | bytes 820
  93.1 16.0 %collective-permute-start.13 = (bf16[32,1024]{1,0:T(8,128)(2,1)S(1)}, bf16[32,1024]{1,0:T(8,128)(2,1)S(1)}, u32[]{:S(2)}, u32[]{:S(2)}) collective-permute-start(bf16[32,1024]{1,0:T(8,128)(2,1)S(1)} %dynamic-slice_bitcast_fusion.2), channel_id=1, source_target_pairs={{0,1},{1,0},{2,3},{3,2},{4,5},{5,4},{6,7},{7,6},{8,9},{9,8},{10,11... | collective-permute-start | bytes 196616 | tf_op jit(solution)/shard_map/ppermute | solution.py:341
  114.5 15.0 %collective-permute-start.14 = (bf16[272,512]{1,0:T(8,128)(2,1)S(1)}, bf16[272,512]{1,0:T(8,128)(2,1)S(1)}, u32[]{:S(2)}, u32[]{:S(2)}) collective-permute-start(bf16[272,512]{1,0:T(8,128)(2,1)S(1)} %dynamic-slice_bitcast_fusion.1), channel_id=1, source_target_pairs={{0,1},{1,0},{2,3},{3,2},{4,5},{5,4},{6,7},{7,6},{8,9},{9,8},{10,11... | collective-permute-start | bytes 835592 | tf_op jit(solution)/shard_map/ppermute | solution.py:341
  116.4 5.7 %collective-permute-start.15 = (bf16[1,64,1024]{2,1,0:T(8,128)(2,1)S(1)}, bf16[1,64,1024]{2,1,0:T(8,128)(2,1)S(1)}, u32[]{:S(2)}, u32[]{:S(2)}) collective-permute-start(bf16[1,64,1024]{2,1,0:T(8,128)(2,1)S(1)} %maximum_bitcast_fusion.4), channel_id=1, source_target_pairs={{0,4},{1,5},{2,6},{3,7},{4,0},{5,1},{6,2},{7,3},{8,12},{9,13},{10,... | collective-permute-start | bytes 393224 | tf_op jit(solution)/shard_map/ppermute | solution.py:341
  129.6 20.4 %collective-permute-start.17 = (bf16[2,64,1024]{2,1,0:T(8,128)(2,1)S(1)}, bf16[2,64,1024]{2,1,0:T(8,128)(2,1)S(1)}, u32[]{:S(2)}, u32[]{:S(2)}) collective-permute-start(bf16[2,64,1024]{2,1,0:T(8,128)(2,1)S(1)} %pad_maximum_fusion.18), channel_id=1, source_target_pairs={{0,8},{1,9},{2,10},{3,11},{4,12},{5,13},{6,14},{7,15},{8,0},{9,1},... | collective-permute-start | bytes 786440 | tf_op jit(solution)/shard_map/ppermute | solution.py:341
  131.0 19.0 %collective-permute-start.16 = (bf16[272,512]{1,0:T(8,128)(2,1)S(1)}, bf16[272,512]{1,0:T(8,128)(2,1)S(1)}, u32[]{:S(2)}, u32[]{:S(2)}) collective-permute-start(bf16[272,512]{1,0:T(8,128)(2,1)S(1)} %fusion.75), channel_id=1, source_target_pairs={{0,2},{1,3},{2,0},{3,1},{4,6},{5,7},{6,4},{7,5},{8,10},{9,11},{10,... | collective-permute-start | bytes 835592 | tf_op jit(solution)/shard_map/ppermute | solution.py:341
  150.1 16.6 %collective-permute-start.19 = (bf16[4,64,1024]{2,1,0:T(8,128)(2,1)S(1)}, bf16[4,64,1024]{2,1,0:T(8,128)(2,1)S(1)}, u32[]{:S(2)}, u32[]{:S(2)}) collective-permute-start(bf16[4,64,1024]{2,1,0:T(8,128)(2,1)S(1)} %pad_maximum_fusion.9), channel_id=1, source_target_pairs={{0,2},{1,3},{2,0},{3,1},{4,6},{5,7},{6,4},{7,5},{8,10},{9,11},{10,... | collective-permute-start | bytes 1572872 | tf_op jit(solution)/shard_map/ppermute | solution.py:341
  154.9 11.1 %collective-permute-start.18 = (bf16[272,512]{1,0:T(8,128)(2,1)S(1)}, bf16[272,512]{1,0:T(8,128)(2,1)S(1)}, u32[]{:S(2)}, u32[]{:S(2)}) collective-permute-start(bf16[272,512]{1,0:T(8,128)(2,1)S(1)} %fusion.67), channel_id=1, source_target_pairs={{0,4},{1,5},{2,6},{3,7},{4,0},{5,1},{6,2},{7,3},{8,12},{9,13},{10,... | collective-permute-start | bytes 835592 | tf_op jit(solution)/shard_map/ppermute | solution.py:341
  167.1 13.9 %copy-start.19 = (bf16[272,512]{1,0:T(8,128)(2,1)}, bf16[272,512]{1,0:T(8,128)(2,1)S(1)}, u32[]{:S(2)}) copy-start(bf16[272,512]{1,0:T(8,128)(2,1)S(1)} %fusion.71) | copy-start | bytes 835588
  167.1 13.7 %collective-permute-start.20 = (bf16[272,512]{1,0:T(8,128)(2,1)S(1)}, bf16[272,512]{1,0:T(8,128)(2,1)S(1)}, u32[]{:S(2)}, u32[]{:S(2)}) collective-permute-start(bf16[272,512]{1,0:T(8,128)(2,1)S(1)} %fusion.71), channel_id=1, source_target_pairs={{0,8},{1,9},{2,10},{3,11},{4,12},{5,13},{6,14},{7,15},{8,0},{9,1},... | collective-permute-start | bytes 835592 | tf_op jit(solution)/shard_map/ppermute | solution.py:341
  167.3 14.3 %copy-start.49 = (f32[1,1024]{1,0:T(1,128)S(1)}, f32[1,1024]{1,0:T(1,128)}, u32[]{:S(2)}) copy-start(f32[1,1024]{1,0:T(1,128)} %get-tuple-element.199) | copy-start | bytes 12292
  167.3 14.3 %copy-start.56 = (pred[272]{0:T(512)(128)(4,1)S(1)}, pred[272]{0:T(512)(128)(4,1)}, u32[]{:S(2)}) copy-start(pred[272]{0:T(512)(128)(4,1)} %iota_compare_fusion.11) | copy-start | bytes 820
  180.9 102.7 %copy-start.47 = (bf16[512]{0:T(512)(128)(2,1)}, bf16[512]{0:T(512)(128)(2,1)S(1)}, u32[]{:S(2)}) copy-start(bf16[512]{0:T(512)(128)(2,1)S(1)} %get-tuple-element.96) | copy-start | bytes 3076
  180.9 102.7 %copy-start.48 = (bf16[512]{0:T(512)(128)(2,1)}, bf16[512]{0:T(512)(128)(2,1)S(1)}, u32[]{:S(2)}) copy-start(bf16[512]{0:T(512)(128)(2,1)S(1)} %get-tuple-element.97) | copy-start | bytes 3076
  181.0 102.7 %copy-start.43 = (bf16[512]{0:T(512)(128)(2,1)}, bf16[512]{0:T(512)(128)(2,1)S(1)}, u32[]{:S(2)}) copy-start(bf16[512]{0:T(512)(128)(2,1)S(1)} %get-tuple-element.98) | copy-start | bytes 3076
  181.0 102.7 %copy-start.44 = (bf16[512]{0:T(512)(128)(2,1)}, bf16[512]{0:T(512)(128)(2,1)S(1)}, u32[]{:S(2)}) copy-start(bf16[512]{0:T(512)(128)(2,1)S(1)} %get-tuple-element.99) | copy-start | bytes 3076
  279.0 7.1 %collective-permute-start.21 = (bf16[32,1024]{1,0:T(8,128)(2,1)}, bf16[32,1024]{1,0:T(8,128)(2,1)}, u32[]{:S(2)}, u32[]{:S(2)}) collective-permute-start(bf16[32,1024]{1,0:T(8,128)(2,1)} %constant_dynamic-slice_fusion.17), channel_id=1, source_target_pairs={{0,1},{1,0},{2,3},{3,2},{4,5},{5,4},{6,7},{7,6},{8,9},{9,8},{10,11... | collective-permute-start | bytes 196616 | tf_op jit(solution)/shard_map/ppermute | solution.py:341
  284.0 8.4 %collective-permute-start.22 = (bf16[272,512]{1,0:T(8,128)(2,1)S(1)}, bf16[272,512]{1,0:T(8,128)(2,1)S(1)}, u32[]{:S(2)}, u32[]{:S(2)}) collective-permute-start(bf16[272,512]{1,0:T(8,128)(2,1)S(1)} %select_select_fusion.2), channel_id=1, source_target_pairs={{0,1},{1,0},{2,3},{3,2},{4,5},{5,4},{6,7},{7,6},{8,9},{9,8},{10,11... | collective-permute-start | bytes 835592 | tf_op jit(solution)/shard_map/ppermute | solution.py:341
  286.1 22.6 %collective-permute-start.25 = (f32[600,1024]{1,0:T(8,128)}, f32[600,1024]{1,0:T(8,128)S(1)}, u32[]{:S(2)}, u32[]{:S(2)}) collective-permute-start(f32[600,1024]{1,0:T(8,128)} %get-tuple-element.47), channel_id=1, source_target_pairs={{0,16},{16,0},{1,17},{17,1},{2,18},{18,2},{3,19},{19,3},{4,20},{20... | collective-permute-start | bytes 7372808 | tf_op jit(solution)/shard_map/ppermute | solution.py:344
  298.6 7.5 %collective-permute-start.23 = (bf16[272,512]{1,0:T(8,128)(2,1)S(1)}, bf16[272,512]{1,0:T(8,128)(2,1)S(1)}, u32[]{:S(2)}, u32[]{:S(2)}) collective-permute-start(bf16[272,512]{1,0:T(8,128)(2,1)S(1)} %dynamic-slice_bitcast_fusion), channel_id=1, source_target_pairs={{0,1},{1,0},{2,3},{3,2},{4,5},{5,4},{6,7},{7,6},{8,9},{9,8},{10,11... | collective-permute-start | bytes 835592 | tf_op jit(solution)/shard_map/ppermute | solution.py:341
  306.3 6.6 %collective-permute-start.24 = (bf16[272,512]{1,0:T(8,128)(2,1)S(1)}, bf16[272,512]{1,0:T(8,128)(2,1)S(1)}, u32[]{:S(2)}, u32[]{:S(2)}) collective-permute-start(bf16[272,512]{1,0:T(8,128)(2,1)S(1)} %fusion.79), channel_id=1, source_target_pairs={{0,2},{1,3},{2,0},{3,1},{4,6},{5,7},{6,4},{7,5},{8,10},{9,11},{10,... | collective-permute-start | bytes 835592 | tf_op jit(solution)/shard_map/ppermute | solution.py:341
  309.4 15.5 %copy-start.3 = (f32[600,1024]{1,0:T(8,128)}, f32[600,1024]{1,0:T(8,128)S(1)}, u32[]{:S(2)}) copy-start(f32[600,1024]{1,0:T(8,128)S(1)} %add.481) | copy-start | bytes 7372804
  313.3 6.6 %collective-permute-start.26 = (bf16[272,512]{1,0:T(8,128)(2,1)S(1)}, bf16[272,512]{1,0:T(8,128)(2,1)S(1)}, u32[]{:S(2)}, u32[]{:S(2)}) collective-permute-start(bf16[272,512]{1,0:T(8,128)(2,1)S(1)} %select_select_fusion.1), channel_id=1, source_target_pairs={{0,4},{1,5},{2,6},{3,7},{4,0},{5,1},{6,2},{7,3},{8,12},{9,13},{10,... | collective-permute-start | bytes 835592 | tf_op jit(solution)/shard_map/ppermute | solution.py:341
  313.9 17.7 %collective-permute-start.28 = (bf16[312,1024]{1,0:T(8,128)(2,1)S(1)}, bf16[312,1024]{1,0:T(8,128)(2,1)S(1)}, u32[]{:S(2)}, u32[]{:S(2)}) collective-permute-start(bf16[312,1024]{1,0:T(8,128)(2,1)S(1)} %pad_maximum_fusion.6), channel_id=1, source_target_pairs={{0,1},{1,0},{2,3},{3,2},{4,5},{5,4},{6,7},{7,6},{8,9},{9,8},{10,11... | collective-permute-start | bytes 1916936 | tf_op jit(solution)/shard_map/ppermute | solution.py:341
  320.3 11.2 %collective-permute-start.27 = (bf16[272,512]{1,0:T(8,128)(2,1)S(1)}, bf16[272,512]{1,0:T(8,128)(2,1)S(1)}, u32[]{:S(2)}, u32[]{:S(2)}) collective-permute-start(bf16[272,512]{1,0:T(8,128)(2,1)S(1)} %select_select_fusion), channel_id=1, source_target_pairs={{0,8},{1,9},{2,10},{3,11},{4,12},{5,13},{6,14},{7,15},{8,0},{9,1},... | collective-permute-start | bytes 835592 | tf_op jit(solution)/shard_map/ppermute | solution.py:341
  344.9 3.1 collective-permute-start.30
  347.4 6.4 %collective-permute-start.29 = (f32[32,1024]{1,0:T(8,128)S(1)}, f32[32,1024]{1,0:T(8,128)S(1)}, u32[]{:S(2)}, u32[]{:S(2)}) collective-permute-start(f32[32,1024]{1,0:T(8,128)S(1)} %constant_dynamic-slice_fusion.14), channel_id=1, source_target_pairs={{0,1},{1,0},{2,3},{3,2},{4,5},{5,4},{6,7},{7,6},{8,9},{9,8},{10,11... | collective-permute-start | bytes 393224 | tf_op jit(solution)/shard_map/ppermute | solution.py:341
  348.2 11.2 %collective-permute-start.31 = (f32[40,1792]{1,0:T(8,128)S(1)}, f32[40,1792]{1,0:T(8,128)S(1)}, u32[]{:S(2)}, u32[]{:S(2)}) collective-permute-start(f32[40,1792]{1,0:T(8,128)S(1)} %pad_maximum_fusion.10), channel_id=1, source_target_pairs={{0,1},{1,0},{2,3},{3,2},{4,5},{5,4},{6,7},{7,6},{8,9},{9,8},{10,11... | collective-permute-start | bytes 860168 | tf_op jit(solution)/shard_map/ppermute | solution.py:341
  (45 other events, 188.8 us)
Sparse Core Ops, SparseCore 0:
  10.9 151.8 all-gather.1

commit v5 on v4

--- a/solution.py
+++ b/solution.py
@@ -56,9 +56,9 @@
     out_rows = 9 * part_rows + extra
     shares = 2 * aligned
     stacked = shares + 16
-    chunk = 32
-    block = 256
-    part = 128
+    chunk = 128
+    block = 512
+    part = 512
     cubic = 0.044715
     root = math.sqrt(2.0 / math.pi)
 
@@ -488,8 +488,6 @@
         mine = lax.dynamic_slice_in_dim(array, place * rows, rows, 0)
         theirs = lax.dynamic_slice_in_dim(array, (place ^ 1) * rows, rows, 0)
         return ordered(mine[None], swap(theirs, 1)[None], parity, 0)
-
-    latents_out = own_rows(final)
 
     def share(a):
         return jnp.concatenate([lax.dynamic_slice_in_dim(a, s * n * own_w + base, aligned, 1) for s in range(2)], axis=1)
@@ -544,6 +542,7 @@
         if chip_sums is None:
             core_sums = after(keep, mine) + core_sums
             other, core_sums = lax.optimization_barrier((other, core_sums))
+            latents_out = own_rows(after(final, mine))
             chip_sums = swap(halved(core_sums, 1 - parity).astype(b16), 1)
             part_att = matmul("ia,ci->ac", share(d_attended), mean_low)
             other = after(other, part_att)

time: 373 us -> 338 us (0.906)
  Pallas kernels: 93 us -> 55 us
    pallas_call x1, Pallas kernels: 93 us -> 55 us  [latent_part(): pl.pallas_call(kernel, name='latent_part', in_specs=[pl.BlockSpec(memory_...]
  transfers between devices with their start and end apart: 33 -> 33, of which waited for: 21 -> 21; matrix products, arithmetic and copies ran while one was open for 16% -> 17% of each run, Pallas kernels for 0% -> 0%
where the time goes in v5:
time: 338 us; the launch traced here: 335 us
  waiting for transfers between devices  143 us (42%)
  Pallas kernels  55 us (16%)
  starting transfers between devices  37.4 us (11%)
  local copies, waits for them, and re-layouts  30.2 us (9%)
  other arithmetic  30 us (9%)
  matrix products  23.6 us (7%)
  between operations  15.9 us (5%)
    ppermute x29, waiting for transfers between devices, swap(): return lax.ppermute(x, 'ctx', [(i, i ^ bit) for i in range(n)])  143 us
    pallas_call x1, Pallas kernels, latent_part(): pl.pallas_call(kernel, name='latent_part', in_specs=[pl.BlockSpec(memory_...  55 us
    ppermute x29, starting transfers between devices, swap(): return lax.ppermute(x, 'ctx', [(i, i ^ bit) for i in range(n)])  37.3 us
    dot_general x15, matrix products, matmul(): return jnp.einsum(form, left, right, preferred_element_type=f32)  23.6 us
    unnamed x123, local copies, waits for them, and re-layouts  10.2 us
  transfers between devices with their start and end apart: 33, of which 21 were waited for; matrix products, arithmetic and copies ran while one was open for 17% of the time, Pallas kernels for 0%

profile of v5, /device:TPU:0, one launch (start us, length us, event | category | flops | bytes accessed | tf_op | source)
XLA Modules:
  0.0 334.9 jit_solution(8608763070894185353)
XLA Ops:
  7.3 2.0 slice.335
  11.8 5.1 %collective-permute-start.2 = (bf16[1,1,1,32,1792]{4,3,0,2,1:T(8,128)(2,1)S(1)}, bf16[1,1,1,32,1792]{4,3,0,2,1:T(8,128)(2,1)S(1)}, u32[]{:S(2)}, u32[]{:S(2)}) collective-permute-start(bf16[1,1,1,32,1792]{4,3,0,2,1:T(8,128)(2,1)S(1)} %bitcast.153), channel_id=1, source_target_pairs={{0,12},{1,13},{2,14},{3,15},{4,8},{5,9},{6,10},{7,11},{8,4},{9,5},... | collective-permute-start | bytes 344072 | tf_op jit(solution)/shard_map/ppermute | solution.py:341
  17.6 1.7 collective-permute-start.7
  22.0 3.8 %collective-permute-start.10 = (bf16[1,1,1,64,1024]{4,3,2,1,0:T(8,128)(2,1)S(1)}, bf16[1,1,1,64,1024]{4,3,2,1,0:T(8,128)(2,1)S(1)}, u32[]{:S(2)}, u32[]{:S(2)}) collective-permute-start(bf16[1,1,1,64,1024]{4,3,2,1,0:T(8,128)(2,1)S(1)} %maximum_bitcast_fusion.3), channel_id=1, source_target_pairs={{0,12},{1,13},{2,14},{3,15},{4,8},{5,9},{6,10},{7,11},{8,4},{9,5},... | collective-permute-start | bytes 393224 | tf_op jit(solution)/shard_map/ppermute | solution.py:341
  25.8 1.4 collective-permute-done
  27.1 2.5 collective-permute-start.8
  29.7 9.1 %collective-permute-done.1 = bf16[1,1,1,32,1792]{4,3,0,2,1:T(8,128)(2,1)S(1)} collective-permute-done((bf16[1,1,1,32,1792]{4,3,0,2,1:T(8,128)(2,1)S(1)}, bf16[1,1,1,32,1792]{4,3,0,2,1:T(8,128)(2,1)S(1)}, u32[]{:S(2)}, u32[]{:S(2)}) %collective-permute-start.1) | collective-permute-done | bytes 114720 | tf_op jit(solution)/shard_map/ppermute | solution.py:341
  38.9 2.5 collective-permute-start.5
  43.0 1.4 collective-permute-start.3
  44.4 5.9 %collective-permute-done.9 = bf16[1,1,1,64,1024]{4,3,2,1,0:T(8,128)(2,1)S(1)} collective-permute-done((bf16[1,1,1,64,1024]{4,3,2,1,0:T(8,128)(2,1)S(1)}, bf16[1,1,1,64,1024]{4,3,2,1,0:T(8,128)(2,1)S(1)}, u32[]{:S(2)}, u32[]{:S(2)}) %collective-permute-start.9) | collective-permute-done | bytes 131104 | tf_op jit(solution)/shard_map/ppermute | solution.py:341
  50.3 9.9 %collective-permute-done.3 = bf16[4,1,32,1792]{3,2,1,0:T(8,128)(2,1)S(1)} collective-permute-done((bf16[4,1,32,1792]{3,2,1,0:T(8,128)(2,1)S(1)}, bf16[4,1,32,1792]{3,2,1,0:T(8,128)(2,1)S(1)}, u32[]{:S(2)}, u32[]{:S(2)}) %collective-permute-start.3) | collective-permute-done | bytes 458784 | tf_op jit(solution)/shard_map/ppermute | solution.py:341
  60.5 1.4 pad_maximum_fusion
  61.9 4.0 %copy.40 = bf16[1,512,1792]{1,2,0:T(8,128)(2,1)} copy(bf16[1,512,1792]{2,1,0:T(8,128)(2,1)} %bitcast.146) | data formatting | bytes 3670016 | tf_op jit(solution)/shard_map/reshape | solution.py:396
  66.2 1.4 fusion.9
  67.6 12.8 %collective-permute-done.11 = bf16[4,1,64,1024]{3,2,0,1:T(8,128)(2,1)S(1)} collective-permute-done((bf16[4,1,64,1024]{3,2,0,1:T(8,128)(2,1)S(1)}, bf16[4,1,64,1024]{3,2,0,1:T(8,128)(2,1)S(1)}, u32[]{:S(2)}, u32[]{:S(2)}) %collective-permute-start.11) | collective-permute-done | bytes 524320 | tf_op jit(solution)/shard_map/ppermute | solution.py:341
  81.6 1.5 fusion.16
  83.3 2.3 broadcast_select_fusion.1
  90.3 2.5 collective-permute-start.12
  93.5 15.3 %collective-permute-done.13 = bf16[32,1024]{1,0:T(8,128)(2,1)S(1)} collective-permute-done((bf16[32,1024]{1,0:T(8,128)(2,1)S(1)}, bf16[32,1024]{1,0:T(8,128)(2,1)S(1)}, u32[]{:S(2)}, u32[]{:S(2)}) %collective-permute-start.13) | collective-permute-done | bytes 65568 | tf_op jit(solution)/shard_map/ppermute | solution.py:341
  108.9 1.4 select_reduce_fusion
  114.2 2.0 collective-permute-start.14
  117.7 4.4 %collective-permute-done.15 = bf16[1,64,1024]{2,1,0:T(8,128)(2,1)S(1)} collective-permute-done((bf16[1,64,1024]{2,1,0:T(8,128)(2,1)S(1)}, bf16[1,64,1024]{2,1,0:T(8,128)(2,1)S(1)}, u32[]{:S(2)}, u32[]{:S(2)}) %collective-permute-start.15) | collective-permute-done | bytes 131104 | tf_op jit(solution)/shard_map/ppermute | solution.py:341
  122.0 7.2 %collective-permute-done.14 = bf16[272,512]{1,0:T(8,128)(2,1)S(1)} collective-permute-done((bf16[272,512]{1,0:T(8,128)(2,1)S(1)}, bf16[272,512]{1,0:T(8,128)(2,1)S(1)}, u32[]{:S(2)}, u32[]{:S(2)}) %collective-permute-start.14) | collective-permute-done | bytes 278560 | tf_op jit(solution)/shard_map/ppermute | solution.py:341
  132.2 17.8 %collective-permute-done.17 = bf16[2,64,1024]{2,1,0:T(8,128)(2,1)S(1)} collective-permute-done((bf16[2,64,1024]{2,1,0:T(8,128)(2,1)S(1)}, bf16[2,64,1024]{2,1,0:T(8,128)(2,1)S(1)}, u32[]{:S(2)}, u32[]{:S(2)}) %collective-permute-start.17) | collective-permute-done | bytes 262176 | tf_op jit(solution)/shard_map/ppermute | solution.py:341
  150.1 4.5 %collective-permute-start.19 = (bf16[4,64,1024]{2,1,0:T(8,128)(2,1)S(1)}, bf16[4,64,1024]{2,1,0:T(8,128)(2,1)S(1)}, u32[]{:S(2)}, u32[]{:S(2)}) collective-permute-start(bf16[4,64,1024]{2,1,0:T(8,128)(2,1)S(1)} %pad_maximum_fusion.9), channel_id=1, source_target_pairs={{0,2},{1,3},{2,0},{3,1},{4,6},{5,7},{6,4},{7,5},{8,10},{9,11},{10,... | collective-permute-start | bytes 1572872 | tf_op jit(solution)/shard_map/ppermute | solution.py:341
  155.0 1.7 constant_dynamic-slice_fusion.10
  157.3 8.7 %collective-permute-done.18 = bf16[272,512]{1,0:T(8,128)(2,1)S(1)} collective-permute-done((bf16[272,512]{1,0:T(8,128)(2,1)S(1)}, bf16[272,512]{1,0:T(8,128)(2,1)S(1)}, u32[]{:S(2)}, u32[]{:S(2)}) %collective-permute-start.18) | collective-permute-done | bytes 278560 | tf_op jit(solution)/shard_map/ppermute | solution.py:341
  168.5 12.4 %collective-permute-done.20 = bf16[272,512]{1,0:T(8,128)(2,1)S(1)} collective-permute-done((bf16[272,512]{1,0:T(8,128)(2,1)S(1)}, bf16[272,512]{1,0:T(8,128)(2,1)S(1)}, u32[]{:S(2)}, u32[]{:S(2)}) %collective-permute-start.20) | collective-permute-done | bytes 278560 | tf_op jit(solution)/shard_map/ppermute | solution.py:341
  181.6 2.9 add_convert_fusion.att
  184.5 55.0 %latent_part.1 = (bf16[512,1024]{1,0:T(8,128)(2,1)}, bf16[512,1024]{1,0:T(8,128)(2,1)}, f32[512,1024]{1,0:T(8,128)}, f32[600,1024]{1,0:T(8,128)}, f32[600,1024]{1,0:T(8,128)}) custom-call(s32[4]{0:T(128)} %pad_add_fusion.num, bf16[512,1024]{1,0:T(8,128)(2,1)} %add_convert_fusion.att, bf16[512,1024]{1,0:T(8,128)(2,1)} %bitcast.145, f32[24,1024]{1,0:T(8,128)} %pad.39.vec, ...), custom_call_target="tpu_custom_call" | custom-call | tf_op jit(solution)/shard_map/latent_part/pallas_call | solution.py:297
  240.6 2.1 multiply_reduce_fusion.4
  243.2 1.5 collective-permute-start.21
  246.1 5.8 %collective-permute-done.21 = bf16[272,512]{1,0:T(8,128)(2,1)S(1)} collective-permute-done((bf16[272,512]{1,0:T(8,128)(2,1)S(1)}, bf16[272,512]{1,0:T(8,128)(2,1)S(1)}, u32[]{:S(2)}, u32[]{:S(2)}) %collective-permute-start.21) | collective-permute-done | bytes 278560 | tf_op jit(solution)/shard_map/ppermute | solution.py:341
  252.9 4.1 %multiply_convert_fusion = bf16[2,512,1024]{2,1,0:T(8,128)(2,1)S(1)} fusion(f32[2,512]{1,0:T(2,128)S(1)} %bitcast.174, f32[2,512]{1,0:T(2,128)S(1)} %bitcast.172, f32[2,512,1024]{2,1,0:T(8,128)} %copy-done.8, f32[2,512]{1,0:T(2,128)S(1)} %bitcast.170, pred[2,1024]{1,0:T(4,128)(4,1)S(1)} %copy-done.42, bf16[2,261,1024]{2,1,0:T(8,128)(2,1)} %fusion.9, ...), kind=kOutput, calls=%fused_computation | convolution fusion | flops 576995328 | bytes 7931904 | tf_op jit(solution)/shard_map/qci,qcj->qij/dot_general | solution.py:17
  258.6 1.4 copy-done.9
  262.7 1.5 collective-permute-start.22
  264.2 6.2 %collective-permute-done.22 = bf16[272,512]{1,0:T(8,128)(2,1)S(1)} collective-permute-done((bf16[272,512]{1,0:T(8,128)(2,1)S(1)}, bf16[272,512]{1,0:T(8,128)(2,1)S(1)}, u32[]{:S(2)}, u32[]{:S(2)}) %collective-permute-start.22) | collective-permute-done | bytes 278560 | tf_op jit(solution)/shard_map/ppermute | solution.py:341
  270.7 1.5 collective-permute-start.24
  273.0 3.0 copy.51
  278.9 1.4 collective-permute-start.23
  281.4 3.3 collective-permute-done.26
  287.0 9.5 %collective-permute-done.27 = bf16[272,512]{1,0:T(8,128)(2,1)S(1)} collective-permute-done((bf16[272,512]{1,0:T(8,128)(2,1)S(1)}, bf16[272,512]{1,0:T(8,128)(2,1)S(1)}, u32[]{:S(2)}, u32[]{:S(2)}) %collective-permute-start.27) | collective-permute-done | bytes 278560 | tf_op jit(solution)/shard_map/ppermute | solution.py:341
  297.5 2.6 convert_reduce_fusion.2
  300.3 3.6 %multiply_reduce_fusion = (f32[1024]{0:T(1024)}, f32[512]{0:T(512)S(1)}, f32[512]{0:T(512)S(1)}, f32[1024]{0:T(1024)}, f32[512,1024]{1,0:T(8,128)}) fusion(f32[512]{0:T(512)S(1)} %copy-done.40, f32[512]{0:T(512)S(1)} %copy-done.37, bf16[4,2,64,1024]{3,2,1,0:T(8,128)(2,1)S(1)} %copy-done.2, f32[1024]{0:T(1024)S(1)} %bitcast.157, ...), kind=kOutput, calls=%fused_computation.29 | convolution fusion | flops 1078981632 | bytes 6311936 | tf_op jit(solution)/shard_map/ie,de->id/dot_general | solution.py:17
  310.0 2.3 multiply_add_fusion
  312.3 1.4 collective-permute-start.29
  314.7 4.1 %collective-permute-done.29 = f32[32,1024]{1,0:T(8,128)S(1)} collective-permute-done((f32[32,1024]{1,0:T(8,128)S(1)}, f32[32,1024]{1,0:T(8,128)S(1)}, u32[]{:S(2)}, u32[]{:S(2)}) %collective-permute-start.29) | collective-permute-done | bytes 131104 | tf_op jit(solution)/shard_map/ppermute | solution.py:341
  319.5 4.9 %collective-permute-done.31 = f32[40,1792]{1,0:T(8,128)S(1)} collective-permute-done((f32[40,1792]{1,0:T(8,128)S(1)}, f32[40,1792]{1,0:T(8,128)S(1)}, u32[]{:S(2)}, u32[]{:S(2)}) %collective-permute-start.31) | collective-permute-done | bytes 286752 | tf_op jit(solution)/shard_map/ppermute | solution.py:341
  (320 shorter events, 54.3 us)
Async XLA Ops:
  7.2 12.1 %copy-start.52 = (bf16[2,261]{1,0:T(2,128)(2,1)S(1)}, bf16[2,261]{1,0:T(2,128)(2,1)}, u32[]{:S(2)}) copy-start(bf16[2,261]{1,0:T(2,128)(2,1)} %param.14) | copy-start | bytes 3136
  7.2 12.2 %copy-start = (bf16[2,261,1024]{2,0,1:T(2,128)(2,1)S(1)}, bf16[2,261,1024]{2,0,1:T(2,128)(2,1)}, u32[]{:S(2)}) copy-start(bf16[2,261,1024]{2,0,1:T(2,128)(2,1)} %param.8) | copy-start | bytes 3207172
  7.2 12.7 %copy-start.53 = (s32[2]{0:T(128)S(1)}, s32[2]{0:T(128)}, u32[]{:S(2)}) copy-start(s32[2]{0:T(128)} %param.9) | copy-start | bytes 28
  7.2 177.3 %all-gather.2.cloned.1.call-start = ((), (), s32[]{:S(2)}) async-start(), calls=%async_computation | async-start | bytes 19464192 | tf_op jit(solution)/shard_map/all_gather | solution.py:406
  11.8 17.8 %collective-permute-start.2 = (bf16[1,1,1,32,1792]{4,3,0,2,1:T(8,128)(2,1)S(1)}, bf16[1,1,1,32,1792]{4,3,0,2,1:T(8,128)(2,1)S(1)}, u32[]{:S(2)}, u32[]{:S(2)}) collective-permute-start(bf16[1,1,1,32,1792]{4,3,0,2,1:T(8,128)(2,1)S(1)} %bitcast.153), channel_id=1, source_target_pairs={{0,12},{1,13},{2,14},{3,15},{4,8},{5,9},{6,10},{7,11},{8,4},{9,5},... | collective-permute-start | bytes 344072 | tf_op jit(solution)/shard_map/ppermute | solution.py:341
  16.9 21.8 %collective-permute-start.1 = (bf16[1,1,1,32,1792]{4,3,0,2,1:T(8,128)(2,1)S(1)}, bf16[1,1,1,32,1792]{4,3,0,2,1:T(8,128)(2,1)S(1)}, u32[]{:S(2)}, u32[]{:S(2)}) collective-permute-start(bf16[1,1,1,32,1792]{4,3,0,2,1:T(8,128)(2,1)S(1)} %bitcast.154), channel_id=1, source_target_pairs={{0,8},{1,9},{2,10},{3,11},{4,12},{5,13},{6,14},{7,15},{8,0},{9,1},... | collective-permute-start | bytes 344072 | tf_op jit(solution)/shard_map/ppermute | solution.py:341
  16.9 10.2 %collective-permute-start = (bf16[1,1,1,32,1792]{4,3,0,2,1:T(8,128)(2,1)S(1)}, bf16[1,1,1,32,1792]{4,3,0,2,1:T(8,128)(2,1)S(1)}, u32[]{:S(2)}, u32[]{:S(2)}) collective-permute-start(bf16[1,1,1,32,1792]{4,3,0,2,1:T(8,128)(2,1)S(1)} %bitcast.155), channel_id=1, source_target_pairs={{0,4},{1,5},{2,6},{3,7},{4,0},{5,1},{6,2},{7,3},{8,12},{9,13},{10,... | collective-permute-start | bytes 344072 | tf_op jit(solution)/shard_map/ppermute | solution.py:341
  17.6 4.3 %collective-permute-start.7 = (bf16[32,1024]{1,0:T(8,128)(2,1)S(1)}, bf16[32,1024]{1,0:T(8,128)(2,1)S(1)}, u32[]{:S(2)}, u32[]{:S(2)}) collective-permute-start(bf16[32,1024]{1,0:T(8,128)(2,1)S(1)} %dynamic-slice_bitcast_fusion.3), channel_id=1, source_target_pairs={{0,1},{1,0},{2,3},{3,2},{4,5},{5,4},{6,7},{7,6},{8,9},{9,8},{10,11... | collective-permute-start | bytes 196616 | tf_op jit(solution)/shard_map/ppermute | solution.py:341
  19.3 223.5 %copy-start.27 = (pred[272]{0:T(512)(128)(4,1)}, pred[272]{0:T(512)(128)(4,1)S(1)}, u32[]{:S(2)}) copy-start(pred[272]{0:T(512)(128)(4,1)S(1)} %get-tuple-element.217) | copy-start | bytes 820
  20.0 91.3 %copy-start.41 = (pred[2,1024]{1,0:T(4,128)(4,1)}, pred[2,1024]{1,0:T(4,128)(4,1)S(1)}, u32[]{:S(2)}) copy-start(pred[2,1024]{1,0:T(4,128)(4,1)S(1)} %broadcast_compare_fusion) | copy-start | bytes 6148
  22.0 22.5 %collective-permute-start.10 = (bf16[1,1,1,64,1024]{4,3,2,1,0:T(8,128)(2,1)S(1)}, bf16[1,1,1,64,1024]{4,3,2,1,0:T(8,128)(2,1)S(1)}, u32[]{:S(2)}, u32[]{:S(2)}) collective-permute-start(bf16[1,1,1,64,1024]{4,3,2,1,0:T(8,128)(2,1)S(1)} %maximum_bitcast_fusion.3), channel_id=1, source_target_pairs={{0,12},{1,13},{2,14},{3,15},{4,8},{5,9},{6,10},{7,11},{8,4},{9,5},... | collective-permute-start | bytes 393224 | tf_op jit(solution)/shard_map/ppermute | solution.py:341
  25.8 24.5 %collective-permute-start.9 = (bf16[1,1,1,64,1024]{4,3,2,1,0:T(8,128)(2,1)S(1)}, bf16[1,1,1,64,1024]{4,3,2,1,0:T(8,128)(2,1)S(1)}, u32[]{:S(2)}, u32[]{:S(2)}) collective-permute-start(bf16[1,1,1,64,1024]{4,3,2,1,0:T(8,128)(2,1)S(1)} %maximum_bitcast_fusion.3), channel_id=1, source_target_pairs={{0,8},{1,9},{2,10},{3,11},{4,12},{5,13},{6,14},{7,15},{8,0},{9,1},... | collective-permute-start | bytes 393224 | tf_op jit(solution)/shard_map/ppermute | solution.py:341
  27.1 15.8 %collective-permute-start.8 = (bf16[1,1,1,64,1024]{4,3,2,1,0:T(8,128)(2,1)S(1)}, bf16[1,1,1,64,1024]{4,3,2,1,0:T(8,128)(2,1)S(1)}, u32[]{:S(2)}, u32[]{:S(2)}) collective-permute-start(bf16[1,1,1,64,1024]{4,3,2,1,0:T(8,128)(2,1)S(1)} %maximum_bitcast_fusion.3), channel_id=1, source_target_pairs={{0,4},{1,5},{2,6},{3,7},{4,0},{5,1},{6,2},{7,3},{8,12},{9,13},{10,... | collective-permute-start | bytes 393224 | tf_op jit(solution)/shard_map/ppermute | solution.py:341
  38.9 21.4 %collective-permute-start.5 = (bf16[4,1,32,1792]{3,2,1,0:T(8,128)(2,1)S(1)}, bf16[4,1,32,1792]{3,2,1,0:T(8,128)(2,1)S(1)}, u32[]{:S(2)}, u32[]{:S(2)}) collective-permute-start(bf16[4,1,32,1792]{3,2,1,0:T(8,128)(2,1)S(1)} %maximum_bitcast_fusion.2), channel_id=1, source_target_pairs={{0,3},{1,2},{2,1},{3,0},{4,7},{5,6},{6,5},{7,4},{8,11},{9,10},{10,... | collective-permute-start | bytes 1376264 | tf_op jit(solution)/shard_map/ppermute | solution.py:341
  41.4 18.8 %collective-permute-start.4 = (bf16[4,1,32,1792]{3,2,1,0:T(8,128)(2,1)S(1)}, bf16[4,1,32,1792]{3,2,1,0:T(8,128)(2,1)S(1)}, u32[]{:S(2)}, u32[]{:S(2)}) collective-permute-start(bf16[4,1,32,1792]{3,2,1,0:T(8,128)(2,1)S(1)} %maximum_bitcast_fusion.2), channel_id=1, source_target_pairs={{0,2},{1,3},{2,0},{3,1},{4,6},{5,7},{6,4},{7,5},{8,10},{9,11},{10,... | collective-permute-start | bytes 1376264 | tf_op jit(solution)/shard_map/ppermute | solution.py:341
  43.0 17.2 %collective-permute-start.3 = (bf16[4,1,32,1792]{3,2,1,0:T(8,128)(2,1)S(1)}, bf16[4,1,32,1792]{3,2,1,0:T(8,128)(2,1)S(1)}, u32[]{:S(2)}, u32[]{:S(2)}) collective-permute-start(bf16[4,1,32,1792]{3,2,1,0:T(8,128)(2,1)S(1)} %maximum_bitcast_fusion.2), channel_id=1, source_target_pairs={{0,1},{1,0},{2,3},{3,2},{4,5},{5,4},{6,7},{7,6},{8,9},{9,8},{10,11... | collective-permute-start | bytes 1376264 | tf_op jit(solution)/shard_map/ppermute | solution.py:341
  65.9 17.3 %collective-permute-start.6 = (bf16[1,512,1792]{1,2,0:T(8,128)(2,1)}, bf16[1,512,1792]{1,2,0:T(8,128)(2,1)}, u32[]{:S(2)}, u32[]{:S(2)}) collective-permute-start(bf16[1,512,1792]{1,2,0:T(8,128)(2,1)} %copy.40), channel_id=1, source_target_pairs={{0,16},{16,0},{1,17},{17,1},{2,18},{18,2},{3,19},{19,3},{4,20},{20... | collective-permute-start | bytes 5505032 | tf_op jit(solution)/shard_map/ppermute | solution.py:344
  66.1 14.4 %collective-permute-start.11 = (bf16[4,1,64,1024]{3,2,0,1:T(8,128)(2,1)S(1)}, bf16[4,1,64,1024]{3,2,0,1:T(8,128)(2,1)S(1)}, u32[]{:S(2)}, u32[]{:S(2)}) collective-permute-start(bf16[4,1,64,1024]{3,2,0,1:T(8,128)(2,1)S(1)} %maximum_bitcast_fusion.1), channel_id=1, source_target_pairs={{0,2},{1,3},{2,0},{3,1},{4,6},{5,7},{6,4},{7,5},{8,10},{9,11},{10,... | collective-permute-start | bytes 1572872 | tf_op jit(solution)/shard_map/ppermute | solution.py:341
  66.1 176.7 %copy-start.30 = (pred[272]{0:T(512)(128)(4,1)}, pred[272]{0:T(512)(128)(4,1)S(1)}, u32[]{:S(2)}) copy-start(pred[272]{0:T(512)(128)(4,1)S(1)} %iota_compare_fusion.10) | copy-start | bytes 820
  89.4 19.5 %copy-start.14 = (bf16[2,261,1024]{2,1,0:T(8,128)(2,1)S(1)}, bf16[2,261,1024]{2,1,0:T(8,128)(2,1)}, u32[]{:S(2)}) copy-start(bf16[2,261,1024]{2,1,0:T(8,128)(2,1)} %fusion.9) | copy-start | bytes 3207172
  90.3 18.5 %collective-permute-start.12 = (bf16[272,512]{1,0:T(8,128)(2,1)S(1)}, bf16[272,512]{1,0:T(8,128)(2,1)S(1)}, u32[]{:S(2)}, u32[]{:S(2)}) collective-permute-start(bf16[272,512]{1,0:T(8,128)(2,1)S(1)} %fusion.33), channel_id=1, source_target_pairs={{0,1},{1,0},{2,3},{3,2},{4,5},{5,4},{6,7},{7,6},{8,9},{9,8},{10,11... | collective-permute-start | bytes 835592 | tf_op jit(solution)/shard_map/ppermute | solution.py:341
  92.8 150.0 %copy-start.33 = (pred[272]{0:T(512)(128)(4,1)}, pred[272]{0:T(512)(128)(4,1)S(1)}, u32[]{:S(2)}) copy-start(pred[272]{0:T(512)(128)(4,1)S(1)} %iota_compare_fusion.9) | copy-start | bytes 820
  92.8 16.0 %collective-permute-start.13 = (bf16[32,1024]{1,0:T(8,128)(2,1)S(1)}, bf16[32,1024]{1,0:T(8,128)(2,1)S(1)}, u32[]{:S(2)}, u32[]{:S(2)}) collective-permute-start(bf16[32,1024]{1,0:T(8,128)(2,1)S(1)} %dynamic-slice_bitcast_fusion.2), channel_id=1, source_target_pairs={{0,1},{1,0},{2,3},{3,2},{4,5},{5,4},{6,7},{7,6},{8,9},{9,8},{10,11... | collective-permute-start | bytes 196616 | tf_op jit(solution)/shard_map/ppermute | solution.py:341
  114.2 15.0 %collective-permute-start.14 = (bf16[272,512]{1,0:T(8,128)(2,1)S(1)}, bf16[272,512]{1,0:T(8,128)(2,1)S(1)}, u32[]{:S(2)}, u32[]{:S(2)}) collective-permute-start(bf16[272,512]{1,0:T(8,128)(2,1)S(1)} %dynamic-slice_bitcast_fusion.1), channel_id=1, source_target_pairs={{0,1},{1,0},{2,3},{3,2},{4,5},{5,4},{6,7},{7,6},{8,9},{9,8},{10,11... | collective-permute-start | bytes 835592 | tf_op jit(solution)/shard_map/ppermute | solution.py:341
  116.2 5.8 %collective-permute-start.15 = (bf16[1,64,1024]{2,1,0:T(8,128)(2,1)S(1)}, bf16[1,64,1024]{2,1,0:T(8,128)(2,1)S(1)}, u32[]{:S(2)}, u32[]{:S(2)}) collective-permute-start(bf16[1,64,1024]{2,1,0:T(8,128)(2,1)S(1)} %maximum_bitcast_fusion.4), channel_id=1, source_target_pairs={{0,4},{1,5},{2,6},{3,7},{4,0},{5,1},{6,2},{7,3},{8,12},{9,13},{10,... | collective-permute-start | bytes 393224 | tf_op jit(solution)/shard_map/ppermute | solution.py:341
  129.3 20.7 %collective-permute-start.17 = (bf16[2,64,1024]{2,1,0:T(8,128)(2,1)S(1)}, bf16[2,64,1024]{2,1,0:T(8,128)(2,1)S(1)}, u32[]{:S(2)}, u32[]{:S(2)}) collective-permute-start(bf16[2,64,1024]{2,1,0:T(8,128)(2,1)S(1)} %pad_maximum_fusion.18), channel_id=1, source_target_pairs={{0,8},{1,9},{2,10},{3,11},{4,12},{5,13},{6,14},{7,15},{8,0},{9,1},... | collective-permute-start | bytes 786440 | tf_op jit(solution)/shard_map/ppermute | solution.py:341
  130.7 19.3 %collective-permute-start.16 = (bf16[272,512]{1,0:T(8,128)(2,1)S(1)}, bf16[272,512]{1,0:T(8,128)(2,1)S(1)}, u32[]{:S(2)}, u32[]{:S(2)}) collective-permute-start(bf16[272,512]{1,0:T(8,128)(2,1)S(1)} %fusion.75), channel_id=1, source_target_pairs={{0,2},{1,3},{2,0},{3,1},{4,6},{5,7},{6,4},{7,5},{8,10},{9,11},{10,... | collective-permute-start | bytes 835592 | tf_op jit(solution)/shard_map/ppermute | solution.py:341
  150.1 16.7 %collective-permute-start.19 = (bf16[4,64,1024]{2,1,0:T(8,128)(2,1)S(1)}, bf16[4,64,1024]{2,1,0:T(8,128)(2,1)S(1)}, u32[]{:S(2)}, u32[]{:S(2)}) collective-permute-start(bf16[4,64,1024]{2,1,0:T(8,128)(2,1)S(1)} %pad_maximum_fusion.9), channel_id=1, source_target_pairs={{0,2},{1,3},{2,0},{3,1},{4,6},{5,7},{6,4},{7,5},{8,10},{9,11},{10,... | collective-permute-start | bytes 1572872 | tf_op jit(solution)/shard_map/ppermute | solution.py:341
  154.9 11.1 %collective-permute-start.18 = (bf16[272,512]{1,0:T(8,128)(2,1)S(1)}, bf16[272,512]{1,0:T(8,128)(2,1)S(1)}, u32[]{:S(2)}, u32[]{:S(2)}) collective-permute-start(bf16[272,512]{1,0:T(8,128)(2,1)S(1)} %fusion.67), channel_id=1, source_target_pairs={{0,4},{1,5},{2,6},{3,7},{4,0},{5,1},{6,2},{7,3},{8,12},{9,13},{10,... | collective-permute-start | bytes 835592 | tf_op jit(solution)/shard_map/ppermute | solution.py:341
  167.1 13.9 %copy-start.19 = (bf16[272,512]{1,0:T(8,128)(2,1)}, bf16[272,512]{1,0:T(8,128)(2,1)S(1)}, u32[]{:S(2)}) copy-start(bf16[272,512]{1,0:T(8,128)(2,1)S(1)} %fusion.71) | copy-start | bytes 835588
  167.1 13.7 %collective-permute-start.20 = (bf16[272,512]{1,0:T(8,128)(2,1)S(1)}, bf16[272,512]{1,0:T(8,128)(2,1)S(1)}, u32[]{:S(2)}, u32[]{:S(2)}) collective-permute-start(bf16[272,512]{1,0:T(8,128)(2,1)S(1)} %fusion.71), channel_id=1, source_target_pairs={{0,8},{1,9},{2,10},{3,11},{4,12},{5,13},{6,14},{7,15},{8,0},{9,1},... | collective-permute-start | bytes 835592 | tf_op jit(solution)/shard_map/ppermute | solution.py:341
  167.3 14.3 %copy-start.49 = (f32[1,1024]{1,0:T(1,128)S(1)}, f32[1,1024]{1,0:T(1,128)}, u32[]{:S(2)}) copy-start(f32[1,1024]{1,0:T(1,128)} %get-tuple-element.201) | copy-start | bytes 12292
  167.3 14.3 %copy-start.56 = (pred[272]{0:T(512)(128)(4,1)S(1)}, pred[272]{0:T(512)(128)(4,1)}, u32[]{:S(2)}) copy-start(pred[272]{0:T(512)(128)(4,1)} %iota_compare_fusion.11) | copy-start | bytes 820
  180.9 61.9 %copy-start.47 = (bf16[512]{0:T(512)(128)(2,1)}, bf16[512]{0:T(512)(128)(2,1)S(1)}, u32[]{:S(2)}) copy-start(bf16[512]{0:T(512)(128)(2,1)S(1)} %get-tuple-element.98) | copy-start | bytes 3076
  180.9 61.9 %copy-start.48 = (bf16[512]{0:T(512)(128)(2,1)}, bf16[512]{0:T(512)(128)(2,1)S(1)}, u32[]{:S(2)}) copy-start(bf16[512]{0:T(512)(128)(2,1)S(1)} %get-tuple-element.99) | copy-start | bytes 3076
  181.0 61.9 %copy-start.43 = (bf16[512]{0:T(512)(128)(2,1)}, bf16[512]{0:T(512)(128)(2,1)S(1)}, u32[]{:S(2)}) copy-start(bf16[512]{0:T(512)(128)(2,1)S(1)} %get-tuple-element.100) | copy-start | bytes 3076
  181.0 61.9 %copy-start.44 = (bf16[512]{0:T(512)(128)(2,1)}, bf16[512]{0:T(512)(128)(2,1)S(1)}, u32[]{:S(2)}) copy-start(bf16[512]{0:T(512)(128)(2,1)S(1)} %get-tuple-element.101) | copy-start | bytes 3076
  243.2 8.6 %collective-permute-start.21 = (bf16[272,512]{1,0:T(8,128)(2,1)S(1)}, bf16[272,512]{1,0:T(8,128)(2,1)S(1)}, u32[]{:S(2)}, u32[]{:S(2)}) collective-permute-start(bf16[272,512]{1,0:T(8,128)(2,1)S(1)} %select_select_fusion.2), channel_id=1, source_target_pairs={{0,1},{1,0},{2,3},{3,2},{4,5},{5,4},{6,7},{7,6},{8,9},{9,8},{10,11... | collective-permute-start | bytes 835592 | tf_op jit(solution)/shard_map/ppermute | solution.py:341
  246.1 29.9 %collective-permute-start.25 = (f32[600,1024]{1,0:T(8,128)}, f32[600,1024]{1,0:T(8,128)S(1)}, u32[]{:S(2)}, u32[]{:S(2)}) collective-permute-start(f32[600,1024]{1,0:T(8,128)} %get-tuple-element.49), channel_id=1, source_target_pairs={{0,16},{16,0},{1,17},{17,1},{2,18},{18,2},{3,19},{19,3},{4,20},{20... | collective-permute-start | bytes 7372808 | tf_op jit(solution)/shard_map/ppermute | solution.py:344
  262.7 7.8 %collective-permute-start.22 = (bf16[272,512]{1,0:T(8,128)(2,1)S(1)}, bf16[272,512]{1,0:T(8,128)(2,1)S(1)}, u32[]{:S(2)}, u32[]{:S(2)}) collective-permute-start(bf16[272,512]{1,0:T(8,128)(2,1)S(1)} %dynamic-slice_bitcast_fusion), channel_id=1, source_target_pairs={{0,1},{1,0},{2,3},{3,2},{4,5},{5,4},{6,7},{7,6},{8,9},{9,8},{10,11... | collective-permute-start | bytes 835592 | tf_op jit(solution)/shard_map/ppermute | solution.py:341
  270.7 6.9 %collective-permute-start.24 = (bf16[272,512]{1,0:T(8,128)(2,1)S(1)}, bf16[272,512]{1,0:T(8,128)(2,1)S(1)}, u32[]{:S(2)}, u32[]{:S(2)}) collective-permute-start(bf16[272,512]{1,0:T(8,128)(2,1)S(1)} %fusion.79), channel_id=1, source_target_pairs={{0,2},{1,3},{2,0},{3,1},{4,6},{5,7},{6,4},{7,5},{8,10},{9,11},{10,... | collective-permute-start | bytes 835592 | tf_op jit(solution)/shard_map/ppermute | solution.py:341
  278.0 6.6 %collective-permute-start.26 = (bf16[272,512]{1,0:T(8,128)(2,1)S(1)}, bf16[272,512]{1,0:T(8,128)(2,1)S(1)}, u32[]{:S(2)}, u32[]{:S(2)}) collective-permute-start(bf16[272,512]{1,0:T(8,128)(2,1)S(1)} %select_select_fusion.1), channel_id=1, source_target_pairs={{0,4},{1,5},{2,6},{3,7},{4,0},{5,1},{6,2},{7,3},{8,12},{9,13},{10,... | collective-permute-start | bytes 835592 | tf_op jit(solution)/shard_map/ppermute | solution.py:341
  278.9 6.4 %collective-permute-start.23 = (bf16[32,1024]{1,0:T(8,128)(2,1)S(1)}, bf16[32,1024]{1,0:T(8,128)(2,1)S(1)}, u32[]{:S(2)}, u32[]{:S(2)}) collective-permute-start(bf16[32,1024]{1,0:T(8,128)(2,1)S(1)} %constant_dynamic-slice_fusion.17), channel_id=1, source_target_pairs={{0,1},{1,0},{2,3},{3,2},{4,5},{5,4},{6,7},{7,6},{8,9},{9,8},{10,11... | collective-permute-start | bytes 196616 | tf_op jit(solution)/shard_map/ppermute | solution.py:341
  280.7 15.9 %collective-permute-start.28 = (bf16[312,1024]{1,0:T(8,128)(2,1)S(1)}, bf16[312,1024]{1,0:T(8,128)(2,1)S(1)}, u32[]{:S(2)}, u32[]{:S(2)}) collective-permute-start(bf16[312,1024]{1,0:T(8,128)(2,1)S(1)} %pad_maximum_fusion.6), channel_id=1, source_target_pairs={{0,1},{1,0},{2,3},{3,2},{4,5},{5,4},{6,7},{7,6},{8,9},{9,8},{10,11... | collective-permute-start | bytes 1916936 | tf_op jit(solution)/shard_map/ppermute | solution.py:341
  285.0 11.5 %collective-permute-start.27 = (bf16[272,512]{1,0:T(8,128)(2,1)S(1)}, bf16[272,512]{1,0:T(8,128)(2,1)S(1)}, u32[]{:S(2)}, u32[]{:S(2)}) collective-permute-start(bf16[272,512]{1,0:T(8,128)(2,1)S(1)} %select_select_fusion), channel_id=1, source_target_pairs={{0,8},{1,9},{2,10},{3,11},{4,12},{5,13},{6,14},{7,15},{8,0},{9,1},... | collective-permute-start | bytes 835592 | tf_op jit(solution)/shard_map/ppermute | solution.py:341
  309.9 3.9 %collective-permute-start.30 = (f32[72,1792]{1,0:T(8,128)S(1)}, f32[72,1792]{1,0:T(8,128)S(1)}, u32[]{:S(2)}, u32[]{:S(2)}) collective-permute-start(f32[72,1792]{1,0:T(8,128)S(1)} %fusion.54), channel_id=1, source_target_pairs={{0,16},{16,0},{1,17},{17,1},{2,18},{18,2},{3,19},{19,3},{4,20},{20... | collective-permute-start | bytes 1548296 | tf_op jit(solution)/shard_map/ppermute | solution.py:344
  312.3 6.4 %collective-permute-start.29 = (f32[32,1024]{1,0:T(8,128)S(1)}, f32[32,1024]{1,0:T(8,128)S(1)}, u32[]{:S(2)}, u32[]{:S(2)}) collective-permute-start(f32[32,1024]{1,0:T(8,128)S(1)} %constant_dynamic-slice_fusion.14), channel_id=1, source_target_pairs={{0,1},{1,0},{2,3},{3,2},{4,5},{5,4},{6,7},{7,6},{8,9},{9,8},{10,11... | collective-permute-start | bytes 393224 | tf_op jit(solution)/shard_map/ppermute | solution.py:341
  314.0 10.4 %collective-permute-start.31 = (f32[40,1792]{1,0:T(8,128)S(1)}, f32[40,1792]{1,0:T(8,128)S(1)}, u32[]{:S(2)}, u32[]{:S(2)}) collective-permute-start(f32[40,1792]{1,0:T(8,128)S(1)} %pad_maximum_fusion.10), channel_id=1, source_target_pairs={{0,1},{1,0},{2,3},{3,2},{4,5},{5,4},{6,7},{7,6},{8,9},{9,8},{10,11... | collective-permute-start | bytes 860168 | tf_op jit(solution)/shard_map/ppermute | solution.py:341
  (45 other events, 202.0 us)
Sparse Core Ops, SparseCore 0:
  10.9 151.8 all-gather.1
